TPU v7x, 32 devices: a whole 2x2x4 slice. The times are simulated.
32 devices in a mesh: dp: 4 (over y, x), ctx: 8 (over z, core).
Axes of the slice: x: 2, y: 2, z: 4, core: 2. Of those that a mesh axis runs over, the one named last changes fastest.
Arguments:
- tokens: bfloat16 [8, 4096, 768], P('dp', 'ctx'), may hold values from -6 to 6
- cotangent: bfloat16 [8, 4096, 768], P('dp', 'ctx'), may hold values from -6 to 6
- lengths: int32 [8], P('dp'), may hold values from 1024 to 4096, as said below
- block_order: int32 [8, 8], P('dp'), may hold values from 0 to 7, each once within a row
- qkv_weight: bfloat16 [768, 2304], P('dp'), may hold values from -0.21875 to 0.21875
- query_bias: bfloat16 [768], P('dp'), may hold values from -4 to 4
- value_bias: bfloat16 [768], P('dp'), may hold values from -0.15625 to 0.15625
- out_weight: bfloat16 [768, 768], P('dp'), may hold values from -6 to 6
- out_bias: bfloat16 [768], P('dp'), may hold values from -4 to 4
- attn_gain: bfloat16 [768], P('dp'), may hold values from 0.5 to 1.5
- attn_shift: bfloat16 [768], P('dp'), may hold values from -1.5 to 1.5
- up_weight: bfloat16 [768, 3072], P('dp'), may hold values from -0.21875 to 0.21875
- up_bias: bfloat16 [3072], P('dp'), may hold values from -1.5 to 1.5
- down_weight: bfloat16 [3072, 768], P('dp'), may hold values from -0.15625 to 0.15625
- down_bias: bfloat16 [768], P('dp'), may hold values from -1.5 to 1.5
- ffn_gain: bfloat16 [768], P('dp'), may hold values from 0.5 to 1.5
- ffn_shift: bfloat16 [768], P('dp'), may hold values from -1.5 to 1.5
Outputs:
- output: bfloat16 [8, 4096, 768], P('dp', 'ctx')
- grad_tokens: bfloat16 [8, 4096, 768], P('dp', 'ctx')
- grad_qkv_weight: float32 [768, 2304], P('dp')
- grad_query_bias: float32 [768], P('dp')
- grad_value_bias: float32 [768], P('dp')
- grad_out_weight: float32 [768, 768], P('dp')
- grad_out_bias: float32 [768], P('dp')
- grad_attn_gain: float32 [768], P('dp')
- grad_attn_shift: float32 [768], P('dp')
- grad_up_weight: float32 [768, 3072], P('dp')
- grad_up_bias: float32 [3072], P('dp')
- grad_down_weight: float32 [3072, 768], P('dp')
- grad_down_bias: float32 [768], P('dp')
- grad_ffn_gain: float32 [768], P('dp')
- grad_ffn_shift: float32 [768], P('dp')
- branch_rms: float32 [8, 3], P('dp')
Inputs may be any that keep to these rules, and one draw needn't show every extreme that they name: `lengths`: some sequence has exactly 4096 valid slots and some exactly 1024. Each row is a permutation: index c of ctx holds positions block_order[s, c] * 512 to block_order[s, c] * 512 + 511 of sequence s.
All inputs are finite; a program needn't handle non-finite values.
Results may differ from a plain program's by a relative error of at most 0.02.
Values may be sent and summed in bfloat16 or wider, within the bound.
A program may use at most 256 MiB of HBM per device.

v0:
```python
import jax
import jax.numpy as jnp
from jax import lax
from jax.sharding import PartitionSpec as P

HEADS = 12


norm_eps = 1e-12
rms_eps = 1e-06
masked_score = -1e30


def slot_places(order_rows, first, count, block):
    slots = first + jnp.arange(count, dtype=jnp.int32)
    owners = slots // block
    within = slots - owners * block
    table = jnp.arange(order_rows.shape[1], dtype=jnp.int32)
    chosen = jnp.sum(
        jnp.where(owners[None, :, None] == table[None, None, :], order_rows[:, None, :], 0), axis=2
    )
    return chosen * block + within


def part_rows(block):
    wanted = block * max(1, 512 // block)
    return wanted


def norm_parts(total, gain, shift):
    mean = jnp.mean(total, axis=-1, keepdims=True)
    centred = total - mean
    inverse = lax.rsqrt(jnp.mean(centred * centred, axis=-1, keepdims=True) + norm_eps)
    unit = centred * inverse
    return (unit * gain + shift, unit, inverse)


def norm_back(grad_unit, unit, inverse):
    mean_grad = jnp.mean(grad_unit, axis=-1, keepdims=True)
    mean_cross = jnp.mean(grad_unit * unit, axis=-1, keepdims=True)
    return inverse * (grad_unit - mean_grad - unit * mean_cross)


def exact_gelu(value):
    return jax.nn.gelu(value, approximate=False)


def cross(left, right):
    return lax.dot_general(
        left, right, (((0,), (0,)), ((), ())), preferred_element_type=jnp.float32
    )


def back_dot(left, right):
    return lax.dot_general(
        left, right, (((1,), (1,)), ((), ())), preferred_element_type=jnp.float32
    )


def seq_sum(values, seqs):
    return jnp.sum(values.reshape(seqs, -1), axis=1)


def shards(
    tokens,
    cotangent,
    lengths,
    block_order,
    qkv_weight,
    query_bias,
    value_bias,
    out_weight,
    out_bias,
    attn_gain,
    attn_shift,
    up_weight,
    up_bias,
    down_weight,
    down_bias,
    ffn_gain,
    ffn_shift,
):
    seqs, block, width = tokens.shape
    heads = HEADS
    head_dim = width // heads
    scale = head_dim ** (-0.5)
    count_rows = seqs * block
    here = lax.axis_index("ctx")
    own_order = lax.dynamic_slice_in_dim(block_order, here, 1, 1)
    places = own_order * block + jnp.arange(block, dtype=jnp.int32)[None, :]
    live = places < lengths[:, None]
    live_rows = jnp.where(live.reshape(count_rows, 1), 1.0, 0.0).astype(jnp.float32)
    attn_set = (
        lax.all_gather(qkv_weight, "dp", axis=0, tiled=True),
        lax.all_gather(query_bias, "dp", axis=0, tiled=True),
        lax.all_gather(value_bias, "dp", axis=0, tiled=True),
        lax.all_gather(out_weight, "dp", axis=0, tiled=True),
        lax.all_gather(out_bias, "dp", axis=0, tiled=True),
        lax.all_gather(attn_gain, "dp", axis=0, tiled=True),
        lax.all_gather(attn_shift, "dp", axis=0, tiled=True),
    )
    qkv_all, query_bias_all, value_bias_all, out_all, out_bias_all, gain_first, shift_first = (
        attn_set
    )
    rows = tokens.reshape(count_rows, width)
    projected = jnp.dot(rows, qkv_all, preferred_element_type=jnp.float32)
    queries = (
        (projected[:, :width] + query_bias_all)
        .astype(jnp.bfloat16)
        .reshape(seqs, block, heads, head_dim)
    )
    keys = (
        projected[:, width : 2 * width].astype(jnp.bfloat16).reshape(seqs, block, heads, head_dim)
    )
    values = (
        (projected[:, 2 * width :] + value_bias_all)
        .astype(jnp.bfloat16)
        .reshape(seqs, block, heads, head_dim)
    )
    start_state = (
        jnp.full((seqs, heads, block), masked_score, jnp.float32),
        jnp.zeros((seqs, heads, block), jnp.float32),
        jnp.zeros((seqs, heads, block, head_dim), jnp.float32),
    )
    key_piece = lax.all_gather(keys, "ctx", axis=1, tiled=True)
    value_piece = lax.all_gather(values, "ctx", axis=1, tiled=True)
    count = key_piece.shape[1]
    step = part_rows(block)

    def attend_inner(index, inner_state):
        best, total, acc = inner_state
        first = index * step
        key_part = lax.dynamic_slice_in_dim(key_piece, first, step, 1)
        value_part = lax.dynamic_slice_in_dim(value_piece, first, step, 1)
        open_keys = slot_places(block_order, first, step, block) < lengths[:, None]
        mask = open_keys[:, None, None, :]
        scores = (
            jnp.einsum("sqhd,skhd->shqk", queries, key_part, preferred_element_type=jnp.float32)
            * scale
        )
        scores = jnp.where(mask, scores, masked_score)
        new_best = jnp.maximum(best, jnp.max(scores, axis=3))
        weights = jnp.where(mask, jnp.exp(scores - new_best[..., None]), 0.0)
        factor = jnp.exp(best - new_best)
        total = total * factor + jnp.sum(weights, axis=3)
        acc = acc * factor[..., None] + jnp.einsum(
            "shqk,skhd->shqd",
            weights.astype(jnp.bfloat16),
            value_part,
            preferred_element_type=jnp.float32,
        )
        return (new_best, total, acc)

    best, total, acc = lax.fori_loop(0, count // step, attend_inner, start_state)
    log_total = best + jnp.log(total)
    mixed = (acc / total[..., None]).transpose(0, 2, 1, 3).reshape(count_rows, width)
    mixed_low = mixed.astype(jnp.bfloat16)
    attn = jnp.dot(mixed_low, out_all, preferred_element_type=jnp.float32) + out_bias_all
    hidden, unit_first, inverse_first = norm_parts(
        rows.astype(jnp.float32) + attn, gain_first, shift_first
    )
    ffn_set = (
        lax.all_gather(up_weight, "dp", axis=0, tiled=True),
        lax.all_gather(up_bias, "dp", axis=0, tiled=True),
        lax.all_gather(down_weight, "dp", axis=0, tiled=True),
        lax.all_gather(down_bias, "dp", axis=0, tiled=True),
        lax.all_gather(ffn_gain, "dp", axis=0, tiled=True),
        lax.all_gather(ffn_shift, "dp", axis=0, tiled=True),
    )
    up_all, up_bias_all, down_all, down_bias_all, gain_second, shift_second = ffn_set
    hidden_low = hidden.astype(jnp.bfloat16)
    upper = jnp.dot(hidden_low, up_all, preferred_element_type=jnp.float32) + up_bias_all
    active, gelu_pull = jax.vjp(exact_gelu, upper)
    active_low = active.astype(jnp.bfloat16)
    branch = jnp.dot(active_low, down_all, preferred_element_type=jnp.float32) + down_bias_all
    normed, unit_second, inverse_second = norm_parts(hidden + branch, gain_second, shift_second)
    result = normed * live_rows
    output = result.astype(jnp.bfloat16).reshape(seqs, block, width)
    square_sums = jnp.stack(
        [
            seq_sum(result * result, seqs),
            seq_sum(attn * attn * live_rows, seqs),
            seq_sum(branch * branch * live_rows, seqs),
        ],
        axis=1,
    )
    up_all, up_bias_all, down_all, down_bias_all, gain_second, shift_second = (
        lax.all_gather(up_weight, "dp", axis=0, tiled=True),
        lax.all_gather(up_bias, "dp", axis=0, tiled=True),
        lax.all_gather(down_weight, "dp", axis=0, tiled=True),
        lax.all_gather(down_bias, "dp", axis=0, tiled=True),
        lax.all_gather(ffn_gain, "dp", axis=0, tiled=True),
        lax.all_gather(ffn_shift, "dp", axis=0, tiled=True),
    )
    grad_out = cotangent.reshape(count_rows, width).astype(jnp.float32) * live_rows
    grad_ffn_gain = jnp.sum(grad_out * unit_second, axis=0)
    grad_ffn_shift = jnp.sum(grad_out, axis=0)
    grad_second = norm_back(grad_out * gain_second, unit_second, inverse_second)
    grad_branch = grad_second.astype(jnp.bfloat16)
    grad_down_bias = jnp.sum(grad_branch, axis=0, dtype=jnp.float32)
    grad_down_weight = cross(active_low, grad_branch)
    grad_active = back_dot(grad_branch, down_all)
    grad_upper = gelu_pull(grad_active)[0].astype(jnp.bfloat16)
    grad_up_bias = jnp.sum(grad_upper, axis=0, dtype=jnp.float32)
    grad_up_weight = cross(hidden_low, grad_upper)
    grad_hidden = grad_second + back_dot(grad_upper, up_all)
    ffn_parts = (
        lax.psum_scatter(grad_up_weight, ("dp", "ctx"), scatter_dimension=0, tiled=True),
        lax.psum_scatter(grad_up_bias, ("dp", "ctx"), scatter_dimension=0, tiled=True),
        lax.psum_scatter(grad_down_weight, ("dp", "ctx"), scatter_dimension=0, tiled=True),
        lax.psum_scatter(grad_down_bias, ("dp", "ctx"), scatter_dimension=0, tiled=True),
        lax.psum_scatter(grad_ffn_gain, ("dp", "ctx"), scatter_dimension=0, tiled=True),
        lax.psum_scatter(grad_ffn_shift, ("dp", "ctx"), scatter_dimension=0, tiled=True),
    )
    qkv_all, query_bias_all, value_bias_all, out_all, out_bias_all, gain_first, shift_first = (
        lax.all_gather(qkv_weight, "dp", axis=0, tiled=True),
        lax.all_gather(query_bias, "dp", axis=0, tiled=True),
        lax.all_gather(value_bias, "dp", axis=0, tiled=True),
        lax.all_gather(out_weight, "dp", axis=0, tiled=True),
        lax.all_gather(out_bias, "dp", axis=0, tiled=True),
        lax.all_gather(attn_gain, "dp", axis=0, tiled=True),
        lax.all_gather(attn_shift, "dp", axis=0, tiled=True),
    )
    grad_attn_gain = jnp.sum(grad_hidden * unit_first, axis=0)
    grad_attn_shift = jnp.sum(grad_hidden, axis=0)
    grad_first = norm_back(grad_hidden * gain_first, unit_first, inverse_first)
    grad_attn = grad_first.astype(jnp.bfloat16)
    grad_out_bias = jnp.sum(grad_attn, axis=0, dtype=jnp.float32)
    grad_out_weight = cross(mixed_low, grad_attn)
    grad_mixed = back_dot(grad_attn, out_all).astype(jnp.bfloat16)
    grad_heads = grad_mixed.reshape(seqs, block, heads, head_dim)
    spread = jnp.sum(
        (grad_mixed.astype(jnp.float32) * mixed).reshape(seqs, block, heads, head_dim), axis=3
    )
    spread_heads = spread.transpose(0, 2, 1)
    log_rows = log_total.transpose(0, 2, 1)
    key_zeros = jnp.zeros((seqs, block, heads, head_dim), jnp.float32)
    query_key_piece = lax.all_gather(keys, "ctx", axis=1, tiled=True)
    query_value_piece = lax.all_gather(values, "ctx", axis=1, tiled=True)
    count = query_key_piece.shape[1]
    query_step = part_rows(block)

    def query_inner(index, acc_in):
        first = index * query_step
        key_part = lax.dynamic_slice_in_dim(query_key_piece, first, query_step, 1)
        value_part = lax.dynamic_slice_in_dim(query_value_piece, first, query_step, 1)
        open_keys = slot_places(block_order, first, query_step, block) < lengths[:, None]
        mask = open_keys[:, None, None, :]
        scores = (
            jnp.einsum("sqhd,skhd->shqk", queries, key_part, preferred_element_type=jnp.float32)
            * scale
        )
        scores = jnp.where(mask, scores, masked_score)
        weights = jnp.where(mask, jnp.exp(scores - log_total[..., None]), 0.0)
        grad_weights = jnp.einsum(
            "sqhd,skhd->shqk", grad_heads, value_part, preferred_element_type=jnp.float32
        )
        grad_scores = (weights * (grad_weights - spread_heads[..., None])).astype(jnp.bfloat16)
        return (
            acc_in
            + jnp.einsum(
                "shqk,skhd->sqhd", grad_scores, key_part, preferred_element_type=jnp.float32
            )
            * scale
        )

    grad_queries = lax.fori_loop(0, count // query_step, query_inner, key_zeros)
    query_piece = lax.all_gather(queries.astype(jnp.float32), "ctx", axis=1, tiled=True).astype(
        jnp.bfloat16
    )
    grad_piece = lax.all_gather(grad_heads.astype(jnp.float32), "ctx", axis=1, tiled=True).astype(
        jnp.bfloat16
    )
    log_piece = lax.all_gather(log_rows, "ctx", axis=1, tiled=True)
    spread_piece = lax.all_gather(spread, "ctx", axis=1, tiled=True)
    count = query_piece.shape[1]
    key_step = part_rows(block)

    def key_inner(index, inner_state):
        grad_keys_in, grad_values_in = inner_state
        first = index * key_step
        query_part = lax.dynamic_slice_in_dim(query_piece, first, key_step, 1)
        grad_part = lax.dynamic_slice_in_dim(grad_piece, first, key_step, 1)
        log_part = lax.dynamic_slice_in_dim(log_piece, first, key_step, 1).transpose(0, 2, 1)
        spread_part = lax.dynamic_slice_in_dim(spread_piece, first, key_step, 1).transpose(0, 2, 1)
        scores = (
            jnp.einsum("sqhd,skhd->shqk", query_part, keys, preferred_element_type=jnp.float32)
            * scale
        )
        weights = jnp.where(live[:, None, None, :], jnp.exp(scores - log_part[..., None]), 0.0)
        grad_values_in = grad_values_in + jnp.einsum(
            "shqk,sqhd->skhd",
            weights.astype(jnp.bfloat16),
            grad_part,
            preferred_element_type=jnp.float32,
        )
        grad_weights = jnp.einsum(
            "sqhd,skhd->shqk", grad_part, values, preferred_element_type=jnp.float32
        )
        grad_scores = (weights * (grad_weights - spread_part[..., None])).astype(jnp.bfloat16)
        grad_keys_in = (
            grad_keys_in
            + jnp.einsum(
                "shqk,sqhd->skhd", grad_scores, query_part, preferred_element_type=jnp.float32
            )
            * scale
        )
        return (grad_keys_in, grad_values_in)

    grad_keys, grad_values = lax.fori_loop(0, count // key_step, key_inner, (key_zeros, key_zeros))
    grad_query_low = grad_queries.astype(jnp.bfloat16).reshape(count_rows, width)
    grad_key_low = grad_keys.astype(jnp.bfloat16).reshape(count_rows, width)
    grad_value_low = grad_values.astype(jnp.bfloat16).reshape(count_rows, width)
    grad_query_bias = jnp.sum(grad_query_low, axis=0, dtype=jnp.float32)
    grad_value_bias = jnp.sum(grad_value_low, axis=0, dtype=jnp.float32)
    grad_projected = jnp.concatenate([grad_query_low, grad_key_low, grad_value_low], axis=1)
    grad_qkv_weight = cross(rows, grad_projected)
    grad_rows = grad_first + back_dot(grad_projected, qkv_all)
    grad_tokens = grad_rows.astype(jnp.bfloat16).reshape(seqs, block, width)
    attn_parts = (
        lax.psum_scatter(grad_qkv_weight, ("dp", "ctx"), scatter_dimension=0, tiled=True),
        lax.psum_scatter(grad_query_bias, ("dp", "ctx"), scatter_dimension=0, tiled=True),
        lax.psum_scatter(grad_value_bias, ("dp", "ctx"), scatter_dimension=0, tiled=True),
        lax.psum_scatter(grad_out_weight, ("dp", "ctx"), scatter_dimension=0, tiled=True),
        lax.psum_scatter(grad_out_bias, ("dp", "ctx"), scatter_dimension=0, tiled=True),
        lax.psum_scatter(grad_attn_gain, ("dp", "ctx"), scatter_dimension=0, tiled=True),
        lax.psum_scatter(grad_attn_shift, ("dp", "ctx"), scatter_dimension=0, tiled=True),
    )
    whole = (
        lax.all_gather(attn_parts[0], "ctx", axis=0, tiled=True),
        lax.all_gather(attn_parts[1], "ctx", axis=0, tiled=True),
        lax.all_gather(attn_parts[2], "ctx", axis=0, tiled=True),
        lax.all_gather(attn_parts[3], "ctx", axis=0, tiled=True),
        lax.all_gather(attn_parts[4], "ctx", axis=0, tiled=True),
        lax.all_gather(attn_parts[5], "ctx", axis=0, tiled=True),
        lax.all_gather(attn_parts[6], "ctx", axis=0, tiled=True),
        lax.all_gather(ffn_parts[0], "ctx", axis=0, tiled=True),
        lax.all_gather(ffn_parts[1], "ctx", axis=0, tiled=True),
        lax.all_gather(ffn_parts[2], "ctx", axis=0, tiled=True),
        lax.all_gather(ffn_parts[3], "ctx", axis=0, tiled=True),
        lax.all_gather(ffn_parts[4], "ctx", axis=0, tiled=True),
        lax.all_gather(ffn_parts[5], "ctx", axis=0, tiled=True),
    )
    seq_squares = lax.psum(square_sums, "ctx")
    branch_rms = jnp.sqrt(seq_squares / (lengths.astype(jnp.float32)[:, None] * width) + rms_eps)
    return (
        output,
        grad_tokens,
        whole[0],
        whole[1],
        whole[2],
        whole[3],
        whole[4],
        whole[5],
        whole[6],
        whole[7],
        whole[8],
        whole[9],
        whole[10],
        whole[11],
        whole[12],
        branch_rms,
    )


def solution(mesh):
    in_specs = (
        P("dp", "ctx", None),
        P("dp", "ctx", None),
        P("dp"),
        P("dp", None),
        P("dp", None),
        P("dp"),
        P("dp"),
        P("dp", None),
        P("dp"),
        P("dp"),
        P("dp"),
        P("dp", None),
        P("dp"),
        P("dp", None),
        P("dp"),
        P("dp"),
        P("dp"),
    )
    out_specs = (
        P("dp", "ctx", None),
        P("dp", "ctx", None),
        P("dp", None),
        P("dp"),
        P("dp"),
        P("dp", None),
        P("dp"),
        P("dp"),
        P("dp"),
        P("dp", None),
        P("dp"),
        P("dp", None),
        P("dp"),
        P("dp"),
        P("dp"),
        P("dp", None),
    )
    return jax.shard_map(shards, mesh=mesh, in_specs=in_specs, out_specs=out_specs, check_vma=False)
```

profile of v0, /device:TPU:1, one launch (start us, length us, event | category | flops | bytes accessed | tf_op | source)
XLA Modules:
  0.0 1859.0 jit_solution(5990668088510129566)
XLA Ops:
  8.0 51.3 %all-gather.13.cloned.1.call-done = bf16[768,2304]{1,0:T(8,128)(2,1)} async-done(((bf16[192,2304]{1,0:T(8,128)(2,1)}), bf16[768,2304]{1,0:T(8,128)(2,1)}) %all-gather.13.cloned.1.call-update) | async-done | bytes 3538960 | tf_op jit(solution)/shard_map/all_gather | solution.py:94
  113.6 76.8 %all-gather.15.cloned.1.call-done = bf16[2,4096,12,64]{1,0,3,2:T(2,128)(2,1)} async-done(((bf16[2,512,12,64]{1,0,3,2:T(2,128)(2,1)}), bf16[2,4096,12,64]{1,0,3,2:T(2,128)(2,1)}) %all-gather.15.cloned.1.call-update) | async-done | bytes 12582928 | tf_op jit(solution)/shard_map/all_gather | solution.py:125
  205.3 102.6 %all-gather.17.cloned.1.call-done = bf16[2,4096,12,64]{1,0,3,2:T(2,128)(2,1)} async-done(((bf16[2,512,12,64]{1,0,3,2:T(2,128)(2,1)}), bf16[2,4096,12,64]{1,0,3,2:T(2,128)(2,1)}) %all-gather.17.cloned.1.call-update) | async-done | bytes 12582928 | tf_op jit(solution)/shard_map/all_gather | solution.py:126
  322.4 310.6 %while.52 = (s32[]{:T(128)}, f32[2,12,512]{2,1,0:T(8,128)S(1)}, f32[2,12,512]{2,1,0:T(8,128)S(1)}, f32[2,12,512,64]{2,3,1,0:T(8,128)}, s32[2,8]{1,0:T(2,128)S(1)...) while((s32[]{:T(128)}, f32[2,12,512]{2,1,0:T(8,128)S(1)}, ...), condition=%wide.region_4.5_spmd.clone, body=%wide.region_0.4_spmd.clone.sunk | while | flops 1694854144 | bytes 112524616 | solution.py:154
  648.4 35.8 %multiply_convert_fusion.8 = (bf16[1024,3072]{1,0:T(8,128)(2,1)}, f32[1024,3072]{1,0:T(8,128)}, f32[1024,3072]{1,0:T(8,128)}) fusion(f32[3072]{0:T(1024)S(1)} %bitcast.155, bf16[768,3072]{1,0:T(8,128)(2,1)} %all-gather.21.cloned.1.call-done, f32[1024,768]{1,0:T(8,128)S(1)} %get-tuple-element.1051, f32[768]{0:T(1024)S(1)} %copy-done.36, ...), kind=kOutput, calls=%fused_computation.94 | convolution fusion | flops 5043388416 | bytes 39348224 | tf_op jit(solution)/shard_map/dot_general | solution.py:172
  702.3 19.4 %convert_reduce_fusion = (f32[3072]{0:T(1024)}, bf16[1024,3072]{1,0:T(8,128)(2,1)}) fusion(f32[1024,3072]{1,0:T(8,128)} %get-tuple-element.1049, bf16[3072,768]{1,0:T(8,128)(2,1)} %all-gather.23.cloned.1.call-done, f32[1024,768]{1,0:T(8,128)} %get-tuple-element.1039, f32[1024,3072]{1,0:T(8,128)} %get-tuple-element.1068, f32[3072]{0:T(1024)S(1)} %bitcast.156), kind=kOutput, calls=%fused_computation.92 | convolution fusion | flops 4886098944 | bytes 39346176 | tf_op jit(solution)/shard_map/dot_general | solution.py:55
  775.7 247.5 %while.53 = (s32[]{:T(128)}, f32[2,512,12,64]{1,3,2,0:T(8,128)}, bf16[2,4096,12,64]{1,3,2,0:T(8,128)(2,1)}, s32[2,8]{1,0:T(2,128)S(1)}, s32[2]{0:T(128)S(1)}, /*...) while((s32[]{:T(128)}, f32[2,512,12,64]{1,3,2,0:T(8,128)}, ...), condition=%wide.region_16.17_spmd.clone, body=%wide.region_14.16_spmd.clone.sunk | while | flops 2462350336 | bytes 64614164 | solution.py:267
  788.0 18.4 bitcast_add_fusion.6
  818.5 18.6 %bitcast_add_fusion.6 = f32[2,512,12,64]{1,3,2,0:T(8,128)} fusion(f32[2,512,12,64]{1,3,2,0:T(8,128)} %get-tuple-element.1338, f32[2,12,512,512]{3,2,1,0:T(8,128)} %fusion.145, f32[2,12,512]{2,1,0:T(8,128)S(1)} %get-tuple-element.1360, f32[2,12,512]{2,1,0:T(8,128)S(1)} %get-tuple-element.1357, pred[2,512]{1,0:T(4,128)(4,1)S(1)} %add_compare_fusion.7, ...), kind=kOutput, calls=%fused_computation.42.clone.1 | convolution fusion | flops 1657012224 | bytes 36276736 | tf_op jit(solution)/shard_map/while/body/eval_jaxpr/shqk,skhd->sqhd/dot_general | solution.py:261
  849.3 18.6 %bitcast_add_fusion.6 = f32[2,512,12,64]{1,3,2,0:T(8,128)} fusion(f32[2,512,12,64]{1,3,2,0:T(8,128)} %get-tuple-element.1338, f32[2,12,512,512]{3,2,1,0:T(8,128)} %fusion.145, f32[2,12,512]{2,1,0:T(8,128)S(1)} %get-tuple-element.1360, f32[2,12,512]{2,1,0:T(8,128)S(1)} %get-tuple-element.1357, pred[2,512]{1,0:T(4,128)(4,1)S(1)} %add_compare_fusion.7, ...), kind=kOutput, calls=%fused_computation.42.clone.1 | convolution fusion | flops 1657012224 | bytes 36276736 | tf_op jit(solution)/shard_map/while/body/eval_jaxpr/shqk,skhd->sqhd/dot_general | solution.py:261
  880.5 19.3 %bitcast_add_fusion.6 = f32[2,512,12,64]{1,3,2,0:T(8,128)} fusion(f32[2,512,12,64]{1,3,2,0:T(8,128)} %get-tuple-element.1338, f32[2,12,512,512]{3,2,1,0:T(8,128)} %fusion.145, f32[2,12,512]{2,1,0:T(8,128)S(1)} %get-tuple-element.1360, f32[2,12,512]{2,1,0:T(8,128)S(1)} %get-tuple-element.1357, pred[2,512]{1,0:T(4,128)(4,1)S(1)} %add_compare_fusion.7, ...), kind=kOutput, calls=%fused_computation.42.clone.1 | convolution fusion | flops 1657012224 | bytes 36276736 | tf_op jit(solution)/shard_map/while/body/eval_jaxpr/shqk,skhd->sqhd/dot_general | solution.py:261
  912.0 18.9 %bitcast_add_fusion.6 = f32[2,512,12,64]{1,3,2,0:T(8,128)} fusion(f32[2,512,12,64]{1,3,2,0:T(8,128)} %get-tuple-element.1338, f32[2,12,512,512]{3,2,1,0:T(8,128)} %fusion.145, f32[2,12,512]{2,1,0:T(8,128)S(1)} %get-tuple-element.1360, f32[2,12,512]{2,1,0:T(8,128)S(1)} %get-tuple-element.1357, pred[2,512]{1,0:T(4,128)(4,1)S(1)} %add_compare_fusion.7, ...), kind=kOutput, calls=%fused_computation.42.clone.1 | convolution fusion | flops 1657012224 | bytes 36276736 | tf_op jit(solution)/shard_map/while/body/eval_jaxpr/shqk,skhd->sqhd/dot_general | solution.py:261
  943.2 18.8 %bitcast_add_fusion.6 = f32[2,512,12,64]{1,3,2,0:T(8,128)} fusion(f32[2,512,12,64]{1,3,2,0:T(8,128)} %get-tuple-element.1338, f32[2,12,512,512]{3,2,1,0:T(8,128)} %fusion.145, f32[2,12,512]{2,1,0:T(8,128)S(1)} %get-tuple-element.1360, f32[2,12,512]{2,1,0:T(8,128)S(1)} %get-tuple-element.1357, pred[2,512]{1,0:T(4,128)(4,1)S(1)} %add_compare_fusion.7, ...), kind=kOutput, calls=%fused_computation.42.clone.1 | convolution fusion | flops 1657012224 | bytes 36276736 | tf_op jit(solution)/shard_map/while/body/eval_jaxpr/shqk,skhd->sqhd/dot_general | solution.py:261
  974.0 18.8 %bitcast_add_fusion.6 = f32[2,512,12,64]{1,3,2,0:T(8,128)} fusion(f32[2,512,12,64]{1,3,2,0:T(8,128)} %get-tuple-element.1338, f32[2,12,512,512]{3,2,1,0:T(8,128)} %fusion.145, f32[2,12,512]{2,1,0:T(8,128)S(1)} %get-tuple-element.1360, f32[2,12,512]{2,1,0:T(8,128)S(1)} %get-tuple-element.1357, pred[2,512]{1,0:T(4,128)(4,1)S(1)} %add_compare_fusion.7, ...), kind=kOutput, calls=%fused_computation.42.clone.1 | convolution fusion | flops 1657012224 | bytes 36276736 | tf_op jit(solution)/shard_map/while/body/eval_jaxpr/shqk,skhd->sqhd/dot_general | solution.py:261
  1004.7 18.6 %bitcast_add_fusion.6 = f32[2,512,12,64]{1,3,2,0:T(8,128)} fusion(f32[2,512,12,64]{1,3,2,0:T(8,128)} %get-tuple-element.1338, f32[2,12,512,512]{3,2,1,0:T(8,128)} %fusion.145, f32[2,12,512]{2,1,0:T(8,128)S(1)} %get-tuple-element.1360, f32[2,12,512]{2,1,0:T(8,128)S(1)} %get-tuple-element.1357, pred[2,512]{1,0:T(4,128)(4,1)S(1)} %add_compare_fusion.7, ...), kind=kOutput, calls=%fused_computation.42.clone.1 | convolution fusion | flops 1657012224 | bytes 36276736 | tf_op jit(solution)/shard_map/while/body/eval_jaxpr/shqk,skhd->sqhd/dot_general | solution.py:261
  1029.4 15.9 all_gather.122
  1072.9 386.9 %while.54 = (s32[]{:T(128)}, f32[2,512,12,64]{1,3,2,0:T(8,128)}, f32[2,512,12,64]{1,3,2,0:T(8,128)}, bf16[2,4096,12,64]{1,0,3,2:T(2,128)(2,1)}, bf16[2,512,12,64...) while((s32[]{:T(128)}, f32[2,512,12,64]{1,3,2,0:T(8,128)}, ...), condition=%wide.region_18.19_spmd.clone, body=%wide.region_17.18_spmd.clone.sunk | while | flops 3288074240 | bytes 104254696 | solution.py:310
  1091.8 16.5 bitcast_add_fusion.7
  1140.6 16.6 bitcast_add_fusion.7
  1189.2 16.5 bitcast_add_fusion.7
  1237.5 16.3 bitcast_add_fusion.7
  1285.5 16.3 bitcast_add_fusion.7
  1333.5 16.3 bitcast_add_fusion.7
  1381.5 16.3 bitcast_add_fusion.7
  1429.6 16.3 bitcast_add_fusion.7
  1490.7 107.5 %reduce-scatter.13.cloned.1.call-done = f32[24,2304]{1,0:T(8,128)} async-done(((f32[768,2304]{1,0:T(8,128)}), f32[24,2304]{1,0:T(8,128)}) %reduce-scatter.13.cloned.1.call-update) | async-done | bytes 221200 | tf_op jit(solution)/shard_map/reduce_scatter | solution.py:321
  1600.7 102.5 %reduce-scatter.7.cloned.1.call-done = f32[24,768]{1,0:T(8,128)} async-done(((f32[768,768]{1,0:T(8,128)}), f32[24,768]{1,0:T(8,128)}) %reduce-scatter.7.cloned.1.call-update) | async-done | bytes 73744 | tf_op jit(solution)/shard_map/reduce_scatter | solution.py:324
  1703.1 19.3 %all_gather.126 = f32[192,768]{1,0:T(8,128)} all-gather(f32[24,768]{1,0:T(8,128)} %reduce-scatter.7.cloned.1.call-done), channel_id=1, replica_groups=mesh['dp'=4,'ctx'=8] {'ctx'}, dimensions={0}, use_global_device_ids=true | all-gather | bytes 663552 | tf_op jit(solution)/shard_map/all_gather | solution.py:333
  1722.5 15.9 all-gather.31.cloned.1.call-done
  1738.4 32.2 %all-gather.33.cloned.1.call-done = f32[768,768]{1,0:T(8,128)} async-done(((f32[96,768]{1,0:T(8,128)}), f32[768,768]{1,0:T(8,128)}) %all-gather.33.cloned.1.call-update) | async-done | bytes 2359312 | tf_op jit(solution)/shard_map/all_gather | solution.py:339
  1770.7 40.0 %all-reduce.26 = (f32[768]{0:T(1024)S(1)}, f32[768]{0:T(1024)S(1)}, f32[768]{0:T(1024)S(1)}, f32[768]{0:T(1024)S(1)}, f32[768]{0:T(1024)S(1)}, /*index=5*/f32[30...) all-reduce(f32[768]{0:T(1024)S(1)} %reduce_sum.272, ...), channel_id=3, replica_groups=mesh['dp'=4,'ctx'=8] {'dp','ctx'}, use_global_device_ids=true, to_apply=%region_21.22.clone | all-reduce | flops 9216 | bytes 73728
  1812.2 24.1 %all-reduce.27 = (f32[192]{0:T(256)}, f32[192]{0:T(256)}, f32[192]{0:T(256)}, f32[192]{0:T(256)}, f32[192]{0:T(256)}, /*index=5*/f32[768]{0:T(1024)}, f32[192]{0...) all-reduce(f32[192]{0:T(256)S(1)} %dynamic-slice_dynamic-update-slice_fus, ...), channel_id=1, replica_groups=mesh['dp'=4,'ctx'=8] {'ctx'}, use_global_device_ids=true, to_apply=%add.8 | all-reduce | flops 2310 | bytes 18480
  (513 shorter events, 916.0 us)
Async XLA Ops:
  7.2 52.0 %all-gather.13.cloned.1.call-start = ((), (), s32[]{:S(2)}) async-start(), calls=%async_computation.4 | async-start | bytes 4423680 | tf_op jit(solution)/shard_map/all_gather | solution.py:94
  7.9 182.4 %all-gather.15.cloned.1.call-start = ((), (), s32[]{:S(2)}) async-start(), calls=%async_computation.5 | async-start | bytes 14155776 | tf_op jit(solution)/shard_map/all_gather | solution.py:125
  72.5 235.4 %all-gather.17.cloned.1.call-start = ((), (), s32[]{:S(2)}) async-start(), calls=%async_computation.6 | async-start | bytes 14155776 | tf_op jit(solution)/shard_map/all_gather | solution.py:126
  92.9 15.4 copy-start.7
  95.3 14.9 copy-start.17
  95.3 546.4 %all-gather.19.cloned.1.call-start = ((), (), s32[]{:S(2)}) async-start(), calls=%async_computation.7 | async-start | bytes 1474560 | tf_op jit(solution)/shard_map/all_gather | solution.py:97
  95.9 552.3 %all-gather.21.cloned.1.call-start = ((), (), s32[]{:S(2)}) async-start(), calls=%async_computation.8 | async-start | bytes 5898240 | tf_op jit(solution)/shard_map/all_gather | solution.py:163
  96.5 587.7 %all-gather.23.cloned.1.call-start = ((), (), s32[]{:S(2)}) async-start(), calls=%async_computation.9 | async-start | bytes 5898240 | tf_op jit(solution)/shard_map/all_gather | solution.py:165
  97.1 974.5 %all-gather.25.cloned.1.call-start = ((), (), s32[]{:S(2)}) async-start(), calls=%async_computation.10 | async-start | bytes 14155776 | tf_op jit(solution)/shard_map/all_gather | solution.py:268
  113.3 958.3 %all-gather.27.cloned.1.call-start = ((), (), s32[]{:S(2)}) async-start(), calls=%async_computation.11 | async-start | bytes 14155776 | tf_op jit(solution)/shard_map/all_gather | solution.py:271
  648.4 35.8 %copy-start.47 = (f32[768]{0:T(1024)S(1)}, f32[768]{0:T(1024)}, u32[]{:S(2)}) copy-start(f32[768]{0:T(1024)} %convert_element_type.166) | copy-start | bytes 9220
  744.6 744.8 %reduce-scatter.9.cloned.1.call-start = ((), (), s32[]{:S(2)}) async-start(), calls=%async_computation.14 | async-start | bytes 9732096 | tf_op jit(solution)/shard_map/reduce_scatter | solution.py:208
  773.8 716.3 %reduce-scatter.11.cloned.1.call-start = ((), (), s32[]{:S(2)}) async-start(), calls=%async_computation.16 | async-start | bytes 9732096 | tf_op jit(solution)/shard_map/reduce_scatter | solution.py:210
  1027.6 33.5 %copy-start.21 = (f32[1024,768]{1,0:T(8,128)S(1)}, f32[1024,768]{1,0:T(8,128)}, u32[]{:S(2)}) copy-start(f32[1024,768]{1,0:T(8,128)} %get-tuple-element.1039) | copy-start | bytes 9437188
  1071.5 526.7 %reduce-scatter.13.cloned.1.call-start = ((), (), s32[]{:S(2)}) async-start(), calls=%async_computation.18 | async-start | bytes 7299072 | tf_op jit(solution)/shard_map/reduce_scatter | solution.py:321
  1482.7 220.5 %reduce-scatter.7.cloned.1.call-start = ((), (), s32[]{:S(2)}) async-start(), calls=%async_computation.13 | async-start | bytes 2433024 | tf_op jit(solution)/shard_map/reduce_scatter | solution.py:324
  1484.5 113.7 %copy-start.67 = (u32[32]{0:T(128)S(1)}, u32[32]{0:T(128)}, u32[]{:S(2)}) copy-start(u32[32]{0:T(128)} %constant.394) | copy-start | bytes 388
  1489.2 110.9 %copy-start.41 = (f32[12,64]{1,0:T(8,128)S(1)}, f32[12,64]{1,0:T(8,128)}, u32[]{:S(2)}) copy-start(f32[12,64]{1,0:T(8,128)} %get-tuple-element.1044) | copy-start | bytes 9220
  1489.2 111.0 %copy-start.46 = (f32[1024]{0:T(1024)S(1)}, f32[1024]{0:T(1024)}, u32[]{:S(2)}) copy-start(f32[1024]{0:T(1024)} %get-tuple-element.945) | copy-start | bytes 12292
  1489.2 111.0 %copy-start.45 = (f32[1024]{0:T(1024)S(1)}, f32[1024]{0:T(1024)}, u32[]{:S(2)}) copy-start(f32[1024]{0:T(1024)} %get-tuple-element.944) | copy-start | bytes 12292
  1489.2 111.0 %copy-start.44 = (f32[1024]{0:T(1024)S(1)}, f32[1024]{0:T(1024)}, u32[]{:S(2)}) copy-start(f32[1024]{0:T(1024)} %get-tuple-element.946) | copy-start | bytes 12292
  1489.2 281.4 %copy-start.50 = (f32[768]{0:T(1024)S(1)}, f32[768]{0:T(1024)}, u32[]{:S(2)}) copy-start(f32[768]{0:T(1024)} %get-tuple-element.942) | copy-start | bytes 9220
  1489.2 281.4 %copy-start.51 = (f32[768]{0:T(1024)S(1)}, f32[768]{0:T(1024)}, u32[]{:S(2)}) copy-start(f32[768]{0:T(1024)} %get-tuple-element.948) | copy-start | bytes 9220
  1489.3 281.4 %copy-start.52 = (f32[768]{0:T(1024)S(1)}, f32[768]{0:T(1024)}, u32[]{:S(2)}) copy-start(f32[768]{0:T(1024)} %get-tuple-element.1038) | copy-start | bytes 9220
  1489.3 281.4 %copy-start.53 = (f32[768]{0:T(1024)S(1)}, f32[768]{0:T(1024)}, u32[]{:S(2)}) copy-start(f32[768]{0:T(1024)} %get-tuple-element.1040) | copy-start | bytes 9220
  1489.3 281.4 %copy-start.55 = (f32[3072]{0:T(1024)S(1)}, f32[3072]{0:T(1024)}, u32[]{:S(2)}) copy-start(f32[3072]{0:T(1024)} %get-tuple-element.1073) | copy-start | bytes 36868
  1489.3 281.4 %copy-start.56 = (f32[768]{0:T(1024)S(1)}, f32[768]{0:T(1024)}, u32[]{:S(2)}) copy-start(f32[768]{0:T(1024)} %get-tuple-element.935) | copy-start | bytes 9220
  1489.3 281.4 %copy-start.57 = (f32[768]{0:T(1024)S(1)}, f32[768]{0:T(1024)}, u32[]{:S(2)}) copy-start(f32[768]{0:T(1024)} %get-tuple-element.941) | copy-start | bytes 9220
  1489.3 347.6 %copy-start.6 = (f32[1024,768]{1,0:T(8,128)S(1)}, f32[1024,768]{1,0:T(8,128)}, u32[]{:S(2)}) copy-start(f32[1024,768]{1,0:T(8,128)} %copy-done.5) | copy-start | bytes 9437188
  1489.3 249.0 %all-gather.31.cloned.1.call-start = ((), (), s32[]{:S(2)}) async-start(), calls=%async_computation.15 | async-start | bytes 2654208 | tf_op jit(solution)/shard_map/all_gather | solution.py:337
  1490.1 280.5 %all-gather.33.cloned.1.call-start = ((), (), s32[]{:S(2)}) async-start(), calls=%async_computation.17 | async-start | bytes 2654208 | tf_op jit(solution)/shard_map/all_gather | solution.py:339
  1490.7 354.8 %all-gather.29.cloned.1.call-start = ((), (), s32[]{:S(2)}) async-start(), calls=%async_computation.12 | async-start | bytes 1990656 | tf_op jit(solution)/shard_map/all_gather | solution.py:330
  (68 other events, 265.8 us)
Sparse Core Ops, SparseCore 0:
  9.9 49.3 all-gather.12
  72.7 117.6 all-gather.14
  192.5 115.3 all-gather.16
  309.6 25.4 all-gather.18
  336.8 57.0 all-gather.20
  395.6 57.0 all-gather.22
  454.3 117.5 all-gather.24
  744.7 116.2 all-gather.26
  867.0 131.4 reduce-scatter.8
  1071.6 131.8 reduce-scatter.10
  1482.8 115.3 reduce-scatter.12
  1604.8 98.3 reduce-scatter.6
  1704.8 33.5 all-gather.30
  1739.8 30.7 all-gather.32
  1772.1 26.2 all-gather.28
where the time goes:
time: 1870 us; the launch traced here: 1860 us
  matrix products  898 us (48%)
  waiting for transfers between devices  492 us (26%)
  local copies, waits for them, and re-layouts  184 us (10%)
  blocking collectives  134 us (7%)
  other arithmetic  132 us (7%)
    dot_general x8, matrix products, query_inner(): jnp.einsum('shqk,skhd->sqhd', grad_scores, key_part, preferred_element_ty...  150 us
    dot_general x8, matrix products, key_inner(): jnp.einsum('shqk,sqhd->skhd', grad_scores, query_part, preferred_element_...  131 us
    dot_general x8, matrix products, key_inner(): jnp.einsum('shqk,sqhd->skhd', weights.astype(jnp.bfloat16), grad_part, pr...  110 us
    reduce_scatter x1, waiting for transfers between devices, shards(): lax.psum_scatter(grad_qkv_weight, ('dp', 'ctx'), scatter_dimension=0, til...  107 us
    all_gather x1, waiting for transfers between devices, shards(): value_piece = lax.all_gather(values, 'ctx', axis=1, tiled=True)  103 us
    reduce_scatter x1, waiting for transfers between devices, shards(): lax.psum_scatter(grad_out_weight, ('dp', 'ctx'), scatter_dimension=0, til...  102 us
    dot_general x8, matrix products, attend_inner(): jnp.einsum('sqhd,skhd->shqk', queries, key_part, preferred_element_type=j...  102 us
    reduce_sum x8, other arithmetic, attend_inner(): total = total * factor + jnp.sum(weights, axis=3)  96.4 us
  transfers between devices with their start and end apart: 15, of which 7 were waited for; matrix products, arithmetic and copies ran while one was open for 63% of the time, Pallas kernels for 0%

commit v1 on v0

v1 whole, which is shorter than its diff:
```python
import functools

import jax
import jax.numpy as jnp
from jax import lax
from jax.experimental import pallas as pl
from jax.experimental.pallas import tpu as pltpu
from jax.sharding import PartitionSpec as P

HEADS = 12

norm_eps = 1e-12
rms_eps = 1e-06
masked_bias = -1e30
log2_e = 1.4426950408889634
lanes = 128
vmem_grant = 56 << 20
f32 = jnp.float32
bf16 = jnp.bfloat16


def norm_parts(total, gain, shift):
    mean = jnp.mean(total, axis=-1, keepdims=True)
    centred = total - mean
    inverse = lax.rsqrt(jnp.mean(centred * centred, axis=-1, keepdims=True) + norm_eps)
    unit = centred * inverse
    return (unit * gain + shift, unit, inverse)


def norm_back(grad_unit, unit, inverse):
    mean_grad = jnp.mean(grad_unit, axis=-1, keepdims=True)
    mean_cross = jnp.mean(grad_unit * unit, axis=-1, keepdims=True)
    return inverse * (grad_unit - mean_grad - unit * mean_cross)


def dot(left, right, left_dim, right_dim):
    return lax.dot_general(
        left, right, (((left_dim,), (right_dim,)), ((), ())), preferred_element_type=f32
    )


def head_lanes(head, head_dim):
    lane = lax.broadcasted_iota(jnp.int32, (1, lanes), 1)
    return (lane // head_dim) == head


def spread_lanes(first_head, second_head, unit, head_dim):
    rows = first_head.shape[0]
    lane = lax.broadcasted_iota(jnp.int32, (rows, lanes), 1)
    place = lane % head_dim
    value = -jnp.where(lane < head_dim, second_head, first_head)
    high = value.astype(bf16).astype(f32)
    rest = value - high
    mid = rest.astype(bf16).astype(f32)
    low = rest - mid
    out = jnp.where(place == 1, high, jnp.where(place == 2, mid, jnp.where(place == 3, low, 0.0)))
    return jnp.where(place == 0, unit, out).astype(bf16)


def attend_kernel(scale, head_dim, step, q_ref, k_ref, v_ref, extra_ref, o_ref, stat_ref, kb, vb):
    keys = k_ref.shape[0]

    @pl.when(pl.program_id(1) == 0)
    def _():
        for h in range(2):
            kb[h] = jnp.where(head_lanes(h, head_dim), k_ref[...], extra_ref[...])
            vb[h] = jnp.where(head_lanes(h, head_dim), v_ref[...], extra_ref[...])

    factor = scale * log2_e
    queries = q_ref[...]
    lane = lax.broadcasted_iota(jnp.int32, (1, lanes), 1)
    bias_lane = jnp.where(lane % head_dim == 0, 1.0, 0.0).astype(bf16)
    outs, logs = ([], [])
    for h in range(2):
        own = jnp.where(head_lanes(h, head_dim), queries, bias_lane)
        best, acc = (None, None)
        for first in range(0, keys, step):
            scores = dot(own, kb[h, first : first + step, :], 1, 1)
            high = jnp.max(scores, axis=1, keepdims=True)
            new_best = high if best is None else jnp.maximum(best, high)
            weights = jnp.exp2((scores - new_best) * factor).astype(bf16)
            part = dot(weights, vb[h, first : first + step, :], 1, 0)
            acc = part if best is None else acc * jnp.exp2((best - new_best) * factor) + part
            best = new_best
        free = (1 - h) * head_dim + 1
        total = acc[:, free : free + 1]
        outs.append(acc / total)
        logs.append(best + jnp.log2(total) * (1.0 / factor))
    o_ref[...] = jnp.where(head_lanes(0, head_dim), outs[0], outs[1]).astype(bf16)
    stat_ref[...] = spread_lanes(logs[0], logs[1], 1.0, head_dim)


def attend(queries, both, extra, head_dim):
    rows, width = queries.shape
    keys = both.shape[0]
    pairs = width // lanes
    row_step = min(512, rows)
    step = min(2048, keys)
    scale = head_dim ** (-0.5)
    return pl.pallas_call(
        functools.partial(attend_kernel, scale, head_dim, step),
        grid=(pairs, rows // row_step),
        in_specs=[
            pl.BlockSpec((row_step, lanes), lambda h, i: (i, h)),
            pl.BlockSpec((keys, lanes), lambda h, i: (0, h)),
            pl.BlockSpec((keys, lanes), lambda h, i: (0, h + pairs)),
            pl.BlockSpec((keys, lanes), lambda h, i: (0, 0)),
        ],
        out_specs=[
            pl.BlockSpec((row_step, lanes), lambda h, i: (i, h)),
            pl.BlockSpec((None, row_step, lanes), lambda h, i: (h, i, 0)),
        ],
        out_shape=[
            jax.ShapeDtypeStruct((rows, width), bf16),
            jax.ShapeDtypeStruct((pairs, rows, lanes), bf16),
        ],
        scratch_shapes=[pltpu.VMEM((2, keys, lanes), bf16), pltpu.VMEM((2, keys, lanes), bf16)],
        compiler_params=pltpu.CompilerParams(vmem_limit_bytes=vmem_grant),
        cost_estimate=pl.CostEstimate(
            flops=4 * rows * keys * width * 4,
            bytes_accessed=keys * width * 4 + rows * width * 6,
            transcendentals=rows * keys * width // head_dim,
        ),
        name="attend",
    )(queries, both, both, extra)


def attend_back_kernel(scale, head_dim, row_step, resumed, *refs):
    q_ref, da_ref, qx_ref, dax_ref, k_ref, v_ref, extra_ref = refs[:7]
    start_ref = refs[7] if resumed else None
    dq_ref, dkv_ref = refs[-2:]
    j = pl.program_id(1)
    rows = q_ref.shape[0]
    factor = scale * log2_e
    keys, values, extra = (k_ref[...], v_ref[...], extra_ref[...])
    dk, dv = (None, None)
    for first in range(0, rows, row_step):
        part = slice(first, first + row_step)
        queries, grads = (q_ref[part, :], da_ref[part, :])
        queries_extra, grads_extra = (qx_ref[part, :], dax_ref[part, :])
        dq = None
        for h in range(2):
            sel = head_lanes(h, head_dim)
            scores = dot(
                jnp.where(sel, queries, queries_extra), jnp.where(sel, keys, extra), 1, 1
            )
            weights = jnp.exp2(scores * factor)
            grad_weights = dot(
                jnp.where(sel, grads, grads_extra), jnp.where(sel, values, extra), 1, 1
            )
            grad_scores = (weights * grad_weights).astype(bf16)
            none = jnp.zeros_like(queries)
            part_dv = dot(jnp.where(sel, grads, none), weights.astype(bf16), 0, 0)
            part_dk = dot(jnp.where(sel, queries, none), grad_scores, 0, 0)
            part_dq = dot(grad_scores, jnp.where(sel, keys, jnp.zeros_like(keys)), 1, 0)
            dv = part_dv if dv is None else dv + part_dv
            dk = part_dk if dk is None else dk + part_dk
            dq = part_dq if dq is None else dq + part_dq
        dq = dq * scale

        @pl.when(j == 0)
        def _():
            dq_ref[part, :] = dq + start_ref[part, :] if resumed else dq

        @pl.when(j > 0)
        def _():
            dq_ref[part, :] += dq

    dkv_ref[0] = (dk * scale).astype(bf16)
    dkv_ref[1] = dv.astype(bf16)


def attend_back(queries, grads, stats, deltas, both, extra, head_dim, first, count, start):
    rows, width = queries.shape
    pairs = width // lanes
    row_step = min(1024, rows)
    step = min(512, count)
    skip = first // step
    scale = head_dim ** (-0.5)
    resumed = start is not None
    more = [pl.BlockSpec((rows, lanes), lambda h, j: (0, h))] if resumed else []
    return pl.pallas_call(
        functools.partial(attend_back_kernel, scale, head_dim, row_step, resumed),
        grid=(pairs, count // step),
        in_specs=[
            pl.BlockSpec((rows, lanes), lambda h, j: (0, h)),
            pl.BlockSpec((rows, lanes), lambda h, j: (0, h)),
            pl.BlockSpec((None, rows, lanes), lambda h, j: (h, 0, 0)),
            pl.BlockSpec((None, rows, lanes), lambda h, j: (h, 0, 0)),
            pl.BlockSpec((step, lanes), lambda h, j: (j + skip, h)),
            pl.BlockSpec((step, lanes), lambda h, j: (j + skip, h + pairs)),
            pl.BlockSpec((step, lanes), lambda h, j: (j + skip, 0)),
        ]
        + more,
        out_specs=[
            pl.BlockSpec((rows, lanes), lambda h, j: (0, h)),
            pl.BlockSpec((2, lanes, step), lambda h, j: (0, h, j)),
        ],
        out_shape=[
            jax.ShapeDtypeStruct((rows, width), f32),
            jax.ShapeDtypeStruct((2, width, count), bf16),
        ],
        compiler_params=pltpu.CompilerParams(vmem_limit_bytes=vmem_grant),
        cost_estimate=pl.CostEstimate(
            flops=10 * rows * count * width * 4,
            bytes_accessed=count * width * 8 + rows * width * 12,
            transcendentals=rows * count * width // head_dim,
        ),
        name="attend_back",
    )(queries, grads, stats, deltas, both, both, extra, *([start] if resumed else []))


def key_lanes(live, head_dim):
    lane = jnp.arange(lanes, dtype=jnp.int32) % head_dim
    bias = jnp.where(live, 0.0, masked_bias)[:, None]
    ones = jnp.where((lane >= 1) & (lane <= 3), 1.0, 0.0)[None, :]
    return jnp.where(lane[None, :] == 0, bias, ones).astype(bf16)


def middle_kernel(
    head_dim,
    chunk,
    mixed_ref,
    x_ref,
    cot_ref,
    live_ref,
    out_ref,
    up_ref,
    down_ref,
    vec_ref,
    up_bias_ref,
    y_ref,
    active_ref,
    hidden_ref,
    dbranch_ref,
    dupper_ref,
    dz_ref,
    dattn_ref,
    dmixed_ref,
    delta_ref,
    sums_ref,
    up_sum_ref,
    slope,
):
    width = x_ref.shape[1]
    inner = up_ref.shape[1]
    out_bias, gain_first, shift_first = (vec_ref[0:1, :], vec_ref[1:2, :], vec_ref[2:3, :])
    down_bias, gain_second, shift_second = (vec_ref[3:4, :], vec_ref[4:5, :], vec_ref[5:6, :])
    live = live_ref[...]
    mixed = mixed_ref[...]
    attn = dot(mixed, out_ref[...], 1, 0) + out_bias
    hidden, unit_first, inverse_first = norm_parts(
        x_ref[...].astype(f32) + attn, gain_first, shift_first
    )
    hidden_low = hidden.astype(bf16)
    hidden_ref[...] = hidden_low
    branch = down_bias
    for first in range(0, inner, chunk):
        part = slice(first, first + chunk)
        upper = dot(hidden_low, up_ref[:, part], 1, 0) + up_bias_ref[:, part]
        below = 0.5 + 0.5 * lax.erf(upper * (0.5**0.5))
        active = (upper * below).astype(bf16)
        bell = jnp.exp2(upper * upper * (-0.5 * log2_e)) * 0.3989422804014327
        slope[:, part] = (below + upper * bell).astype(bf16)
        active_ref[:, part] = active
        branch = branch + dot(active, down_ref[part, :], 1, 0)
    normed, unit_second, inverse_second = norm_parts(hidden + branch, gain_second, shift_second)
    result = normed * live
    y_ref[...] = result.astype(bf16)
    grad_out = cot_ref[...].astype(f32) * live
    grad_second = norm_back(grad_out * gain_second, unit_second, inverse_second)
    grad_branch = grad_second.astype(bf16)
    dbranch_ref[...] = grad_branch
    grad_hidden = grad_second
    up_sums = []
    for first in range(0, inner, chunk):
        part = slice(first, first + chunk)
        grad_active = dot(grad_branch, down_ref[part, :], 1, 1)
        grad_upper = (grad_active * slope[:, part].astype(f32)).astype(bf16)
        dupper_ref[:, part] = grad_upper
        up_sums.append(jnp.sum(grad_upper.astype(f32), axis=0, keepdims=True))
        grad_hidden = grad_hidden + dot(grad_upper, up_ref[:, part], 1, 1)
    grad_first = norm_back(grad_hidden * gain_first, unit_first, inverse_first)
    dz_ref[...] = grad_first
    grad_attn = grad_first.astype(bf16)
    dattn_ref[...] = grad_attn
    grad_mixed = dot(grad_attn, out_ref[...], 1, 1).astype(bf16)
    dmixed_ref[...] = grad_mixed
    cross = grad_mixed.astype(f32) * mixed.astype(f32)
    lane = lax.broadcasted_iota(jnp.int32, (1, lanes), 1)
    lower = lane < head_dim
    for p in range(width // lanes):
        pair = cross[:, p * lanes : (p + 1) * lanes]
        first_head = jnp.sum(jnp.where(lower, pair, 0.0), axis=1, keepdims=True)
        second_head = jnp.sum(jnp.where(lower, 0.0, pair), axis=1, keepdims=True)
        delta_ref[p] = spread_lanes(first_head, second_head, 0.0, head_dim)
    sums = [
        grad_attn.astype(f32),
        grad_hidden * unit_first,
        grad_hidden,
        grad_branch.astype(f32),
        grad_out * unit_second,
        grad_out,
        result * result,
        attn * attn * live,
        branch * branch * live,
    ]
    first_step = pl.program_id(0) == 0

    @pl.when(first_step)
    def _():
        sums_ref[...] = jnp.zeros_like(sums_ref)
        up_sum_ref[...] = jnp.zeros_like(up_sum_ref)

    for i, value in enumerate(sums):
        sums_ref[i : i + 1, :] += jnp.sum(value, axis=0, keepdims=True)
    up_sum_ref[0:1, :] += jnp.concatenate(up_sums, axis=1)


def middle(mixed, rows, cot, live, out_all, up_all, down_all, vectors, up_bias, head_dim):
    count, width = rows.shape
    inner = up_all.shape[1]
    pairs = width // lanes
    row_step = min(256, count)
    chunk = min(768, inner)

    def fixed(shape):
        return pl.BlockSpec(shape, lambda i: (0, 0), pipeline_mode=pl.Buffered(1))

    def block(columns):
        return pl.BlockSpec((row_step, columns), lambda i: (i, 0))

    return pl.pallas_call(
        functools.partial(middle_kernel, head_dim, chunk),
        grid=(count // row_step,),
        in_specs=[
            block(width),
            block(width),
            block(width),
            block(1),
            fixed((width, width)),
            fixed((width, inner)),
            fixed((inner, width)),
            fixed(vectors.shape),
            fixed(up_bias.shape),
        ],
        out_specs=[
            block(width),
            block(inner),
            block(width),
            block(width),
            block(inner),
            block(width),
            block(width),
            block(width),
            pl.BlockSpec((pairs, row_step, lanes), lambda i: (0, i, 0)),
            pl.BlockSpec((16, width), lambda i: (0, 0)),
            pl.BlockSpec((8, inner), lambda i: (0, 0)),
        ],
        out_shape=[
            jax.ShapeDtypeStruct((count, width), bf16),
            jax.ShapeDtypeStruct((count, inner), bf16),
            jax.ShapeDtypeStruct((count, width), bf16),
            jax.ShapeDtypeStruct((count, width), bf16),
            jax.ShapeDtypeStruct((count, inner), bf16),
            jax.ShapeDtypeStruct((count, width), f32),
            jax.ShapeDtypeStruct((count, width), bf16),
            jax.ShapeDtypeStruct((count, width), bf16),
            jax.ShapeDtypeStruct((pairs, count, lanes), bf16),
            jax.ShapeDtypeStruct((16, width), f32),
            jax.ShapeDtypeStruct((8, inner), f32),
        ],
        scratch_shapes=[pltpu.VMEM((row_step, inner), bf16)],
        compiler_params=pltpu.CompilerParams(vmem_limit_bytes=vmem_grant),
        cost_estimate=pl.CostEstimate(
            flops=4 * count * width * (2 * inner + width),
            bytes_accessed=4 * width * inner + count * (18 * width + 4 * inner),
            transcendentals=4 * count * inner,
        ),
        name="middle",
    )(mixed, rows, cot, live, out_all, up_all, down_all, vectors, up_bias)


def up_out_kernel(blocks, hidden_ref, dupper_ref, mixed_ref, dattn_ref, o_ref):
    s = pl.program_id(0)

    @pl.when(s < blocks)
    def _():
        o_ref[...] = dot(hidden_ref[...], dupper_ref[...], 0, 0).astype(bf16).reshape(o_ref.shape)

    @pl.when(s == blocks)
    def _():
        o_ref[...] = dot(mixed_ref[...], dattn_ref[...], 0, 0).astype(bf16).reshape(o_ref.shape)


def down_kernel(active_ref, dbranch_ref, held_ref, o_ref):
    del held_ref
    o_ref[...] = dot(active_ref[...], dbranch_ref[...], 0, 0).astype(bf16).reshape(o_ref.shape)


def middle_grads(hidden, dupper, mixed, dattn, active, dbranch, owners, ring):
    count, width = hidden.shape
    inner = dupper.shape[1]
    devices = owners * ring
    share = width // devices
    blocks = inner // width
    tall = inner // devices
    piece = blocks * share + tall + share
    shape = jax.ShapeDtypeStruct((devices, piece, width), bf16)
    params = pltpu.CompilerParams(vmem_limit_bytes=vmem_grant)
    whole = pl.BlockSpec((count, width), lambda s: (0, 0))
    held = pl.pallas_call(
        functools.partial(up_out_kernel, blocks),
        grid=(blocks + 1,),
        in_specs=[
            whole,
            pl.BlockSpec((count, width), lambda s: (0, jnp.minimum(s, blocks - 1))),
            whole,
            whole,
        ],
        out_specs=pl.BlockSpec(
            (devices, share, width),
            lambda s: (0, jnp.where(s < blocks, s, piece // share - 1), 0),
        ),
        out_shape=shape,
        compiler_params=params,
        cost_estimate=pl.CostEstimate(
            flops=2 * count * width * (inner + width),
            bytes_accessed=2 * (count + width) * (inner + 3 * width),
            transcendentals=0,
        ),
        name="up_grads",
    )(hidden, dupper, mixed, dattn)
    return pl.pallas_call(
        down_kernel,
        grid=(owners,),
        in_specs=[
            pl.BlockSpec((count, inner // owners), lambda s: (0, s)),
            whole,
            pl.BlockSpec(memory_space=pl.ANY),
        ],
        out_specs=pl.BlockSpec((ring, tall, width), lambda s: (s, blocks * share // tall, 0)),
        out_shape=shape,
        input_output_aliases={2: 0},
        compiler_params=params,
        cost_estimate=pl.CostEstimate(
            flops=2 * count * width * inner,
            bytes_accessed=2 * (count + width) * (inner + width),
            transcendentals=0,
        ),
        name="down_grads",
    )(active, dbranch, held)


def shards(
    ring,
    tokens,
    cotangent,
    lengths,
    block_order,
    qkv_weight,
    query_bias,
    value_bias,
    out_weight,
    out_bias,
    attn_gain,
    attn_shift,
    up_weight,
    up_bias,
    down_weight,
    down_bias,
    ffn_gain,
    ffn_shift,
):
    seqs, block, width = tokens.shape
    head_dim = width // HEADS
    assert seqs == 2 and ring % 4 == 0
    half = ring // 2
    here = lax.axis_index("ctx")
    side = here // half

    def pick(array, index):
        return lax.dynamic_index_in_dim(array, index, 0, keepdims=False)

    def exchange(array, bit):
        return lax.ppermute(array, "ctx", [(i, i ^ bit) for i in range(ring)])

    def to_home(kept, sent):
        other = exchange(sent, half)
        first = jnp.where(side == 0, kept, other)
        second = jnp.where(side == 0, other, kept)
        return jnp.stack([first, second])

    def gather(array):
        return lax.all_gather(array, "dp", axis=0, tiled=True)

    qkv_all = gather(qkv_weight)
    own = pick(tokens, side)
    moved = exchange(pick(tokens, 1 - side), half)
    bits = []
    bit = half // 2
    while bit:
        bits.append(bit)
        bit //= 2
    ids = jnp.stack([here, here ^ half])
    pieces = [own, moved, exchange(own, bits[0]), exchange(moved, bits[0])]
    ids = jnp.concatenate([ids, ids ^ bits[0]])
    stream = jnp.concatenate(pieces, axis=0)
    for bit in bits[1:]:
        stream = jnp.concatenate([stream, exchange(stream, bit)], axis=0)
        ids = jnp.concatenate([ids, ids ^ bit])
    rows = stream[: 2 * block]
    count_rows = 2 * block

    order = pick(block_order, side)
    length = pick(lengths, side)
    table = jnp.arange(ring, dtype=jnp.int32)
    place_of = jnp.sum(jnp.where(ids[:, None] == table[None, :], order[None, :], 0), axis=1)
    places = place_of[:, None] * block + jnp.arange(block, dtype=jnp.int32)[None, :]
    live_keys = (places < length).reshape(-1)
    live_rows = live_keys[:count_rows, None].astype(f32)
    extra = key_lanes(live_keys, head_dim)

    row = lax.axis_index("dp")
    owners = lax.axis_size("dp")
    singles = [
        query_bias,
        value_bias,
        out_bias,
        attn_gain,
        attn_shift,
        down_bias,
        ffn_gain,
        ffn_shift,
    ]
    share = query_bias.shape[0]
    packed = jnp.concatenate(singles + [up_bias])[None, :]
    held = [packed]
    for k in range(1, owners):
        held.append(lax.ppermute(packed, "dp", [(i, i ^ k) for i in range(owners)]))
    vectors = []
    for d in range(owners):
        found = held[0]
        for k in range(1, owners):
            found = jnp.where((row ^ d) == k, held[k], found)
        vectors.append(found)
    vectors = jnp.concatenate(vectors, axis=0).astype(f32)
    bias = [vectors[:, i * share : (i + 1) * share].reshape(1, width) for i in range(8)]
    up_bias_all = vectors[:, 8 * share :].reshape(1, -1)
    queries = (
        jnp.dot(rows, qkv_all[:, :width], preferred_element_type=f32) + bias[0]
    ).astype(bf16)
    kv_bias = jnp.concatenate([jnp.zeros_like(bias[1]), bias[1]], axis=1)
    both = (jnp.dot(stream, qkv_all[:, width:], preferred_element_type=f32) + kv_bias).astype(bf16)
    out_all = gather(out_weight)
    up_all = gather(up_weight)
    down_all = gather(down_weight)
    held, _ = lax.optimization_barrier((cotangent, stream))
    cot = jnp.concatenate([pick(held, side), exchange(pick(held, 1 - side), half)], axis=0)

    mixed, stats = attend(queries, both, extra, head_dim)
    (
        result,
        active,
        hidden,
        grad_branch,
        grad_upper,
        grad_first,
        grad_attn,
        grad_mixed,
        deltas,
        sums,
        up_sum,
    ) = middle(
        mixed,
        rows,
        cot,
        live_rows,
        out_all,
        up_all,
        down_all,
        jnp.concatenate(bias[2:] + [jnp.zeros((2, width), f32)], axis=0),
        up_bias_all,
        head_dim,
    )
    output = to_home(result[:block], result[block:])

    def scatter(grad):
        return lax.psum_scatter(grad, ("dp", "ctx"), scatter_dimension=0, tiled=True)

    def spread(part):
        return lax.all_gather(part, "ctx", axis=0, tiled=True)

    devices = owners * ring
    inner = up_weight.shape[1]
    laid = width % (8 * devices) == 0 and inner % width == 0
    if laid:
        piece = middle_grads(hidden, grad_upper, mixed, grad_attn, active, grad_branch, owners, ring)
        pieces = spread(scatter(piece)).astype(f32)
        each, tall = (width // devices, inner // devices)
        blocks = inner // width
        cut = blocks * each
        grad_up_weight = jnp.concatenate(
            [pieces[:, i * each : (i + 1) * each, :].reshape(share, width) for i in range(blocks)],
            axis=1,
        )
        grad_down_weight = pieces[:, cut : cut + tall, :].reshape(-1, width)
        grad_out_weight = pieces[:, cut + tall :, :].reshape(share, width)
    else:
        grad_up_weight = spread(scatter(dot(hidden, grad_upper, 0, 0).astype(bf16))).astype(f32)
        grad_down_weight = spread(scatter(dot(active, grad_branch, 0, 0).astype(bf16))).astype(f32)
        grad_out_weight = spread(scatter(dot(mixed, grad_attn, 0, 0).astype(bf16))).astype(f32)

    kv_weight = qkv_all[:, width:]
    total_keys = stream.shape[0]
    grad_queries = None
    grad_kv_weight = None
    grad_value_bias = None
    arrived = []
    last = total_keys
    for bit in list(reversed(bits)) + [0]:
        first = last // 2 if bit else 0
        grad_queries, grad_both = attend_back(
            queries, grad_mixed, stats, deltas, both, extra, head_dim, first, last - first, grad_queries
        )
        kv_grads = grad_both.reshape(2 * width, last - first)
        part = dot(stream[first:last], kv_grads, 0, 1)
        grad_kv_weight = part if grad_kv_weight is None else grad_kv_weight + part
        part = jnp.sum(grad_both[1], axis=1, dtype=f32)
        grad_value_bias = part if grad_value_bias is None else grad_value_bias + part
        grad_stream = dot(kv_grads, kv_weight, 0, 1)
        for other in arrived:
            grad_stream = grad_stream + other[first:last].astype(f32)
        if bit:
            arrived.append(exchange(grad_stream.astype(bf16), bit))
        last = first
    grad_query_low = grad_queries.astype(bf16)
    grad_rows = grad_first + dot(grad_query_low, qkv_all[:, :width], 1, 1) + grad_stream
    grad_rows_low = grad_rows.astype(bf16)
    grad_tokens = to_home(grad_rows_low[:block], grad_rows_low[block:])

    grad_query_bias = jnp.sum(grad_query_low, axis=0, dtype=f32)
    grad_qkv_weight = jnp.concatenate([dot(rows, grad_query_low, 0, 0), grad_kv_weight], axis=1)
    qkv_part = scatter(grad_qkv_weight.astype(bf16))

    small = [grad_query_bias, grad_value_bias] + [sums[i] for i in range(6)] + [up_sum[0]]
    squares = jnp.sum(sums[6:9], axis=1)
    square_sums = jnp.where(jnp.arange(2)[:, None] == side, squares[None, :], 0.0)
    slots = jnp.where(
        jnp.arange(owners)[:, None] == row, square_sums.reshape(1, -1), 0.0
    ).reshape(-1)
    summed = lax.psum(jnp.concatenate(small + [slots]), ("dp", "ctx"))
    totals = []
    start = 0
    for v in small:
        size = v.shape[0] // owners
        totals.append(lax.dynamic_slice_in_dim(summed, start + row * size, size))
        start += v.shape[0]
    seq_squares = lax.dynamic_slice_in_dim(summed, start + row * 6, 6).reshape(2, 3)
    branch_rms = jnp.sqrt(seq_squares / (lengths.astype(f32)[:, None] * width) + rms_eps)
    return (
        output,
        grad_tokens,
        spread(qkv_part).astype(f32),
        totals[0],
        totals[1],
        grad_out_weight,
        totals[2],
        totals[3],
        totals[4],
        grad_up_weight,
        totals[8],
        grad_down_weight,
        totals[5],
        totals[6],
        totals[7],
        branch_rms,
    )


def solution(mesh):
    in_specs = (
        P("dp", "ctx", None),
        P("dp", "ctx", None),
        P("dp"),
        P("dp", None),
        P("dp", None),
        P("dp"),
        P("dp"),
        P("dp", None),
        P("dp"),
        P("dp"),
        P("dp"),
        P("dp", None),
        P("dp"),
        P("dp", None),
        P("dp"),
        P("dp"),
        P("dp"),
    )
    out_specs = (
        P("dp", "ctx", None),
        P("dp", "ctx", None),
        P("dp", None),
        P("dp"),
        P("dp"),
        P("dp", None),
        P("dp"),
        P("dp"),
        P("dp"),
        P("dp", None),
        P("dp"),
        P("dp", None),
        P("dp"),
        P("dp"),
        P("dp"),
        P("dp", None),
    )
    return jax.shard_map(
        functools.partial(shards, mesh.shape["ctx"]),
        mesh=mesh,
        in_specs=in_specs,
        out_specs=out_specs,
        check_vma=False,
    )
```

time: 1870 us -> 665 us (0.36)
  matrix products: 898 us -> 61.7 us
  waiting for transfers between devices: 492 us -> 118 us
  Pallas kernels: 0 us -> 283 us
  local copies, waits for them, and re-layouts: 184 us -> 26.2 us
  other arithmetic: 132 us -> 25.6 us
  blocking collectives: 134 us -> 113 us
    dot_general x68 -> x10, matrix products: 898 us -> 61.7 us  [the longest x8 42.6 us: dot(): lax.dot_general(left, right, (((left_dim,), (right_dim,)), ((), ())), pre...]
    pallas_call x0 -> x7, Pallas kernels: none -> 283 us  [the longest x3 150 us: attend_back(): pl.pallas_call(functools.partial(attend_back_kernel, scale, head_dim, row...]
    all_gather x11 -> x5, waiting for transfers between devices: 279 us -> 27.2 us  [the longest x4 27.2 us: gather(): return lax.all_gather(array, 'dp', axis=0, tiled=True)]
    reduce_scatter x4 -> x2, waiting for transfers between devices: 210 us -> 0.02 us  [scatter(): lax.psum_scatter(grad, ('dp', 'ctx'), scatter_dimension=0, tiled=True)]
    reduce_sum x36 -> x6, other arithmetic: 116 us -> 4.94 us  [the longest x3 4.39 us: shards(): part = jnp.sum(grad_both[1], axis=1, dtype=f32)]
    ppermute x0 -> x12, waiting for transfers between devices: none -> 88.6 us  [the longest x9 88.6 us: exchange(): return lax.ppermute(array, 'ctx', [(i, i ^ bit) for i in range(ring)])]
    unnamed x3 -> x0, blocking collectives: 75.8 us -> none
    psum x0 -> x1, blocking collectives: none -> 65.4 us  [shards(): summed = lax.psum(jnp.concatenate(small + [slots]), ('dp', 'ctx'))]
  transfers between devices with their start and end apart: 15 -> 19, of which waited for: 7 -> 4; matrix products, arithmetic and copies ran while one was open for 63% -> 16% of each run, Pallas kernels for 0% -> 34%
where the time goes in v1:
time: 665 us; the launch traced here: 658 us
  Pallas kernels  283 us (43%)
  waiting for transfers between devices  118 us (18%)
  blocking collectives  113 us (17%)
  matrix products  61.7 us (9%)
  local copies, waits for them, and re-layouts  26.2 us (4%)
  other arithmetic  25.6 us (4%)
  starting transfers between devices  16 us (2%)
  between operations  14.9 us (2%)
    pallas_call x3, Pallas kernels, attend_back(): pl.pallas_call(functools.partial(attend_back_kernel, scale, head_dim, row...  150 us
    ppermute x9, waiting for transfers between devices, exchange(): return lax.ppermute(array, 'ctx', [(i, i ^ bit) for i in range(ring)])  88.6 us
    pallas_call x1, Pallas kernels, attend(): pl.pallas_call(functools.partial(attend_kernel, scale, head_dim, step), g...  71.1 us
    psum x1, blocking collectives, shards(): summed = lax.psum(jnp.concatenate(small + [slots]), ('dp', 'ctx'))  65.4 us
    all_gather x1, blocking collectives, spread(): return lax.all_gather(part, 'ctx', axis=0, tiled=True)  47.2 us
    dot_general x8, matrix products, dot(): lax.dot_general(left, right, (((left_dim,), (right_dim,)), ((), ())), pre...  42.6 us
    pallas_call x1, Pallas kernels, middle(): pl.pallas_call(functools.partial(middle_kernel, head_dim, chunk), grid=(c...  41.4 us
    all_gather x4, waiting for transfers between devices, gather(): return lax.all_gather(array, 'dp', axis=0, tiled=True)  27.2 us
  transfers between devices with their start and end apart: 19, of which 4 were waited for; matrix products, arithmetic and copies ran while one was open for 16% of the time, Pallas kernels for 34%

profile of v1, /device:TPU:1, one launch (start us, length us, event | category | flops | bytes accessed | tf_op | source)
XLA Modules:
  0.0 658.1 jit_solution(2892994414182376646)
XLA Ops:
  9.6 2.1 dynamic-slice_bitcast_fusion.2
  11.7 3.1 collective-permute-start
  15.0 2.2 collective-permute-start.1
  21.1 28.1 %collective-permute-done = bf16[512,768]{1,0:T(8,128)(2,1)S(1)} collective-permute-done((bf16[512,768]{1,0:T(8,128)(2,1)}, bf16[512,768]{1,0:T(8,128)(2,1)S(1)}, u32[]{:S(2)}, u32[]{:S(2)}) %collective-permute-start) | collective-permute-done | bytes 786464 | tf_op jit(solution)/shard_map/ppermute | solution.py:486
  51.9 16.9 %collective-permute-done.5 = bf16[512,768]{1,0:T(8,128)(2,1)S(1)} collective-permute-done((bf16[512,768]{1,0:T(8,128)(2,1)S(1)}, bf16[512,768]{1,0:T(8,128)(2,1)S(1)}, u32[]{:S(2)}, u32[]{:S(2)}) %collective-permute-start.5) | collective-permute-done | bytes 786464 | tf_op jit(solution)/shard_map/ppermute | solution.py:486
  70.8 2.4 collective-permute-start.6
  82.1 3.8 constant_dynamic-update-slice_fusion
  86.9 4.0 add_convert_fusion.4.q_ref.refs_0_
  90.8 15.2 %add_convert_fusion.k_ref.v_ref.refs_4_.refs_5_ = bf16[4096,1536]{1,0:T(8,128)(2,1)} fusion(bf16[4096,768]{1,0:T(8,128)(2,1)} %constant_dynamic-update-slice_fusion, f32[1536]{0:T(1024)S(1)} %pad_reduce_fusion, bf16[768,2304]{1,0:T(8,128)(2,1)S(1)} %copy-done.19), kind=kOutput, calls=%fused_computation | convolution fusion | flops 9676259328 | bytes 21241856 | tf_op jit(solution)/shard_map/dot_general | solution.py:554
  106.0 71.1 %attend.1 = (bf16[1024,768]{1,0:T(8,128)(2,1)}, bf16[6,1024,128]{2,1,0:T(8,128)(2,1)}) custom-call(bf16[1024,768]{1,0:T(8,128)(2,1)} %add_convert_fusion.4.q_ref.refs_0_, bf16[4096,1536]{1,0:T(8,128)(2,1)} %add_convert_fusion.k_ref.v_ref.refs_4_.refs_5_, bf16[4096,1536]{1,0:T(8,128)(2,1)} %add_convert_fusion.k_ref.v_ref.refs_4_.refs_5_, ...), custom_call_target="tpu_custom_call" | custom-call | flops 51539607552 | bytes 17301504 | tf_op jit(solution)/shard_map/attend/pallas_call | solution.py:100
  177.1 2.4 pad_maximum_fusion.4.cot_ref
  179.5 27.2 %all-gather.12.cloned.1.call-done.down_ref = bf16[3072,768]{1,0:T(8,128)(2,1)} async-done(((bf16[768,768]{1,0:T(8,128)(2,1)}), bf16[3072,768]{1,0:T(8,128)(2,1)}) %all-gather.12.cloned.1.call-update) | async-done | bytes 4718608 | tf_op jit(solution)/shard_map/all_gather | solution.py:495
  206.7 41.4 %middle.1 = (bf16[1024,768]{1,0:T(8,128)(2,1)}, bf16[1024,3072]{1,0:T(8,128)(2,1)}, bf16[1024,768]{1,0:T(8,128)(2,1)}, bf16[1024,768]{1,0:T(8,128)(2,1)}, bf16[1...) custom-call(bf16[1024,768]{1,0:T(8,128)(2,1)} %get-tuple-element.36., ...), custom_call_target="tpu_custom_call" | custom-call | flops 21743271936 | bytes 36175872 | tf_op jit(solution)/shard_map/middle/pallas_call | solution.py:333
  248.1 11.7 %up_grads.1.held_ref = bf16[32,216,768]{2,1,0:T(8,128)(2,1)} custom-call(bf16[1024,768]{1,0:T(8,128)(2,1)} %get-tuple-element.53.hidden_ref, bf16[1024,3072]{1,0:T(8,128)(2,1)} %get-tuple-element.54.dupper_ref, bf16[1024,768]{1,0:T(8,128)(2,1)} %get-tuple-element.36.mixed_ref, bf16[1024,768]{1,0:T(8,128)(2,1)} %get-tuple-element.55.dattn_ref), custom_call_target="tpu_custom_call" | custom-call | flops 6039797760 | bytes 19267584 | tf_op jit(solution)/shard_map/up_grads/pallas_call | solution.py:412
  259.8 9.3 %down_grads.1 = bf16[32,216,768]{2,1,0:T(8,128)(2,1)} custom-call(bf16[1024,3072]{1,0:T(8,128)(2,1)} %get-tuple-element.51.active_ref, bf16[1024,768]{1,0:T(8,128)(2,1)} %get-tuple-element.52.dbranch_ref, bf16[32,216,768]{2,1,0:T(8,128)(2,1)} %up_grads.1.held_ref), custom_call_target="tpu_custom_call", output_to_operand_aliasing={{}: (2, {})} | custom-call | flops 4831838208 | bytes 13762560 | tf_op jit(solution)/shard_map/down_grads/pallas_call | solution.py:434
  269.1 73.6 %attend_back.3 = (f32[1024,768]{1,0:T(8,128)}, bf16[2,768,2048]{2,1,0:T(8,128)(2,1)}) custom-call(bf16[1024,768]{1,0:T(8,128)(2,1)} %add_convert_fusion.4.q_ref.refs_0_, bf16[1024,768]{1,0:T(8,128)(2,1)} %get-tuple-element.40.refs_1_, bf16[6,1024,128]{2,1,0:T(8,128)(2,1)} %get-tuple-element.41.refs_2_, bf16[6,1024,128]{2,1,0:T(8,128)(2,1)} %get-tuple-element.42.refs_3_, ...), custom_call_target="tpu_custom_call" | custom-call | flops 64424509440 | bytes 22020096 | tf_op jit(solution)/shard_map/attend_back/pallas_call | solution.py:182
  342.7 38.1 %attend_back.4 = (f32[1024,768]{1,0:T(8,128)}, bf16[2,768,1024]{2,1,0:T(8,128)(2,1)}) custom-call(bf16[1024,768]{1,0:T(8,128)(2,1)} %add_convert_fusion.4.q_ref.refs_0_, bf16[1024,768]{1,0:T(8,128)(2,1)} %get-tuple-element.40.refs_1_, bf16[6,1024,128]{2,1,0:T(8,128)(2,1)} %get-tuple-element.41.refs_2_, bf16[6,1024,128]{2,1,0:T(8,128)(2,1)} %get-tuple-element.42.refs_3_, ...), custom_call_target="tpu_custom_call" | custom-call | flops 32212254720 | bytes 15728640 | tf_op jit(solution)/shard_map/attend_back/pallas_call | solution.py:182
  380.8 38.1 %attend_back.5 = (f32[1024,768]{1,0:T(8,128)}, bf16[2,768,1024]{2,1,0:T(8,128)(2,1)}) custom-call(bf16[1024,768]{1,0:T(8,128)(2,1)} %add_convert_fusion.4.q_ref.refs_0_, bf16[1024,768]{1,0:T(8,128)(2,1)} %get-tuple-element.40.refs_1_, bf16[6,1024,128]{2,1,0:T(8,128)(2,1)} %get-tuple-element.41.refs_2_, bf16[6,1024,128]{2,1,0:T(8,128)(2,1)} %get-tuple-element.42.refs_3_, ...), custom_call_target="tpu_custom_call" | custom-call | flops 32212254720 | bytes 15728640 | tf_op jit(solution)/shard_map/attend_back/pallas_call | solution.py:182
  418.9 4.4 convolution_convert_fusion.1
  425.1 4.6 fusion.19
  429.7 8.3 %fusion.23 = f32[768,1536]{1,0:T(8,128)S(1)} fusion(bf16[2048,768]{1,0:T(8,128)(2,1)} %collective-permute-done.6, bf16[1536,2048]{1,0:T(8,128)(2,1)} %bitcast.57), kind=kOutput, calls=%fused_computation.104 | convolution fusion | flops 4831838208 | bytes 14155776 | tf_op jit(solution)/shard_map/dot_general | solution.py:37
  438.1 2.9 add_convert_fusion.1
  443.2 9.9 %convolution_convert_fusion = bf16[2048,768]{1,0:T(8,128)(2,1)} fusion(bf16[1536,2048]{1,0:T(8,128)(2,1)} %bitcast.58, bf16[768,2304]{1,0:T(8,128)(2,1)} %all-gather.6.cloned.1.call-done), kind=kOutput, calls=%fused_computation.4 | convolution fusion | flops 4833411072 | bytes 11796480 | tf_op jit(solution)/shard_map/dot_general | solution.py:37
  458.9 2.4 convert_reduce_fusion
  461.5 7.0 %add_convert_fusion.3 = bf16[1024,768]{1,0:T(8,128)(2,1)} fusion(bf16[2048,768]{1,0:T(8,128)(2,1)} %collective-permute-done.9, bf16[1536,1024]{1,0:T(8,128)(2,1)} %bitcast.61, bf16[768,2304]{1,0:T(8,128)(2,1)} %all-gather.6.cloned.1.call-done), kind=kOutput, calls=%fused_computation.10 | convolution fusion | flops 2418278400 | bytes 8650752 | tf_op jit(solution)/shard_map/dot_general | solution.py:37
  469.8 65.4 %psum.7 = f32[9240]{0:T(1024)S(1)} all-reduce(f32[9240]{0:T(1024)S(1)} %constant_dynamic-update-slice_fusion.7), channel_id=1, replica_groups=mesh['dp'=4,'ctx'=8] {'dp','ctx'}, use_global_device_ids=true, to_apply=%region_7.8 | all-reduce | flops 9240 | bytes 73920 | tf_op jit(solution)/shard_map/psum | solution.py:652
  536.8 2.9 fusion.11
  539.8 2.7 fusion.6
  544.5 3.1 add_convert_fusion.2
  549.5 43.6 %collective-permute-done.8 = bf16[512,768]{1,0:T(8,128)(2,1)S(1)} collective-permute-done((bf16[512,768]{1,0:T(8,128)(2,1)S(1)}, bf16[512,768]{1,0:T(8,128)(2,1)S(1)}, u32[]{:S(2)}, u32[]{:S(2)}) %collective-permute-start.8) | collective-permute-done | bytes 786464 | tf_op jit(solution)/shard_map/ppermute | solution.py:486
  594.6 47.2 %all_gather.22 = bf16[192,2304]{1,0:T(8,128)(2,1)S(1)} all-gather(bf16[24,2304]{1,0:T(8,128)(2,1)} %reduce-scatter.3.cloned.1.call-done), channel_id=1, replica_groups=mesh['dp'=4,'ctx'=8] {'ctx'}, dimensions={0}, use_global_device_ids=true | all-gather | bytes 995328 | tf_op jit(solution)/shard_map/all_gather | solution.py:592
  644.5 2.4 fusion.20
  (185 shorter events, 46.0 us)
Async XLA Ops:
  7.2 13.5 %copy-start = (s32[2,8]{1,0:T(2,128)S(1)}, s32[2,8]{1,0:T(2,128)}, u32[]{:S(2)}) copy-start(s32[2,8]{1,0:T(2,128)} %param.20) | copy-start | bytes 196
  7.2 10.5 %copy-start.13 = (bf16[2,512,768]{2,1,0:T(8,128)(2,1)S(1)}, bf16[2,512,768]{2,1,0:T(8,128)(2,1)}, u32[]{:S(2)}) copy-start(bf16[2,512,768]{2,1,0:T(8,128)(2,1)} %param.17) | copy-start | bytes 4718596
  7.3 79.5 %all-gather.6.cloned.1.call-start = ((), (), s32[]{:S(2)}) async-start(), calls=%async_computation.2 | async-start | bytes 4423680 | tf_op jit(solution)/shard_map/all_gather | solution.py:495
  8.0 171.4 %all-gather.8.cloned.1.call-start = ((), (), s32[]{:S(2)}) async-start(), calls=%async_computation.3 | async-start | bytes 1474560 | tf_op jit(solution)/shard_map/all_gather | solution.py:495
  8.8 11.3 %copy-start.31 = (s32[2]{0:T(128)S(1)}, s32[2]{0:T(128)}, u32[]{:S(2)}) copy-start(s32[2]{0:T(128)} %param.19) | copy-start | bytes 28
  8.8 170.7 %all-gather.10.cloned.1.call-start = ((), (), s32[]{:S(2)}) async-start(), calls=%async_computation.4 | async-start | bytes 5898240 | tf_op jit(solution)/shard_map/all_gather | solution.py:495
  9.5 197.2 %all-gather.12.cloned.1.call-start = ((), (), s32[]{:S(2)}) async-start(), calls=%async_computation.5 | async-start | bytes 5898240 | tf_op jit(solution)/shard_map/all_gather | solution.py:495
  11.7 37.5 %collective-permute-start = (bf16[512,768]{1,0:T(8,128)(2,1)}, bf16[512,768]{1,0:T(8,128)(2,1)S(1)}, u32[]{:S(2)}, u32[]{:S(2)}) collective-permute-start(bf16[512,768]{1,0:T(8,128)(2,1)} %dynamic-slice_bitcast_fusion.2), channel_id=1, source_target_pairs={{0,4},{1,5},{2,6},{3,7},{4,0},{5,1},{6,2},{7,3},{8,12},{9,13},{10,... | collective-permute-start | bytes 2359304 | tf_op jit(solution)/shard_map/ppermute | solution.py:486
  15.0 60.9 %collective-permute-start.1 = (bf16[1,2304]{1,0:T(2,128)(2,1)S(1)}, bf16[1,2304]{1,0:T(2,128)(2,1)S(1)}, u32[]{:S(2)}, u32[]{:S(2)}) collective-permute-start(bf16[1,2304]{1,0:T(2,128)(2,1)S(1)} %broadcast_in_dim.114), channel_id=1, source_target_pairs={{0,24},{8,16},{16,8},{24,0},{1,25},{9,17},{17,9},{25,1},{2,26},{10... | collective-permute-start | bytes 13832 | tf_op jit(solution)/shard_map/ppermute | solution.py:540
  17.2 58.6 %collective-permute-start.2 = (bf16[1,2304]{1,0:T(2,128)(2,1)S(1)}, bf16[1,2304]{1,0:T(2,128)(2,1)S(1)}, u32[]{:S(2)}, u32[]{:S(2)}) collective-permute-start(bf16[1,2304]{1,0:T(2,128)(2,1)S(1)} %broadcast_in_dim.114), channel_id=1, source_target_pairs={{0,16},{8,24},{16,0},{24,8},{1,17},{9,25},{17,1},{25,9},{2,18},{10... | collective-permute-start | bytes 13832 | tf_op jit(solution)/shard_map/ppermute | solution.py:540
  17.4 58.4 %collective-permute-start.3 = (bf16[1,2304]{1,0:T(2,128)(2,1)S(1)}, bf16[1,2304]{1,0:T(2,128)(2,1)S(1)}, u32[]{:S(2)}, u32[]{:S(2)}) collective-permute-start(bf16[1,2304]{1,0:T(2,128)(2,1)S(1)} %broadcast_in_dim.114), channel_id=1, source_target_pairs={{0,8},{8,0},{16,24},{24,16},{1,9},{9,1},{17,25},{25,17},{2,10},{10... | collective-permute-start | bytes 13832 | tf_op jit(solution)/shard_map/ppermute | solution.py:540
  18.7 68.1 %copy-start.6 = (bf16[512,768]{1,0:T(8,128)(2,1)}, bf16[512,768]{1,0:T(8,128)(2,1)S(1)}, u32[]{:S(2)}) copy-start(bf16[512,768]{1,0:T(8,128)(2,1)S(1)} %get-tuple-element.63) | copy-start | bytes 2359300
  18.7 33.2 %collective-permute-start.4 = (bf16[512,768]{1,0:T(8,128)(2,1)S(1)}, bf16[512,768]{1,0:T(8,128)(2,1)S(1)}, u32[]{:S(2)}, u32[]{:S(2)}) collective-permute-start(bf16[512,768]{1,0:T(8,128)(2,1)S(1)} %get-tuple-element.63), channel_id=1, source_target_pairs={{0,2},{1,3},{2,0},{3,1},{4,6},{5,7},{6,4},{7,5},{8,10},{9,11},{10,... | collective-permute-start | bytes 2359304 | tf_op jit(solution)/shard_map/ppermute | solution.py:486
  20.0 441.4 %reduce-scatter.5.cloned.1.call-start = ((), (), s32[]{:S(2)}) async-start(), calls=%async_computation.7 | async-start | bytes 10948608 | tf_op jit(solution)/shard_map/reduce_scatter | solution.py:589
  49.2 37.7 %copy-start.4 = (bf16[512,768]{1,0:T(8,128)(2,1)}, bf16[512,768]{1,0:T(8,128)(2,1)S(1)}, u32[]{:S(2)}) copy-start(bf16[512,768]{1,0:T(8,128)(2,1)S(1)} %collective-permute-done) | copy-start | bytes 2359300
  49.2 19.6 %collective-permute-start.5 = (bf16[512,768]{1,0:T(8,128)(2,1)S(1)}, bf16[512,768]{1,0:T(8,128)(2,1)S(1)}, u32[]{:S(2)}, u32[]{:S(2)}) collective-permute-start(bf16[512,768]{1,0:T(8,128)(2,1)S(1)} %collective-permute-done), channel_id=1, source_target_pairs={{0,2},{1,3},{2,0},{3,1},{4,6},{5,7},{6,4},{7,5},{8,10},{9,11},{10,... | collective-permute-start | bytes 2359304 | tf_op jit(solution)/shard_map/ppermute | solution.py:486
  51.9 27.0 %copy-start.9 = (bf16[512,768]{1,0:T(8,128)(2,1)}, bf16[512,768]{1,0:T(8,128)(2,1)S(1)}, u32[]{:S(2)}) copy-start(bf16[512,768]{1,0:T(8,128)(2,1)S(1)} %collective-permute-done.4) | copy-start | bytes 2359300
  68.8 12.4 %copy-start.11 = (bf16[512,768]{1,0:T(8,128)(2,1)}, bf16[512,768]{1,0:T(8,128)(2,1)S(1)}, u32[]{:S(2)}) copy-start(bf16[512,768]{1,0:T(8,128)(2,1)S(1)} %collective-permute-done.5) | copy-start | bytes 2359300
  70.8 11.3 %collective-permute-start.6 = (bf16[2048,768]{1,0:T(8,128)(2,1)}, bf16[2048,768]{1,0:T(8,128)(2,1)}, u32[]{:S(2)}, u32[]{:S(2)}) collective-permute-start(bf16[2048,768]{1,0:T(8,128)(2,1)} %pad_maximum_fusion.1), channel_id=1, source_target_pairs={{0,1},{1,0},{2,3},{3,2},{4,5},{5,4},{6,7},{7,6},{8,9},{9,8},{10,11... | collective-permute-start | bytes 9437192 | tf_op jit(solution)/shard_map/ppermute | solution.py:486
  86.0 91.1 %collective-permute-start.7 = (bf16[512,768]{1,0:T(8,128)(2,1)S(1)}, bf16[512,768]{1,0:T(8,128)(2,1)}, u32[]{:S(2)}, u32[]{:S(2)}) collective-permute-start(bf16[512,768]{1,0:T(8,128)(2,1)S(1)} %get-tuple-element.74), channel_id=1, source_target_pairs={{0,4},{1,5},{2,6},{3,7},{4,0},{5,1},{6,2},{7,3},{8,12},{9,13},{10,... | collective-permute-start | bytes 2359304 | tf_op jit(solution)/shard_map/ppermute | solution.py:486
  269.1 325.5 %reduce-scatter.3.cloned.1.call-start = ((), (), s32[]{:S(2)}) async-start(), calls=%async_computation.6 | async-start | bytes 3649536 | tf_op jit(solution)/shard_map/reduce_scatter | solution.py:589
  380.8 38.1 %copy-start.5 = (bf16[512,768]{1,0:T(8,128)(2,1)S(1)}, bf16[512,768]{1,0:T(8,128)(2,1)}, u32[]{:S(2)}) copy-start(bf16[512,768]{1,0:T(8,128)(2,1)} %copy-done.4) | copy-start | bytes 2359300
  380.8 38.1 %copy-start.7 = (bf16[512,768]{1,0:T(8,128)(2,1)S(1)}, bf16[512,768]{1,0:T(8,128)(2,1)}, u32[]{:S(2)}) copy-start(bf16[512,768]{1,0:T(8,128)(2,1)} %copy-done.6) | copy-start | bytes 2359300
  443.1 10.7 %copy-start.32 = (s32[2]{0:T(128)S(1)}, s32[2]{0:T(128)}, u32[]{:S(2)}) copy-start(s32[2]{0:T(128)} %param.19) | copy-start | bytes 28
  443.1 11.6 %copy-start.21 = (f32[16,768]{1,0:T(8,128)S(1)}, f32[16,768]{1,0:T(8,128)}, u32[]{:S(2)}) copy-start(f32[16,768]{1,0:T(8,128)} %get-tuple-element.49) | copy-start | bytes 147460
  443.1 11.9 %copy-start.2 = (f32[1024,768]{1,0:T(8,128)S(1)}, f32[1024,768]{1,0:T(8,128)}, u32[]{:S(2)}) copy-start(f32[1024,768]{1,0:T(8,128)} %get-tuple-element.45) | copy-start | bytes 9437188
  443.1 201.3 %all-gather.14.cloned.1.call-start = ((), (), s32[]{:S(2)}) async-start(), calls=%async_computation.8 | async-start | bytes 2985984 | tf_op jit(solution)/shard_map/all_gather | solution.py:592
  453.1 8.5 %collective-permute-start.9 = (bf16[2048,768]{1,0:T(8,128)(2,1)}, bf16[2048,768]{1,0:T(8,128)(2,1)}, u32[]{:S(2)}, u32[]{:S(2)}) collective-permute-start(bf16[2048,768]{1,0:T(8,128)(2,1)} %convolution_convert_fusion), channel_id=1, source_target_pairs={{0,1},{1,0},{2,3},{3,2},{4,5},{5,4},{6,7},{7,6},{8,9},{9,8},{10,11... | collective-permute-start | bytes 9437192 | tf_op jit(solution)/shard_map/ppermute | solution.py:486
  468.5 75.9 %collective-permute-start.10 = (bf16[1024,768]{1,0:T(8,128)(2,1)}, bf16[1024,768]{1,0:T(8,128)(2,1)}, u32[]{:S(2)}, u32[]{:S(2)}) collective-permute-start(bf16[1024,768]{1,0:T(8,128)(2,1)} %add_convert_fusion.3), channel_id=1, source_target_pairs={{0,2},{1,3},{2,0},{3,1},{4,6},{5,7},{6,4},{7,5},{8,10},{9,11},{10,... | collective-permute-start | bytes 4718600 | tf_op jit(solution)/shard_map/ppermute | solution.py:486
  536.5 56.7 %collective-permute-start.8 = (bf16[512,768]{1,0:T(8,128)(2,1)S(1)}, bf16[512,768]{1,0:T(8,128)(2,1)S(1)}, u32[]{:S(2)}, u32[]{:S(2)}) collective-permute-start(bf16[512,768]{1,0:T(8,128)(2,1)S(1)} %slice.126), channel_id=1, source_target_pairs={{0,4},{1,5},{2,6},{3,7},{4,0},{5,1},{6,2},{7,3},{8,12},{9,13},{10,... | collective-permute-start | bytes 2359304 | tf_op jit(solution)/shard_map/ppermute | solution.py:486
  544.5 48.7 %copy-start.15 = (bf16[1024,768]{1,0:T(8,128)(2,1)S(1)}, bf16[1024,768]{1,0:T(8,128)(2,1)}, u32[]{:S(2)}) copy-start(bf16[1024,768]{1,0:T(8,128)(2,1)} %get-tuple-element.38) | copy-start | bytes 4718596
  547.6 95.5 %collective-permute-start.11 = (bf16[512,768]{1,0:T(8,128)(2,1)S(1)}, bf16[512,768]{1,0:T(8,128)(2,1)S(1)}, u32[]{:S(2)}, u32[]{:S(2)}) collective-permute-start(bf16[512,768]{1,0:T(8,128)(2,1)S(1)} %slice.163), channel_id=1, source_target_pairs={{0,4},{1,5},{2,6},{3,7},{4,0},{5,1},{6,2},{7,3},{8,12},{9,13},{10,... | collective-permute-start | bytes 2359304 | tf_op jit(solution)/shard_map/ppermute | solution.py:486
  (20 other events, 121.0 us)
Sparse Core Ops, SparseCore 0:
  10.0 49.3 all-gather.5
  61.2 27.7 all-gather.7
  90.8 57.0 all-gather.9
  149.6 57.0 all-gather.11
  269.2 139.8 reduce-scatter.4
  443.2 139.0 reduce-scatter.2
  583.9 52.7 all-gather.13

commit v2 on v1

--- a/solution.py
+++ b/solution.py
@@ -452,6 +452,235 @@
     )(active, dbranch, held)
 
 
+def closing_kernel(
+    owners, ring, widths, dq_ref, x_ref, *refs
+):
+    shares = refs[: len(widths)]
+    small_ref, home_ref, out_ref, small_out_ref, home_out_ref = refs[len(widths) : len(widths) + 5]
+    (
+        xs,
+        dq,
+        dkv,
+        whole,
+        parts,
+        in_core,
+        by_owner,
+        in_owner,
+        by_piece,
+        in_piece,
+        done,
+        in_done,
+        small,
+        small_core,
+        small_owner,
+        small_piece,
+        load_sem,
+        send_sem,
+        recv_sem,
+    ) = refs[len(widths) + 5 :]
+    row, here = (lax.axis_index("dp"), lax.axis_index("ctx"))
+    core, depth = (lax.rem(here, 2), here // 2)
+    deep = ring // 2
+    count = dq.shape[0]
+    loads = [
+        pltpu.make_async_copy(dq_ref, dq, load_sem.at[0]),
+        pltpu.make_async_copy(x_ref, xs, load_sem.at[1]),
+    ]
+    first = xs.shape[0]
+    for i, width in enumerate(widths):
+        first -= width
+        loads.append(
+            pltpu.make_async_copy(
+                shares[i], dkv.at[:, :, pl.ds(first, width)], load_sem.at[2 + i]
+            )
+        )
+    for load in loads:
+        load.start()
+
+    mate = (row, here ^ 1)
+    owner_peers = [(row ^ k, here) for k in range(1, owners)]
+    depth_peers = [(row, here ^ (2 * k)) for k in range(1, deep)]
+    barrier = pltpu.get_barrier_semaphore()
+    peers = [mate] + owner_peers + depth_peers
+    for peer in peers:
+        pl.semaphore_signal(barrier, inc=1, device_id=peer, device_id_type=pl.DeviceIdType.MESH)
+
+    sent = []
+
+    def send(source, target, peer, m, slot):
+        copy = pltpu.make_async_remote_copy(
+            src_ref=source,
+            dst_ref=target,
+            send_sem=send_sem.at[m, slot],
+            recv_sem=recv_sem.at[m, slot],
+            device_id=peer,
+            device_id_type=pl.DeviceIdType.MESH,
+        )
+        copy.start()
+        sent.append(copy)
+        return copy
+
+    at_owner = 1
+    at_piece = owners
+    at_done = at_piece + deep - 1
+    at_back = at_done + deep - 1
+    tile = 256
+
+    def to_core(m):
+        def one(t, carry):
+            columns = pl.ds(pl.multiple_of(t * tile, tile), tile)
+            if m == 0:
+                whole[columns, :] = dot(xs[0:count, columns], dq[...].astype(bf16), 0, 0)
+            else:
+                whole[columns, :] = dot(xs[:, columns], dkv[m - 1], 0, 1)
+            return carry
+
+        lax.fori_loop(0, whole.shape[0] // tile, one, 0)
+        parts[m] = whole[...].reshape(parts.shape[1:]).astype(bf16)
+        return [send(parts.at[m, :, 1 - core], in_core.at[m], mate, m, 0)]
+
+    def to_owner(m):
+        mine = parts[m, :, core].astype(f32)
+        by_owner[m] = (mine + in_core[m].astype(f32)).astype(bf16)
+        return [
+            send(by_owner.at[m, row ^ k], in_owner.at[m, k - 1], owner_peers[k - 1], m, at_owner + k - 1)
+            for k in range(1, owners)
+        ]
+
+    def to_piece(m):
+        total = by_owner[m, row].astype(f32)
+        for k in range(1, owners):
+            total = total + in_owner[m, k - 1].astype(f32)
+        by_piece[m] = total.reshape(by_piece.shape[1:]).astype(bf16)
+        return [
+            send(
+                by_piece.at[m, depth ^ k],
+                in_piece.at[m, k - 1],
+                depth_peers[k - 1],
+                m,
+                at_piece + k - 1,
+            )
+            for k in range(1, deep)
+        ]
+
+    def to_done(m):
+        total = by_piece[m, depth].astype(f32)
+        for k in range(1, deep):
+            total = total + in_piece[m, k - 1].astype(f32)
+        done[m, depth] = total.astype(bf16)
+        return [
+            send(done.at[m, depth], done.at[m, depth], depth_peers[k - 1], m, at_done + k - 1)
+            for k in range(1, deep)
+        ]
+
+    def to_back(m):
+        return [send(done.at[m], in_done.at[m], mate, m, at_back)]
+
+    def finish(m):
+        size = out_ref.shape[1]
+        columns = slice(m * whole.shape[1], (m + 1) * whole.shape[1])
+        out_ref[core, :, columns] = done[m].astype(f32).reshape(size, whole.shape[1])
+        out_ref[1 - core, :, columns] = in_done[m].astype(f32).reshape(size, whole.shape[1])
+        return []
+
+    stages = [to_core, to_owner, to_piece, to_done, to_back, finish]
+    waiting = [[], [], []]
+    loads[0].wait()
+    loads[1].wait()
+    small[...] = small_ref[...]
+    small[0:1, :] = jnp.sum(dq[...].astype(bf16).astype(f32), axis=0, keepdims=True)
+    for load in loads[2:]:
+        load.wait()
+    ones = jnp.ones((8, dkv.shape[2]), bf16)
+    small[1:2, :] = dot(ones, dkv[1], 1, 1)[0:1, :]
+    pl.semaphore_wait(barrier, len(peers))
+    home = send(home_ref, home_out_ref, (row, here ^ (ring // 2)), 3, at_back)
+    small_waits = [send(small, small_core, mate, 3, 0)]
+    for step in range(len(stages) + 2):
+        for m in range(3):
+            stage = step - m
+            if 0 <= stage < len(stages):
+                for copy in waiting[m]:
+                    copy.wait_recv()
+                waiting[m] = stages[stage](m)
+        if step == 1:
+            small_waits[0].wait_recv()
+            small_owner[0] = small[...] + small_core[...]
+            small_waits = [
+                send(small_owner.at[0], small_owner.at[k], owner_peers[k - 1], 3, k)
+                for k in range(1, owners)
+            ]
+        if step == 3:
+            total = small_owner[0]
+            for k in range(1, owners):
+                small_waits[k - 1].wait_recv()
+                total = total + small_owner[k]
+            small_piece[0] = total
+            small_waits = [
+                send(small_piece.at[0], small_piece.at[k], depth_peers[k - 1], 3, at_piece + k - 1)
+                for k in range(1, deep)
+            ]
+        if step == 5:
+            total = small_piece[0]
+            for k in range(1, deep):
+                small_waits[k - 1].wait_recv()
+                total = total + small_piece[k]
+            small_out_ref[...] = total
+    home.wait_recv()
+    for copy in sent:
+        copy.wait_send()
+
+
+def closing(dq, stream, shares, small, home, owners, ring):
+    count, width = dq.shape
+    keys = stream.shape[0]
+    widths = tuple(v.shape[2] for v in shares)
+    deep = ring // 2
+    half = width // owners // 2
+    piece = half // deep
+    slots = 1 + (owners - 1) + 2 * (deep - 1) + 1
+    any_space = pl.BlockSpec(memory_space=pl.ANY)
+    in_vmem = pl.BlockSpec(memory_space=pltpu.VMEM)
+    return pl.pallas_call(
+        functools.partial(closing_kernel, owners, ring, widths),
+        in_specs=[any_space] * (2 + len(shares)) + [in_vmem, any_space],
+        out_specs=[in_vmem, in_vmem, any_space],
+        out_shape=[
+            jax.ShapeDtypeStruct((2, half, 3 * width), f32),
+            jax.ShapeDtypeStruct(small.shape, f32),
+            jax.ShapeDtypeStruct(home.shape, home.dtype),
+        ],
+        scratch_shapes=[
+            pltpu.VMEM((keys, width), bf16),
+            pltpu.VMEM((count, width), f32),
+            pltpu.VMEM((2, width, keys), bf16),
+            pltpu.VMEM((width, width), f32),
+            pltpu.VMEM((3, owners, 2, half, width), bf16),
+            pltpu.VMEM((3, owners, half, width), bf16),
+            pltpu.VMEM((3, owners, half, width), bf16),
+            pltpu.VMEM((3, owners - 1, half, width), bf16),
+            pltpu.VMEM((3, deep, piece, width), bf16),
+            pltpu.VMEM((3, deep - 1, piece, width), bf16),
+            pltpu.VMEM((3, deep, piece, width), bf16),
+            pltpu.VMEM((3, deep, piece, width), bf16),
+            pltpu.VMEM(small.shape, f32),
+            pltpu.VMEM(small.shape, f32),
+            pltpu.VMEM((owners,) + small.shape, f32),
+            pltpu.VMEM((deep,) + small.shape, f32),
+            pltpu.SemaphoreType.DMA((2 + len(shares),)),
+            pltpu.SemaphoreType.DMA((4, slots)),
+            pltpu.SemaphoreType.DMA((4, slots)),
+        ],
+        compiler_params=pltpu.CompilerParams(
+            vmem_limit_bytes=vmem_grant, collective_id=0, has_side_effects=True
+        ),
+        cost_estimate=pl.CostEstimate(
+            flops=20 * keys * width * width, bytes_accessed=100 << 20, transcendentals=0
+        ),
+        name="closing",
+    )(dq, stream, *shares, small, home)
+
+
 def shards(
     ring,
     tokens,
@@ -485,8 +714,7 @@
     def exchange(array, bit):
         return lax.ppermute(array, "ctx", [(i, i ^ bit) for i in range(ring)])
 
-    def to_home(kept, sent):
-        other = exchange(sent, half)
+    def arrange(kept, other):
         first = jnp.where(side == 0, kept, other)
         second = jnp.where(side == 0, other, kept)
         return jnp.stack([first, second])
@@ -583,7 +811,7 @@
         up_bias_all,
         head_dim,
     )
-    output = to_home(result[:block], result[block:])
+    output = arrange(result[:block], exchange(result[block:], half))
 
     def scatter(grad):
         return lax.psum_scatter(grad, ("dp", "ctx"), scatter_dimension=0, tiled=True)
@@ -614,8 +842,7 @@
     kv_weight = qkv_all[:, width:]
     total_keys = stream.shape[0]
     grad_queries = None
-    grad_kv_weight = None
-    grad_value_bias = None
+    shares = []
     arrived = []
     last = total_keys
     for bit in list(reversed(bits)) + [0]:
@@ -623,45 +850,64 @@
         grad_queries, grad_both = attend_back(
             queries, grad_mixed, stats, deltas, both, extra, head_dim, first, last - first, grad_queries
         )
+        shares.append(grad_both)
         kv_grads = grad_both.reshape(2 * width, last - first)
-        part = dot(stream[first:last], kv_grads, 0, 1)
-        grad_kv_weight = part if grad_kv_weight is None else grad_kv_weight + part
-        part = jnp.sum(grad_both[1], axis=1, dtype=f32)
-        grad_value_bias = part if grad_value_bias is None else grad_value_bias + part
         grad_stream = dot(kv_grads, kv_weight, 0, 1)
         for other in arrived:
             grad_stream = grad_stream + other[first:last].astype(f32)
         if bit:
-            arrived.append(exchange(grad_stream.astype(bf16), bit))
+            low = grad_stream.astype(bf16)
+            low, grad_queries = lax.optimization_barrier((low, grad_queries))
+            arrived.append(exchange(low, bit))
         last = first
     grad_query_low = grad_queries.astype(bf16)
     grad_rows = grad_first + dot(grad_query_low, qkv_all[:, :width], 1, 1) + grad_stream
     grad_rows_low = grad_rows.astype(bf16)
-    grad_tokens = to_home(grad_rows_low[:block], grad_rows_low[block:])
-
-    grad_query_bias = jnp.sum(grad_query_low, axis=0, dtype=f32)
-    grad_qkv_weight = jnp.concatenate([dot(rows, grad_query_low, 0, 0), grad_kv_weight], axis=1)
-    qkv_part = scatter(grad_qkv_weight.astype(bf16))
-
-    small = [grad_query_bias, grad_value_bias] + [sums[i] for i in range(6)] + [up_sum[0]]
+    grad_rows_low, grad_queries = lax.optimization_barrier((grad_rows_low, grad_queries))
+
     squares = jnp.sum(sums[6:9], axis=1)
-    square_sums = jnp.where(jnp.arange(2)[:, None] == side, squares[None, :], 0.0)
-    slots = jnp.where(
-        jnp.arange(owners)[:, None] == row, square_sums.reshape(1, -1), 0.0
-    ).reshape(-1)
-    summed = lax.psum(jnp.concatenate(small + [slots]), ("dp", "ctx"))
-    totals = []
-    start = 0
-    for v in small:
-        size = v.shape[0] // owners
-        totals.append(lax.dynamic_slice_in_dim(summed, start + row * size, size))
-        start += v.shape[0]
-    seq_squares = lax.dynamic_slice_in_dim(summed, start + row * 6, 6).reshape(2, 3)
+    lane = jnp.arange(width)
+    mine = (lane // 3) == (row * 2 + side)
+    squares = jnp.where(
+        lane % 3 == 0, squares[0], jnp.where(lane % 3 == 1, squares[1], squares[2])
+    )
+    squares = jnp.where(mine, squares, 0.0)[None, :]
+    small = jnp.concatenate(
+        [jnp.zeros((2, width), f32), sums[:6], squares, up_sum[0].reshape(-1, width)], axis=0
+    )
+    small = jnp.pad(small, ((0, -small.shape[0] % 8), (0, 0)))
+    if laid:
+        grad_qkv_weight, summed, other = closing(
+            grad_queries, stream, shares, small, grad_rows_low[block:], owners, ring
+        )
+        grad_qkv_weight = grad_qkv_weight.reshape(share, 3 * width)
+    else:
+        other = exchange(grad_rows_low[block:], half)
+        kv_parts = []
+        for which in range(2):
+            last = total_keys
+            part = 0.0
+            for v in shares:
+                part = part + dot(stream[last - v.shape[2] : last], v[which], 0, 1)
+                last = last - v.shape[2]
+            kv_parts.append(part)
+        grad_qkv_weight = jnp.concatenate([dot(rows, grad_query_low, 0, 0)] + kv_parts, axis=1)
+        grad_qkv_weight = spread(scatter(grad_qkv_weight.astype(bf16))).astype(f32)
+        grad_query_bias = jnp.sum(grad_query_low, axis=0, dtype=f32)
+        grad_value_bias = sum(jnp.sum(v[1], axis=1, dtype=f32) for v in shares)
+        small = jnp.concatenate([grad_query_bias[None], grad_value_bias[None], small[2:]], axis=0)
+        summed = lax.psum(small, ("dp", "ctx"))
+
+    grad_tokens = arrange(grad_rows_low[:block], other)
+    totals = [lax.dynamic_slice_in_dim(summed[i], row * share, share) for i in range(8)]
+    tall = inner // owners
+    up_total = lax.dynamic_slice_in_dim(summed[9:].reshape(-1), row * tall, tall)
+    seq_squares = lax.dynamic_slice_in_dim(summed[8], row * 6, 6).reshape(2, 3)
     branch_rms = jnp.sqrt(seq_squares / (lengths.astype(f32)[:, None] * width) + rms_eps)
     return (
         output,
         grad_tokens,
-        spread(qkv_part).astype(f32),
+        grad_qkv_weight,
         totals[0],
         totals[1],
         grad_out_weight,
@@ -669,7 +915,7 @@
         totals[3],
         totals[4],
         grad_up_weight,
-        totals[8],
+        up_total,
         grad_down_weight,
         totals[5],
         totals[6],

time: 665 us -> 581 us (0.87)
  blocking collectives: 113 us -> 0 us
  Pallas kernels: 283 us -> 377 us
  waiting for transfers between devices: 118 us -> 65.2 us
  matrix products: 61.7 us -> 40.3 us
  local copies, waits for them, and re-layouts: 26.2 us -> 36.8 us
    pallas_call x0 -> x1, Pallas kernels: none -> 93.7 us  [closing(): pl.pallas_call(functools.partial(closing_kernel, owners, ring, widths), i...]
    psum x1 -> x0, blocking collectives: 65.4 us -> none  [shards(): summed = lax.psum(jnp.concatenate(small + [slots]), ('dp', 'ctx'))]
    all_gather x1 -> x0, blocking collectives: 47.2 us -> none  [spread(): return lax.all_gather(part, 'ctx', axis=0, tiled=True)]
    ppermute x9 -> x8, waiting for transfers between devices: 88.6 us -> 45.5 us  [exchange(): return lax.ppermute(array, 'ctx', [(i, i ^ bit) for i in range(ring)])]
    dot_general x8 -> x4, matrix products: 42.6 us -> 20.9 us  [dot(): lax.dot_general(left, right, (((left_dim,), (right_dim,)), ((), ())), pre...]
    all_gather x4, waiting for transfers between devices: 27.2 us -> 17.6 us  [gather(): return lax.all_gather(array, 'dp', axis=0, tiled=True)]
    ppermute x9 -> x8, starting transfers between devices: 13 us -> 15.1 us  [exchange(): return lax.ppermute(array, 'ctx', [(i, i ^ bit) for i in range(ring)])]
  transfers between devices with their start and end apart: 19 -> 17, of which waited for: 4 -> 3; matrix products, arithmetic and copies ran while one was open for 16% -> 15% of each run, Pallas kernels for 34% -> 59%
where the time goes in v2:
time: 581 us; the launch traced here: 574 us
  Pallas kernels  377 us (65%)
  waiting for transfers between devices  65.2 us (11%)
  matrix products  40.3 us (7%)
  local copies, waits for them, and re-layouts  36.8 us (6%)
  other arithmetic  21 us (4%)
  starting transfers between devices  18.7 us (3%)
  between operations  14.6 us (3%)
    pallas_call x3, Pallas kernels, attend_back(): pl.pallas_call(functools.partial(attend_back_kernel, scale, head_dim, row...  150 us
    pallas_call x1, Pallas kernels, closing(): pl.pallas_call(functools.partial(closing_kernel, owners, ring, widths), i...  93.7 us
    pallas_call x1, Pallas kernels, attend(): pl.pallas_call(functools.partial(attend_kernel, scale, head_dim, step), g...  71.1 us
    ppermute x8, waiting for transfers between devices, exchange(): return lax.ppermute(array, 'ctx', [(i, i ^ bit) for i in range(ring)])  45.5 us
    pallas_call x1, Pallas kernels, middle(): pl.pallas_call(functools.partial(middle_kernel, head_dim, chunk), grid=(c...  41.3 us
    dot_general x4, matrix products, dot(): lax.dot_general(left, right, (((left_dim,), (right_dim,)), ((), ())), pre...  20.9 us
    all_gather x4, waiting for transfers between devices, gather(): return lax.all_gather(array, 'dp', axis=0, tiled=True)  17.6 us
    dot_general x1, matrix products, shards(): jnp.dot(stream, qkv_all[:, width:], preferred_element_type=f32) + kv_bias  15.5 us
  transfers between devices with their start and end apart: 17, of which 3 were waited for; matrix products, arithmetic and copies ran while one was open for 15% of the time, Pallas kernels for 59%

profile of v2, /device:TPU:1, one launch (start us, length us, event | category | flops | bytes accessed | tf_op | source)
XLA Modules:
  0.0 573.7 jit_solution(17647544870265771202)
XLA Ops:
  9.5 6.1 %concatenate.40 = bf16[2304]{0:T(1024)(128)(2,1)S(1)} concatenate(bf16[192]{0:T(256)(128)(2,1)} %param.22, bf16[192]{0:T(256)(128)(2,1)} %param.23, bf16[192]{0:T(256)(128)(2,1)} %param.25, bf16[192]{0:T(256)(128)(2,1)} %param.26, bf16[192]{0:T(256)(128)(2,1)} %param.27, bf16[192]{0:T(256)(128)(2,1)} %param.31, bf16[192]{0:T(256)(128)(2,1)} %param.32, bf16[192]{0:T(256)(128)(2,1)} %param.33, ...), dimensions={0} | concatenate | bytes 9216 | tf_op jit(solution)/shard_map/concatenate | solution.py:765
  15.6 2.1 collective-permute-start.3
  19.0 2.2 dynamic-slice_bitcast_fusion.2
  21.1 2.5 collective-permute-start
  27.0 30.6 %collective-permute-done = bf16[512,768]{1,0:T(8,128)(2,1)S(1)} collective-permute-done((bf16[512,768]{1,0:T(8,128)(2,1)}, bf16[512,768]{1,0:T(8,128)(2,1)S(1)}, u32[]{:S(2)}, u32[]{:S(2)}) %collective-permute-start) | collective-permute-done | bytes 786464 | tf_op jit(solution)/shard_map/ppermute | solution.py:715
  57.6 1.6 collective-permute-start.5
  60.7 14.9 %collective-permute-done.5 = bf16[512,768]{1,0:T(8,128)(2,1)S(1)} collective-permute-done((bf16[512,768]{1,0:T(8,128)(2,1)S(1)}, bf16[512,768]{1,0:T(8,128)(2,1)S(1)}, u32[]{:S(2)}, u32[]{:S(2)}) %collective-permute-start.5) | collective-permute-done | bytes 786464 | tf_op jit(solution)/shard_map/ppermute | solution.py:715
  75.6 1.9 pad_maximum_fusion
  77.6 2.1 collective-permute-start.6
  89.1 3.9 constant_dynamic-update-slice_fusion.x_ref
  93.1 3.1 collective-permute-start.7
  96.2 4.0 add_convert_fusion.3.q_ref.refs_0_
  100.1 15.5 %add_convert_fusion.k_ref.v_ref.refs_4_.refs_5_ = bf16[4096,1536]{1,0:T(8,128)(2,1)} fusion(bf16[4096,768]{1,0:T(8,128)(2,1)} %constant_dynamic-update-slice_fusion.x_ref, f32[1536]{0:T(1024)S(1)} %pad_reduce_fusion, bf16[768,2304]{1,0:T(8,128)(2,1)S(1)} %copy-done.8), kind=kOutput, calls=%fused_computation | convolution fusion | flops 9676259328 | bytes 21241856 | tf_op jit(solution)/shard_map/dot_general | solution.py:782
  115.6 71.1 %attend.1 = (bf16[1024,768]{1,0:T(8,128)(2,1)}, bf16[6,1024,128]{2,1,0:T(8,128)(2,1)}) custom-call(bf16[1024,768]{1,0:T(8,128)(2,1)} %add_convert_fusion.3.q_ref.refs_0_, bf16[4096,1536]{1,0:T(8,128)(2,1)} %add_convert_fusion.k_ref.v_ref.refs_4_.refs_5_, bf16[4096,1536]{1,0:T(8,128)(2,1)} %add_convert_fusion.k_ref.v_ref.refs_4_.refs_5_, ...), custom_call_target="tpu_custom_call" | custom-call | flops 51539607552 | bytes 17301504 | tf_op jit(solution)/shard_map/attend/pallas_call | solution.py:100
  186.7 2.4 pad_maximum_fusion.3.cot_ref
  189.1 17.6 %all-gather.12.cloned.1.call-done.down_ref = bf16[3072,768]{1,0:T(8,128)(2,1)} async-done(((bf16[768,768]{1,0:T(8,128)(2,1)}), bf16[3072,768]{1,0:T(8,128)(2,1)}) %all-gather.12.cloned.1.call-update) | async-done | bytes 4718608 | tf_op jit(solution)/shard_map/all_gather | solution.py:723
  206.7 41.3 %middle.1 = (bf16[1024,768]{1,0:T(8,128)(2,1)}, bf16[1024,3072]{1,0:T(8,128)(2,1)}, bf16[1024,768]{1,0:T(8,128)(2,1)}, bf16[1024,768]{1,0:T(8,128)(2,1)}, bf16[1...) custom-call(bf16[1024,768]{1,0:T(8,128)(2,1)} %get-tuple-element.45., ...), custom_call_target="tpu_custom_call" | custom-call | flops 21743271936 | bytes 36175872 | tf_op jit(solution)/shard_map/middle/pallas_call | solution.py:333
  249.2 2.2 collective-permute-start.8
  251.4 11.7 %up_grads.1.held_ref = bf16[32,216,768]{2,1,0:T(8,128)(2,1)} custom-call(bf16[1024,768]{1,0:T(8,128)(2,1)} %get-tuple-element.71.hidden_ref, bf16[1024,3072]{1,0:T(8,128)(2,1)} %get-tuple-element.72.dupper_ref, bf16[1024,768]{1,0:T(8,128)(2,1)} %get-tuple-element.45.mixed_ref, bf16[1024,768]{1,0:T(8,128)(2,1)} %get-tuple-element.73.dattn_ref), custom_call_target="tpu_custom_call" | custom-call | flops 6039797760 | bytes 19267584 | tf_op jit(solution)/shard_map/up_grads/pallas_call | solution.py:412
  263.1 9.2 %down_grads.1 = bf16[32,216,768]{2,1,0:T(8,128)(2,1)} custom-call(bf16[1024,3072]{1,0:T(8,128)(2,1)} %get-tuple-element.69.active_ref, bf16[1024,768]{1,0:T(8,128)(2,1)} %get-tuple-element.70.dbranch_ref, bf16[32,216,768]{2,1,0:T(8,128)(2,1)} %up_grads.1.held_ref), custom_call_target="tpu_custom_call", output_to_operand_aliasing={{}: (2, {})} | custom-call | flops 4831838208 | bytes 13762560 | tf_op jit(solution)/shard_map/down_grads/pallas_call | solution.py:434
  272.3 73.7 %attend_back.3 = (f32[1024,768]{1,0:T(8,128)}, bf16[2,768,2048]{2,1,0:T(8,128)(2,1)}) custom-call(bf16[1024,768]{1,0:T(8,128)(2,1)} %add_convert_fusion.3.q_ref.refs_0_, bf16[1024,768]{1,0:T(8,128)(2,1)} %get-tuple-element.49.refs_1_, bf16[6,1024,128]{2,1,0:T(8,128)(2,1)} %get-tuple-element.50.refs_2_, bf16[6,1024,128]{2,1,0:T(8,128)(2,1)} %get-tuple-element.51.refs_3_, ...), custom_call_target="tpu_custom_call" | custom-call | flops 64424509440 | bytes 22020096 | tf_op jit(solution)/shard_map/attend_back/pallas_call | solution.py:182
  346.0 9.7 %convolution_convert_fusion = bf16[2048,768]{1,0:T(8,128)(2,1)} fusion(bf16[1536,2048]{1,0:T(8,128)(2,1)} %bitcast.78, bf16[768,2304]{1,0:T(8,128)(2,1)S(1)} %copy-done.9), kind=kOutput, calls=%fused_computation.1 | convolution fusion | flops 4833411072 | bytes 11796480 | tf_op jit(solution)/shard_map/dot_general | solution.py:37
  356.6 38.0 %attend_back.4 = (f32[1024,768]{1,0:T(8,128)}, bf16[2,768,1024]{2,1,0:T(8,128)(2,1)}) custom-call(bf16[1024,768]{1,0:T(8,128)(2,1)} %add_convert_fusion.3.q_ref.refs_0_, bf16[1024,768]{1,0:T(8,128)(2,1)} %get-tuple-element.49.refs_1_, bf16[6,1024,128]{2,1,0:T(8,128)(2,1)} %get-tuple-element.50.refs_2_, bf16[6,1024,128]{2,1,0:T(8,128)(2,1)} %get-tuple-element.51.refs_3_, ...), custom_call_target="tpu_custom_call" | custom-call | flops 32212254720 | bytes 15728640 | tf_op jit(solution)/shard_map/attend_back/pallas_call | solution.py:182
  396.4 2.0 compare_select_fusion.2
  401.6 5.1 add_convert_fusion.2
  408.0 38.3 %attend_back.5 = (f32[1024,768]{1,0:T(8,128)}, bf16[2,768,1024]{2,1,0:T(8,128)(2,1)}) custom-call(bf16[1024,768]{1,0:T(8,128)(2,1)} %add_convert_fusion.3.q_ref.refs_0_, bf16[1024,768]{1,0:T(8,128)(2,1)} %get-tuple-element.49.refs_1_, bf16[6,1024,128]{2,1,0:T(8,128)(2,1)} %get-tuple-element.50.refs_2_, bf16[6,1024,128]{2,1,0:T(8,128)(2,1)} %get-tuple-element.51.refs_3_, ...), custom_call_target="tpu_custom_call" | custom-call | flops 32212254720 | bytes 15728640 | tf_op jit(solution)/shard_map/attend_back/pallas_call | solution.py:182
  446.4 3.5 fusion
  449.9 2.7 fusion.2
  452.6 2.4 add_convert_fusion.1
  455.9 93.7 %closing.1 = (f32[2,96,2304]{2,1,0:T(8,128)}, f32[16,768]{1,0:T(8,128)}, bf16[512,768]{1,0:T(8,128)(2,1)}) custom-call(f32[1024,768]{1,0:T(8,128)} %get-tuple-element.63.dq_ref, bf16[4096,768]{1,0:T(8,128)(2,1)} %constant_dynamic-update-slice_fusion.x_ref, bf16[2,768,2048]{2,1,0:T(8,128)(2,1)} %get-tuple-element.52.refs_0_, ...), custom_call_target="tpu_custom_call" | custom-call | flops 48318382080 | bytes 104857600 | tf_op jit(solution)/shard_map/closing/pallas_call | solution.py:644
  558.2 2.4 fusion.15
  560.6 1.7 pad_maximum_fusion.1
  (132 shorter events, 40.2 us)
Async XLA Ops:
  7.2 19.6 %copy-start = (s32[2,8]{1,0:T(2,128)S(1)}, s32[2,8]{1,0:T(2,128)}, u32[]{:S(2)}) copy-start(s32[2,8]{1,0:T(2,128)} %param.20) | copy-start | bytes 196
  7.2 16.4 %copy-start.5 = (bf16[2,512,768]{2,1,0:T(8,128)(2,1)S(1)}, bf16[2,512,768]{2,1,0:T(8,128)(2,1)}, u32[]{:S(2)}) copy-start(bf16[2,512,768]{2,1,0:T(8,128)(2,1)} %param.17) | copy-start | bytes 4718596
  7.2 88.9 %all-gather.6.cloned.1.call-start = ((), (), s32[]{:S(2)}) async-start(), calls=%async_computation.1 | async-start | bytes 4423680 | tf_op jit(solution)/shard_map/all_gather | solution.py:723
  7.9 181.2 %all-gather.8.cloned.1.call-start = ((), (), s32[]{:S(2)}) async-start(), calls=%async_computation.2 | async-start | bytes 1474560 | tf_op jit(solution)/shard_map/all_gather | solution.py:723
  8.7 17.3 %copy-start.16 = (s32[2]{0:T(128)S(1)}, s32[2]{0:T(128)}, u32[]{:S(2)}) copy-start(s32[2]{0:T(128)} %param.19) | copy-start | bytes 28
  8.7 180.4 %all-gather.10.cloned.1.call-start = ((), (), s32[]{:S(2)}) async-start(), calls=%async_computation.3 | async-start | bytes 5898240 | tf_op jit(solution)/shard_map/all_gather | solution.py:723
  9.4 197.3 %all-gather.12.cloned.1.call-start = ((), (), s32[]{:S(2)}) async-start(), calls=%async_computation.4 | async-start | bytes 5898240 | tf_op jit(solution)/shard_map/all_gather | solution.py:723
  15.6 67.2 %collective-permute-start.3 = (bf16[1,2304]{1,0:T(2,128)(2,1)S(1)}, bf16[1,2304]{1,0:T(2,128)(2,1)S(1)}, u32[]{:S(2)}, u32[]{:S(2)}) collective-permute-start(bf16[1,2304]{1,0:T(2,128)(2,1)S(1)} %broadcast_in_dim.85), channel_id=1, source_target_pairs={{0,8},{8,0},{16,24},{24,16},{1,9},{9,1},{17,25},{25,17},{2,10},{10... | collective-permute-start | bytes 13832 | tf_op jit(solution)/shard_map/ppermute | solution.py:768
  17.7 65.1 %collective-permute-start.2 = (bf16[1,2304]{1,0:T(2,128)(2,1)S(1)}, bf16[1,2304]{1,0:T(2,128)(2,1)S(1)}, u32[]{:S(2)}, u32[]{:S(2)}) collective-permute-start(bf16[1,2304]{1,0:T(2,128)(2,1)S(1)} %broadcast_in_dim.85), channel_id=1, source_target_pairs={{0,16},{8,24},{16,0},{24,8},{1,17},{9,25},{17,1},{25,9},{2,18},{10... | collective-permute-start | bytes 13832 | tf_op jit(solution)/shard_map/ppermute | solution.py:768
  18.9 63.9 %collective-permute-start.1 = (bf16[1,2304]{1,0:T(2,128)(2,1)S(1)}, bf16[1,2304]{1,0:T(2,128)(2,1)S(1)}, u32[]{:S(2)}, u32[]{:S(2)}) collective-permute-start(bf16[1,2304]{1,0:T(2,128)(2,1)S(1)} %broadcast_in_dim.85), channel_id=1, source_target_pairs={{0,24},{8,16},{16,8},{24,0},{1,25},{9,17},{17,9},{25,1},{2,26},{10... | collective-permute-start | bytes 13832 | tf_op jit(solution)/shard_map/ppermute | solution.py:768
  21.1 36.5 %collective-permute-start = (bf16[512,768]{1,0:T(8,128)(2,1)}, bf16[512,768]{1,0:T(8,128)(2,1)S(1)}, u32[]{:S(2)}, u32[]{:S(2)}) collective-permute-start(bf16[512,768]{1,0:T(8,128)(2,1)} %dynamic-slice_bitcast_fusion.2), channel_id=1, source_target_pairs={{0,4},{1,5},{2,6},{3,7},{4,0},{5,1},{6,2},{7,3},{8,12},{9,13},{10,... | collective-permute-start | bytes 2359304 | tf_op jit(solution)/shard_map/ppermute | solution.py:715
  24.6 36.1 %collective-permute-start.4 = (bf16[512,768]{1,0:T(8,128)(2,1)S(1)}, bf16[512,768]{1,0:T(8,128)(2,1)S(1)}, u32[]{:S(2)}, u32[]{:S(2)}) collective-permute-start(bf16[512,768]{1,0:T(8,128)(2,1)S(1)} %get-tuple-element.75), channel_id=1, source_target_pairs={{0,2},{1,3},{2,0},{3,1},{4,6},{5,7},{6,4},{7,5},{8,10},{9,11},{10,... | collective-permute-start | bytes 2359304 | tf_op jit(solution)/shard_map/ppermute | solution.py:715
  25.9 430.0 %reduce-scatter.2.cloned.1.call-start = ((), (), s32[]{:S(2)}) async-start(), calls=%async_computation.5 | async-start | bytes 10948608 | tf_op jit(solution)/shard_map/reduce_scatter | solution.py:817
  57.6 18.1 %collective-permute-start.5 = (bf16[512,768]{1,0:T(8,128)(2,1)S(1)}, bf16[512,768]{1,0:T(8,128)(2,1)S(1)}, u32[]{:S(2)}, u32[]{:S(2)}) collective-permute-start(bf16[512,768]{1,0:T(8,128)(2,1)S(1)} %collective-permute-done), channel_id=1, source_target_pairs={{0,2},{1,3},{2,0},{3,1},{4,6},{5,7},{6,4},{7,5},{8,10},{9,11},{10,... | collective-permute-start | bytes 2359304 | tf_op jit(solution)/shard_map/ppermute | solution.py:715
  77.6 11.5 %collective-permute-start.6 = (bf16[2048,768]{1,0:T(8,128)(2,1)}, bf16[2048,768]{1,0:T(8,128)(2,1)}, u32[]{:S(2)}, u32[]{:S(2)}) collective-permute-start(bf16[2048,768]{1,0:T(8,128)(2,1)} %pad_maximum_fusion), channel_id=1, source_target_pairs={{0,1},{1,0},{2,3},{3,2},{4,5},{5,4},{6,7},{7,6},{8,9},{9,8},{10,11... | collective-permute-start | bytes 9437192 | tf_op jit(solution)/shard_map/ppermute | solution.py:715
  84.3 3.8 copy-start.12
  89.1 3.9 copy-start.6
  93.1 93.7 %collective-permute-start.7 = (bf16[512,768]{1,0:T(8,128)(2,1)S(1)}, bf16[512,768]{1,0:T(8,128)(2,1)}, u32[]{:S(2)}, u32[]{:S(2)}) collective-permute-start(bf16[512,768]{1,0:T(8,128)(2,1)S(1)} %get-tuple-element.86), channel_id=1, source_target_pairs={{0,4},{1,5},{2,6},{3,7},{4,0},{5,1},{6,2},{7,3},{8,12},{9,13},{10,... | collective-permute-start | bytes 2359304 | tf_op jit(solution)/shard_map/ppermute | solution.py:715
  96.2 4.0 copy-start.8
  249.2 149.8 %collective-permute-start.8 = (bf16[512,768]{1,0:T(8,128)(2,1)S(1)}, bf16[512,768]{1,0:T(8,128)(2,1)S(1)}, u32[]{:S(2)}, u32[]{:S(2)}) collective-permute-start(bf16[512,768]{1,0:T(8,128)(2,1)S(1)} %slice.138), channel_id=1, source_target_pairs={{0,4},{1,5},{2,6},{3,7},{4,0},{5,1},{6,2},{7,3},{8,12},{9,13},{10,... | collective-permute-start | bytes 2359304 | tf_op jit(solution)/shard_map/ppermute | solution.py:715
  272.3 285.9 %all-gather.14.cloned.1.call-start = ((), (), s32[]{:S(2)}) async-start(), calls=%async_computation.6 | async-start | bytes 2985984 | tf_op jit(solution)/shard_map/all_gather | solution.py:820
  272.3 73.7 %copy-start.9 = (bf16[768,2304]{1,0:T(8,128)(2,1)S(1)}, bf16[768,2304]{1,0:T(8,128)(2,1)}, u32[]{:S(2)}) copy-start(bf16[768,2304]{1,0:T(8,128)(2,1)} %all-gather.6.cloned.1.call-done) | copy-start | bytes 10616836
  355.7 39.0 %copy-start.14 = (f32[16,768]{1,0:T(8,128)S(1)}, f32[16,768]{1,0:T(8,128)}, u32[]{:S(2)}) copy-start(f32[16,768]{1,0:T(8,128)} %get-tuple-element.64) | copy-start | bytes 147460
  355.7 42.6 %copy-start.13 = (f32[2,768]{1,0:T(2,128)S(1)}, f32[2,768]{1,0:T(2,128)}, u32[]{:S(2)}) copy-start(f32[2,768]{1,0:T(2,128)} %copy-done.12) | copy-start | bytes 18436
  355.7 43.3 %copy-start.7 = (bf16[1024,768]{1,0:T(8,128)(2,1)S(1)}, bf16[1024,768]{1,0:T(8,128)(2,1)}, u32[]{:S(2)}) copy-start(bf16[1024,768]{1,0:T(8,128)(2,1)} %get-tuple-element.47) | copy-start | bytes 4718596
  355.7 44.7 %collective-permute-start.9 = (bf16[2048,768]{1,0:T(8,128)(2,1)}, bf16[2048,768]{1,0:T(8,128)(2,1)}, u32[]{:S(2)}, u32[]{:S(2)}) collective-permute-start(bf16[2048,768]{1,0:T(8,128)(2,1)} %convolution_convert_fusion), channel_id=1, source_target_pairs={{0,1},{1,0},{2,3},{3,2},{4,5},{5,4},{6,7},{7,6},{8,9},{9,8},{10,11... | collective-permute-start | bytes 9437192 | tf_op jit(solution)/shard_map/ppermute | solution.py:715
  406.6 39.7 %copy-start.11 = (bf16[768,2304]{1,0:T(8,128)(2,1)S(1)}, bf16[768,2304]{1,0:T(8,128)(2,1)}, u32[]{:S(2)}) copy-start(bf16[768,2304]{1,0:T(8,128)(2,1)} %all-gather.6.cloned.1.call-done) | copy-start | bytes 10616836
  406.6 45.9 %collective-permute-start.10 = (bf16[1024,768]{1,0:T(8,128)(2,1)S(1)}, bf16[1024,768]{1,0:T(8,128)(2,1)S(1)}, u32[]{:S(2)}, u32[]{:S(2)}) collective-permute-start(bf16[1024,768]{1,0:T(8,128)(2,1)S(1)} %add_convert_fusion.2), channel_id=1, source_target_pairs={{0,2},{1,3},{2,0},{3,1},{4,6},{5,7},{6,4},{7,5},{8,10},{9,11},{10,... | collective-permute-start | bytes 4718600 | tf_op jit(solution)/shard_map/ppermute | solution.py:715
  446.4 3.5 copy-start.17
  449.9 2.7 copy-start.3
  560.6 2.6 copy-start.2
  560.6 6.0 %copy-start.1 = (s32[2,8]{1,0:T(2,128)S(1)}, s32[2,8]{1,0:T(2,128)}, u32[]{:S(2)}) copy-start(s32[2,8]{1,0:T(2,128)} %param.20) | copy-start | bytes 196
  (3 other events, 7.3 us)
Sparse Core Ops, SparseCore 0:
  9.9 49.4 all-gather.5
  61.2 27.7 all-gather.7
  90.8 57.0 all-gather.9
  149.6 57.0 all-gather.11
  272.4 138.5 reduce-scatter.1
  456.0 59.3 all-gather.13

commit v3 on v2

--- a/solution.py
+++ b/solution.py
@@ -215,6 +215,186 @@
     bias = jnp.where(live, 0.0, masked_bias)[:, None]
     ones = jnp.where((lane >= 1) & (lane <= 3), 1.0, 0.0)[None, :]
     return jnp.where(lane[None, :] == 0, bias, ones).astype(bf16)
+
+
+def opening_kernel(
+    owners,
+    ring,
+    pieces,
+    own_ref,
+    other_ref,
+    weight_ref,
+    packed_ref,
+    x_ref,
+    w_ref,
+    vec_ref,
+    q_ref,
+    kv_ref,
+    xs,
+    ws,
+    vec,
+    qs,
+    kvs,
+    load_sem,
+    store_sem,
+    send_sem,
+    recv_sem,
+):
+    row, here = (lax.axis_index("dp"), lax.axis_index("ctx"))
+    core = lax.rem(here, 2)
+    block, width = own_ref.shape
+    share = weight_ref.shape[0]
+    half = share // 2
+    mate, deep, far = ((row, here ^ 1), (row, here ^ 2), (row, here ^ (ring // 2)))
+    owner_peers = [(row ^ k, here) for k in range(1, owners)]
+    peers = [mate, deep, far] + owner_peers
+    barrier = pltpu.get_barrier_semaphore()
+    for peer in peers:
+        pl.semaphore_signal(barrier, inc=1, device_id=peer, device_id_type=pl.DeviceIdType.MESH)
+    own_load = pltpu.make_async_copy(own_ref, xs.at[0], load_sem.at[0])
+    weight_load = pltpu.make_async_copy(weight_ref, ws.at[row], load_sem.at[1])
+    vec_load = pltpu.make_async_copy(packed_ref, vec.at[row], load_sem.at[2])
+    for load in (own_load, weight_load, vec_load):
+        load.start()
+    sent, stored = ([], [])
+    count = [0]
+
+    def send(source, target, peer):
+        slot = count[0]
+        count[0] += 1
+        copy = pltpu.make_async_remote_copy(
+            src_ref=source,
+            dst_ref=target,
+            send_sem=send_sem.at[slot],
+            recv_sem=recv_sem.at[slot],
+            device_id=peer,
+            device_id_type=pl.DeviceIdType.MESH,
+        )
+        copy.start()
+        sent.append(copy)
+        return copy
+
+    def store(source, target):
+        copy = pltpu.make_async_copy(source, target, store_sem.at[len(stored)])
+        copy.start()
+        stored.append(copy)
+
+    step = block // pieces
+    parts = [pl.ds(j * step, step) for j in range(pieces)]
+    pl.semaphore_wait(barrier, len(peers))
+    weights = [
+        send(weight_ref.at[pl.ds(core * half, half)], ws.at[row, pl.ds(core * half, half)], peer)
+        for peer in owner_peers
+    ]
+    moved = [send(other_ref.at[part], xs.at[1, part], far) for part in parts]
+    own_deep = send(own_ref, xs.at[2], deep)
+    own_mate = send(own_ref, xs.at[4], mate)
+    vectors = [send(packed_ref, vec.at[row], peer) for peer in owner_peers]
+
+    moved_deep, moved_mate = ([], [])
+    weights_mate = []
+    for j, part in enumerate(parts):
+        moved[j].wait_recv()
+        moved_deep.append(send(xs.at[1, part], xs.at[3, part], deep))
+        moved_mate.append(send(xs.at[1, part], xs.at[5, part], mate))
+        if j == pieces // 2:
+            for k in range(1, owners):
+                weights[k - 1].wait_recv()
+                held = ws.at[row ^ k, pl.ds(core * half, half)]
+                weights_mate.append(send(held, held, mate))
+    own_deep.wait_recv()
+    deep_mate = send(xs.at[2], xs.at[6], mate)
+    for load in (own_load, weight_load, vec_load):
+        load.wait()
+    for copy in vectors + weights_mate:
+        copy.wait_recv()
+    for d in range(owners):
+        store(ws.at[d], w_ref.at[d])
+    store(vec, vec_ref)
+
+    def bias(which):
+        return jnp.concatenate(
+            [vec[d, :, which * share : (which + 1) * share] for d in range(owners)], axis=1
+        ).astype(f32)
+
+    value_bias = bias(1)
+    none = jnp.zeros_like(value_bias)
+
+    def product(place, first, last):
+        total = None
+        for d in range(owners):
+            left = xs[place, :, d * share : (d + 1) * share]
+            part = dot(left, ws[d, :, first:last], 1, 0)
+            total = part if total is None else total + part
+        return total
+
+    def project(place):
+        store(xs.at[place], x_ref.at[place])
+        if place < 2:
+            qs[place] = (product(place, 0, width) + bias(0)).astype(bf16)
+            store(qs.at[place], q_ref.at[place])
+        kvs[place, :, :width] = product(place, width, 2 * width).astype(bf16)
+        kvs[place, :, width:] = (product(place, 2 * width, 3 * width) + value_bias).astype(bf16)
+        store(kvs.at[place], kv_ref.at[place])
+
+    project(0)
+    own_mate.wait_recv()
+    project(4)
+    project(1)
+    for copy in moved_mate:
+        copy.wait_recv()
+    project(5)
+    project(2)
+    deep_mate.wait_recv()
+    project(6)
+    far_mate = []
+    for j, part in enumerate(parts):
+        moved_deep[j].wait_recv()
+        far_mate.append(send(xs.at[3, part], xs.at[7, part], mate))
+    project(3)
+    for copy in far_mate:
+        copy.wait_recv()
+    project(7)
+    for copy in sent:
+        copy.wait_send()
+    for copy in stored:
+        copy.wait()
+
+
+def opening(own, other, weight, packed, owners, ring):
+    block, width = own.shape
+    share = weight.shape[0]
+    blocks = ring
+    pieces = 4
+    any_space = pl.BlockSpec(memory_space=pl.ANY)
+    copies = 2 * (owners - 1) + 3 * pieces + 3 + (owners - 1) + pieces
+    shapes = [
+        jax.ShapeDtypeStruct((blocks, block, width), bf16),
+        jax.ShapeDtypeStruct((owners,) + weight.shape, bf16),
+        jax.ShapeDtypeStruct((owners,) + packed.shape, bf16),
+        jax.ShapeDtypeStruct((2, block, width), bf16),
+        jax.ShapeDtypeStruct((blocks, block, 2 * width), bf16),
+    ]
+    return pl.pallas_call(
+        functools.partial(opening_kernel, owners, ring, pieces),
+        in_specs=[any_space] * 4,
+        out_specs=[any_space] * 5,
+        out_shape=shapes,
+        scratch_shapes=[pltpu.VMEM(v.shape, v.dtype) for v in shapes]
+        + [
+            pltpu.SemaphoreType.DMA((3,)),
+            pltpu.SemaphoreType.DMA((owners + 1 + 2 * blocks + 2,)),
+            pltpu.SemaphoreType.DMA((copies,)),
+            pltpu.SemaphoreType.DMA((copies,)),
+        ],
+        compiler_params=pltpu.CompilerParams(
+            vmem_limit_bytes=vmem_grant, collective_id=1, has_side_effects=True
+        ),
+        cost_estimate=pl.CostEstimate(
+            flops=8 * blocks * block * width * width, bytes_accessed=200 << 20, transcendentals=0
+        ),
+        name="opening",
+    )(own, other, weight, packed)
 
 
 def middle_kernel(
@@ -452,11 +632,9 @@
     )(active, dbranch, held)
 
 
-def closing_kernel(
-    owners, ring, widths, dq_ref, x_ref, *refs
-):
-    shares = refs[: len(widths)]
-    small_ref, home_ref, out_ref, small_out_ref, home_out_ref = refs[len(widths) : len(widths) + 5]
+def closing_kernel(owners, ring, firsts, dq_ref, x_ref, *refs):
+    shares = refs[: len(firsts)]
+    small_ref, home_ref, out_ref, small_out_ref, home_out_ref = refs[len(firsts) : len(firsts) + 5]
     (
         xs,
         dq,
@@ -477,7 +655,7 @@
         load_sem,
         send_sem,
         recv_sem,
-    ) = refs[len(widths) + 5 :]
+    ) = refs[len(firsts) + 5 :]
     row, here = (lax.axis_index("dp"), lax.axis_index("ctx"))
     core, depth = (lax.rem(here, 2), here // 2)
     deep = ring // 2
@@ -486,14 +664,9 @@
         pltpu.make_async_copy(dq_ref, dq, load_sem.at[0]),
         pltpu.make_async_copy(x_ref, xs, load_sem.at[1]),
     ]
-    first = xs.shape[0]
-    for i, width in enumerate(widths):
-        first -= width
-        loads.append(
-            pltpu.make_async_copy(
-                shares[i], dkv.at[:, :, pl.ds(first, width)], load_sem.at[2 + i]
-            )
-        )
+    for i, first in enumerate(firsts):
+        columns = pl.ds(first, shares[i].shape[2])
+        loads.append(pltpu.make_async_copy(shares[i], dkv.at[:, :, columns], load_sem.at[2 + i]))
     for load in loads:
         load.start()
 
@@ -634,7 +807,8 @@
 def closing(dq, stream, shares, small, home, owners, ring):
     count, width = dq.shape
     keys = stream.shape[0]
-    widths = tuple(v.shape[2] for v in shares)
+    firsts = tuple(first for first, _ in shares)
+    shares = [v for _, v in shares]
     deep = ring // 2
     half = width // owners // 2
     piece = half // deep
@@ -642,7 +816,7 @@
     any_space = pl.BlockSpec(memory_space=pl.ANY)
     in_vmem = pl.BlockSpec(memory_space=pltpu.VMEM)
     return pl.pallas_call(
-        functools.partial(closing_kernel, owners, ring, widths),
+        functools.partial(closing_kernel, owners, ring, firsts),
         in_specs=[any_space] * (2 + len(shares)) + [in_vmem, any_space],
         out_specs=[in_vmem, in_vmem, any_space],
         out_shape=[
@@ -722,22 +896,15 @@
     def gather(array):
         return lax.all_gather(array, "dp", axis=0, tiled=True)
 
-    qkv_all = gather(qkv_weight)
-    own = pick(tokens, side)
-    moved = exchange(pick(tokens, 1 - side), half)
+    own, other = (pick(tokens, side), pick(tokens, 1 - side))
     bits = []
     bit = half // 2
     while bit:
         bits.append(bit)
         bit //= 2
     ids = jnp.stack([here, here ^ half])
-    pieces = [own, moved, exchange(own, bits[0]), exchange(moved, bits[0])]
-    ids = jnp.concatenate([ids, ids ^ bits[0]])
-    stream = jnp.concatenate(pieces, axis=0)
-    for bit in bits[1:]:
-        stream = jnp.concatenate([stream, exchange(stream, bit)], axis=0)
+    for bit in bits:
         ids = jnp.concatenate([ids, ids ^ bit])
-    rows = stream[: 2 * block]
     count_rows = 2 * block
 
     order = pick(block_order, side)
@@ -751,6 +918,10 @@
 
     row = lax.axis_index("dp")
     owners = lax.axis_size("dp")
+    devices = owners * ring
+    inner = up_weight.shape[1]
+    share = query_bias.shape[0]
+    laid = ring == 8 and width % (8 * devices) == 0 and inner % width == 0 and block % 32 == 0
     singles = [
         query_bias,
         value_bias,
@@ -761,25 +932,32 @@
         ffn_gain,
         ffn_shift,
     ]
-    share = query_bias.shape[0]
     packed = jnp.concatenate(singles + [up_bias])[None, :]
-    held = [packed]
-    for k in range(1, owners):
-        held.append(lax.ppermute(packed, "dp", [(i, i ^ k) for i in range(owners)]))
-    vectors = []
-    for d in range(owners):
-        found = held[0]
-        for k in range(1, owners):
-            found = jnp.where((row ^ d) == k, held[k], found)
-        vectors.append(found)
-    vectors = jnp.concatenate(vectors, axis=0).astype(f32)
+    if laid:
+        stream, qkv_all, vectors, queries, both = opening(
+            own, other, qkv_weight, packed, owners, ring
+        )
+        stream = stream.reshape(-1, width)
+        qkv_all = qkv_all.reshape(width, -1)
+        vectors = vectors.reshape(owners, -1).astype(f32)
+        queries = queries.reshape(-1, width)
+        both = both.reshape(-1, 2 * width)
+    else:
+        qkv_all = gather(qkv_weight)
+        vectors = gather(packed).astype(f32)
+        stream = jnp.concatenate([own, exchange(other, half)], axis=0)
+        for bit in bits:
+            stream = jnp.concatenate([stream, exchange(stream, bit)], axis=0)
+    rows = stream[:count_rows]
     bias = [vectors[:, i * share : (i + 1) * share].reshape(1, width) for i in range(8)]
     up_bias_all = vectors[:, 8 * share :].reshape(1, -1)
-    queries = (
-        jnp.dot(rows, qkv_all[:, :width], preferred_element_type=f32) + bias[0]
-    ).astype(bf16)
-    kv_bias = jnp.concatenate([jnp.zeros_like(bias[1]), bias[1]], axis=1)
-    both = (jnp.dot(stream, qkv_all[:, width:], preferred_element_type=f32) + kv_bias).astype(bf16)
+    if not laid:
+        queries = (
+            jnp.dot(rows, qkv_all[:, :width], preferred_element_type=f32) + bias[0]
+        ).astype(bf16)
+        kv_bias = jnp.concatenate([jnp.zeros_like(bias[1]), bias[1]], axis=1)
+        both = jnp.dot(stream, qkv_all[:, width:], preferred_element_type=f32) + kv_bias
+        both = both.astype(bf16)
     out_all = gather(out_weight)
     up_all = gather(up_weight)
     down_all = gather(down_weight)
@@ -816,15 +994,49 @@
     def scatter(grad):
         return lax.psum_scatter(grad, ("dp", "ctx"), scatter_dimension=0, tiled=True)
 
-    def spread(part):
-        return lax.all_gather(part, "ctx", axis=0, tiled=True)
-
-    devices = owners * ring
-    inner = up_weight.shape[1]
-    laid = width % (8 * devices) == 0 and inner % width == 0
+    def spread(parts):
+        return jax.tree.map(lambda v: lax.all_gather(v, "ctx", axis=0, tiled=True), parts)
+
     if laid:
-        piece = middle_grads(hidden, grad_upper, mixed, grad_attn, active, grad_branch, owners, ring)
-        pieces = spread(scatter(piece)).astype(f32)
+        scattered = scatter(
+            middle_grads(hidden, grad_upper, mixed, grad_attn, active, grad_branch, owners, ring)
+        )
+    else:
+        grads = (dot(hidden, grad_upper, 0, 0), dot(active, grad_branch, 0, 0), dot(mixed, grad_attn, 0, 0))
+        scattered = tuple(scatter(grad.astype(bf16)) for grad in grads)
+    gathered = []
+
+    kv_weight = qkv_all[:, width:]
+    size = 2 * block
+    grad_queries = None
+    shares = []
+
+    def reduced(place, level):
+        nonlocal grad_queries
+        if level == len(bits):
+            first = place * size
+            if place == 0:
+                held, grad_queries = lax.optimization_barrier((scattered, grad_queries))
+                gathered.append(spread(held))
+            grad_queries, grad_both = attend_back(
+                queries, grad_mixed, stats, deltas, both, extra, head_dim, first, size, grad_queries
+            )
+            shares.append((first, grad_both))
+            return dot(grad_both.reshape(2 * width, size), kv_weight, 0, 1)
+        low = reduced(place + (1 << level), level + 1).astype(bf16)
+        low, grad_queries = lax.optimization_barrier((low, grad_queries))
+        other = exchange(low, bits[level])
+        return reduced(place, level + 1) + other.astype(f32)
+
+    grad_stream = reduced(0, 0)
+    grad_query_low = grad_queries.astype(bf16)
+    grad_rows = grad_first + dot(grad_query_low, qkv_all[:, :width], 1, 1) + grad_stream
+    grad_rows_low = grad_rows.astype(bf16)
+    grad_rows_low, grad_queries, pieces = lax.optimization_barrier(
+        (grad_rows_low, grad_queries, gathered[0])
+    )
+    if laid:
+        pieces = pieces.astype(f32)
         each, tall = (width // devices, inner // devices)
         blocks = inner // width
         cut = blocks * each
@@ -835,35 +1047,7 @@
         grad_down_weight = pieces[:, cut : cut + tall, :].reshape(-1, width)
         grad_out_weight = pieces[:, cut + tall :, :].reshape(share, width)
     else:
-        grad_up_weight = spread(scatter(dot(hidden, grad_upper, 0, 0).astype(bf16))).astype(f32)
-        grad_down_weight = spread(scatter(dot(active, grad_branch, 0, 0).astype(bf16))).astype(f32)
-        grad_out_weight = spread(scatter(dot(mixed, grad_attn, 0, 0).astype(bf16))).astype(f32)
-
-    kv_weight = qkv_all[:, width:]
-    total_keys = stream.shape[0]
-    grad_queries = None
-    shares = []
-    arrived = []
-    last = total_keys
-    for bit in list(reversed(bits)) + [0]:
-        first = last // 2 if bit else 0
-        grad_queries, grad_both = attend_back(
-            queries, grad_mixed, stats, deltas, both, extra, head_dim, first, last - first, grad_queries
-        )
-        shares.append(grad_both)
-        kv_grads = grad_both.reshape(2 * width, last - first)
-        grad_stream = dot(kv_grads, kv_weight, 0, 1)
-        for other in arrived:
-            grad_stream = grad_stream + other[first:last].astype(f32)
-        if bit:
-            low = grad_stream.astype(bf16)
-            low, grad_queries = lax.optimization_barrier((low, grad_queries))
-            arrived.append(exchange(low, bit))
-        last = first
-    grad_query_low = grad_queries.astype(bf16)
-    grad_rows = grad_first + dot(grad_query_low, qkv_all[:, :width], 1, 1) + grad_stream
-    grad_rows_low = grad_rows.astype(bf16)
-    grad_rows_low, grad_queries = lax.optimization_barrier((grad_rows_low, grad_queries))
+        grad_up_weight, grad_down_weight, grad_out_weight = (v.astype(f32) for v in pieces)
 
     squares = jnp.sum(sums[6:9], axis=1)
     lane = jnp.arange(width)
@@ -885,16 +1069,14 @@
         other = exchange(grad_rows_low[block:], half)
         kv_parts = []
         for which in range(2):
-            last = total_keys
             part = 0.0
-            for v in shares:
-                part = part + dot(stream[last - v.shape[2] : last], v[which], 0, 1)
-                last = last - v.shape[2]
+            for first, v in shares:
+                part = part + dot(stream[first : first + size], v[which], 0, 1)
             kv_parts.append(part)
         grad_qkv_weight = jnp.concatenate([dot(rows, grad_query_low, 0, 0)] + kv_parts, axis=1)
         grad_qkv_weight = spread(scatter(grad_qkv_weight.astype(bf16))).astype(f32)
         grad_query_bias = jnp.sum(grad_query_low, axis=0, dtype=f32)
-        grad_value_bias = sum(jnp.sum(v[1], axis=1, dtype=f32) for v in shares)
+        grad_value_bias = sum(jnp.sum(v[1], axis=1, dtype=f32) for _, v in shares)
         small = jnp.concatenate([grad_query_bias[None], grad_value_bias[None], small[2:]], axis=0)
         summed = lax.psum(small, ("dp", "ctx"))
 

time: 581 us -> 543 us (0.935)
  waiting for transfers between devices: 65.2 us -> 17.9 us
  Pallas kernels: 377 us -> 424 us
  matrix products: 40.3 us -> 22.9 us
  starting transfers between devices: 18.7 us -> 7.11 us
  local copies, waits for them, and re-layouts: 36.8 us -> 29.8 us
    ppermute x8 -> x5, waiting for transfers between devices: 45.5 us -> 0.01 us  [exchange(): return lax.ppermute(array, 'ctx', [(i, i ^ bit) for i in range(ring)])]
    pallas_call x1 -> x2, Pallas kernels: 93.7 us -> 139 us  [the longest x1 77 us: closing(): pl.pallas_call(functools.partial(closing_kernel, owners, ring, firsts), i...]
    dot_general x2 -> x0, matrix products: 19.5 us -> none  [the longest x1 15.5 us: shards(): jnp.dot(stream, qkv_all[:, width:], preferred_element_type=f32) + kv_bias]
    all_gather x4 -> x3, waiting for transfers between devices: 17.6 us -> 5.66 us  [gather(): return lax.all_gather(array, 'dp', axis=0, tiled=True)]
    reduce_scatter x1, waiting for transfers between devices: 0.01 us -> 10.8 us  [scatter(): lax.psum_scatter(grad, ('dp', 'ctx'), scatter_dimension=0, tiled=True)]
    ppermute x8 -> x5, starting transfers between devices: 15.1 us -> 6.92 us  [exchange(): return lax.ppermute(array, 'ctx', [(i, i ^ bit) for i in range(ring)])]
    pallas_call x3 -> x4, Pallas kernels: 150 us -> 153 us  [attend_back(): pl.pallas_call(functools.partial(attend_back_kernel, scale, head_dim, row...]
    dot_general x4 -> x5, matrix products: 20.9 us -> 22.9 us  [dot(): lax.dot_general(left, right, (((left_dim,), (right_dim,)), ((), ())), pre...]
  transfers between devices with their start and end apart: 17 -> 10, of which waited for: 3 -> 2; matrix products, arithmetic and copies ran while one was open for 15% -> 10% of each run, Pallas kernels for 59% -> 53%
where the time goes in v3:
time: 543 us; the launch traced here: 534 us
  Pallas kernels  424 us (78%)
  local copies, waits for them, and re-layouts  29.8 us (5%)
  matrix products  22.9 us (4%)
  waiting for transfers between devices  17.9 us (3%)
  other arithmetic  16.9 us (3%)
  between operations  14.6 us (3%)
  starting transfers between devices  7.11 us (1%)
    pallas_call x4, Pallas kernels, attend_back(): pl.pallas_call(functools.partial(attend_back_kernel, scale, head_dim, row...  153 us
    pallas_call x1, Pallas kernels, closing(): pl.pallas_call(functools.partial(closing_kernel, owners, ring, firsts), i...  77 us
    pallas_call x1, Pallas kernels, attend(): pl.pallas_call(functools.partial(attend_kernel, scale, head_dim, step), g...  70.6 us
    pallas_call x1, Pallas kernels, opening(): pl.pallas_call(functools.partial(opening_kernel, owners, ring, pieces), i...  61.6 us
    pallas_call x1, Pallas kernels, middle(): pl.pallas_call(functools.partial(middle_kernel, head_dim, chunk), grid=(c...  41.6 us
    dot_general x5, matrix products, dot(): lax.dot_general(left, right, (((left_dim,), (right_dim,)), ((), ())), pre...  22.9 us
    pallas_call x1, Pallas kernels, middle_grads(): pl.pallas_call(functools.partial(up_out_kernel, blocks), grid=(blocks + 1...  11.7 us
  transfers between devices with their start and end apart: 10, of which 2 were waited for; matrix products, arithmetic and copies ran while one was open for 10% of the time, Pallas kernels for 53%

profile of v3, /device:TPU:1, one launch (start us, length us, event | category | flops | bytes accessed | tf_op | source)
XLA Modules:
  0.0 533.6 jit_solution(10075715572959804692)
XLA Ops:
  8.8 6.1 %concatenate.23 = bf16[2304]{0:T(1024)(128)(2,1)S(1)} concatenate(bf16[192]{0:T(256)(128)(2,1)} %param.22, bf16[192]{0:T(256)(128)(2,1)} %param.23, bf16[192]{0:T(256)(128)(2,1)} %param.25, bf16[192]{0:T(256)(128)(2,1)} %param.26, bf16[192]{0:T(256)(128)(2,1)} %param.27, bf16[192]{0:T(256)(128)(2,1)} %param.31, bf16[192]{0:T(256)(128)(2,1)} %param.32, bf16[192]{0:T(256)(128)(2,1)} %param.33, ...), dimensions={0} | concatenate | bytes 9216 | tf_op jit(solution)/shard_map/concatenate | solution.py:935
  15.5 2.6 dynamic-slice_bitcast_fusion.2
  18.1 61.6 %opening.1 = (bf16[8,512,768]{2,1,0:T(8,128)(2,1)}, bf16[4,192,2304]{2,1,0:T(8,128)(2,1)}, bf16[4,1,2304]{2,1,0:T(2,128)(2,1)}, bf16[2,512,768]{2,1,0:T(8,128)(2,1)}, bf16[8,512,1536]{2,1,0:T(8,128)(2,1)}) custom-call(bf16[512,768]{1,0:T(8,128)(2,1)} %get-tuple-element.110.own_ref, bf16[512,768]{1,0:T(8,128)(2,1)} %get-tuple-element.109.other_ref, ...), custom_call_target="tpu_custom_call" | custom-call | flops 19327352832 | bytes 209715200 | tf_op jit(solution)/shard_map/opening/pallas_call | solution.py:378
  79.8 2.3 collective-permute-start
  84.0 1.6 select_convert_fusion.extra_ref.refs_6_
  85.5 70.6 %attend.1 = (bf16[1024,768]{1,0:T(8,128)(2,1)}, bf16[6,1024,128]{2,1,0:T(8,128)(2,1)}) custom-call(bf16[1024,768]{1,0:T(8,128)(2,1)} %bitcast.109, bf16[4096,1536]{1,0:T(8,128)(2,1)} %bitcast.95, bf16[4096,1536]{1,0:T(8,128)(2,1)} %bitcast.96, bf16[4096,128]{1,0:T(8,128)(2,1)} %select_convert_fusion.extra_ref.refs_6_), custom_call_target="tpu_custom_call" | custom-call | flops 51539607552 | bytes 17301504 | tf_op jit(solution)/shard_map/attend/pallas_call | solution.py:100
  156.9 2.7 slice.115
  162.4 1.2 pad_maximum_fusion.1.cot_ref
  163.7 5.7 %all-gather.9.cloned.1.call-done.down_ref = bf16[3072,768]{1,0:T(8,128)(2,1)} async-done(((bf16[768,768]{1,0:T(8,128)(2,1)}), bf16[3072,768]{1,0:T(8,128)(2,1)}) %all-gather.9.cloned.1.call-update) | async-done | bytes 4718608 | tf_op jit(solution)/shard_map/all_gather | solution.py:897
  169.3 41.6 %middle.1 = (bf16[1024,768]{1,0:T(8,128)(2,1)}, bf16[1024,3072]{1,0:T(8,128)(2,1)}, bf16[1024,768]{1,0:T(8,128)(2,1)}, bf16[1024,768]{1,0:T(8,128)(2,1)}, bf16[1...) custom-call(bf16[1024,768]{1,0:T(8,128)(2,1)} %get-tuple-element.59., ...), custom_call_target="tpu_custom_call" | custom-call | flops 21743271936 | bytes 36175872 | tf_op jit(solution)/shard_map/middle/pallas_call | solution.py:513
  210.9 11.7 %up_grads.1.held_ref = bf16[32,216,768]{2,1,0:T(8,128)(2,1)} custom-call(bf16[1024,768]{1,0:T(8,128)(2,1)} %get-tuple-element.70.hidden_ref, bf16[1024,3072]{1,0:T(8,128)(2,1)} %get-tuple-element.71.dupper_ref, bf16[1024,768]{1,0:T(8,128)(2,1)} %get-tuple-element.59.mixed_ref, bf16[1024,768]{1,0:T(8,128)(2,1)} %get-tuple-element.72.dattn_ref), custom_call_target="tpu_custom_call" | custom-call | flops 6039797760 | bytes 19267584 | tf_op jit(solution)/shard_map/up_grads/pallas_call | solution.py:592
  222.6 9.2 %down_grads.1 = bf16[32,216,768]{2,1,0:T(8,128)(2,1)} custom-call(bf16[1024,3072]{1,0:T(8,128)(2,1)} %get-tuple-element.68.active_ref, bf16[1024,768]{1,0:T(8,128)(2,1)} %get-tuple-element.69.dbranch_ref, bf16[32,216,768]{2,1,0:T(8,128)(2,1)} %up_grads.1.held_ref), custom_call_target="tpu_custom_call", output_to_operand_aliasing={{}: (2, {})} | custom-call | flops 4831838208 | bytes 13762560 | tf_op jit(solution)/shard_map/down_grads/pallas_call | solution.py:614
  233.3 2.2 collective-permute-start.1
  235.5 38.0 %attend_back.4 = (f32[1024,768]{1,0:T(8,128)}, bf16[2,768,1024]{2,1,0:T(8,128)(2,1)}) custom-call(bf16[1024,768]{1,0:T(8,128)(2,1)} %bitcast.110, bf16[1024,768]{1,0:T(8,128)(2,1)} %get-tuple-element.65.refs_1_, bf16[6,1024,128]{2,1,0:T(8,128)(2,1)} %get-tuple-element.66.refs_2_, bf16[6,1024,128]{2,1,0:T(8,128)(2,1)} %get-tuple-element.67.refs_3_, ...), custom_call_target="tpu_custom_call" | custom-call | flops 32212254720 | bytes 15728640 | tf_op jit(solution)/shard_map/attend_back/pallas_call | solution.py:182
  273.5 5.8 %convolution_convert_fusion.1 = bf16[1024,768]{1,0:T(8,128)(2,1)} fusion(bf16[1536,1024]{1,0:T(8,128)(2,1)} %bitcast.105, bf16[768,2304]{1,0:T(8,128)(2,1)S(1)} %bitcast.76), kind=kOutput, calls=%fused_computation.5 | convolution fusion | flops 2416705536 | bytes 7077888 | tf_op jit(solution)/shard_map/dot_general | solution.py:37
  280.3 38.0 %attend_back.5 = (f32[1024,768]{1,0:T(8,128)}, bf16[2,768,1024]{2,1,0:T(8,128)(2,1)}) custom-call(bf16[1024,768]{1,0:T(8,128)(2,1)} %bitcast.111, bf16[1024,768]{1,0:T(8,128)(2,1)} %get-tuple-element.65.refs_1_, bf16[6,1024,128]{2,1,0:T(8,128)(2,1)} %get-tuple-element.66.refs_2_, bf16[6,1024,128]{2,1,0:T(8,128)(2,1)} %get-tuple-element.67.refs_3_, ...), custom_call_target="tpu_custom_call" | custom-call | flops 32212254720 | bytes 15728640 | tf_op jit(solution)/shard_map/attend_back/pallas_call | solution.py:182
  320.0 2.0 compare_select_fusion.2
  322.7 1.3 pad_maximum_fusion.2
  324.0 1.3 copy-done.11
  325.3 5.0 add_convert_fusion.1
  331.5 38.3 %attend_back.6 = (f32[1024,768]{1,0:T(8,128)}, bf16[2,768,1024]{2,1,0:T(8,128)(2,1)}) custom-call(bf16[1024,768]{1,0:T(8,128)(2,1)} %bitcast.112, bf16[1024,768]{1,0:T(8,128)(2,1)} %get-tuple-element.65.refs_1_, bf16[6,1024,128]{2,1,0:T(8,128)(2,1)} %get-tuple-element.66.refs_2_, bf16[6,1024,128]{2,1,0:T(8,128)(2,1)} %get-tuple-element.67.refs_3_, ...), custom_call_target="tpu_custom_call" | custom-call | flops 32212254720 | bytes 15728640 | tf_op jit(solution)/shard_map/attend_back/pallas_call | solution.py:182
  369.8 5.9 %convolution_convert_fusion = bf16[1024,768]{1,0:T(8,128)(2,1)} fusion(bf16[1536,1024]{1,0:T(8,128)(2,1)} %bitcast.107, bf16[768,2304]{1,0:T(8,128)(2,1)S(1)} %bitcast.78), kind=kOutput, calls=%fused_computation.4 | convolution fusion | flops 2416705536 | bytes 7077888 | tf_op jit(solution)/shard_map/dot_general | solution.py:37
  376.1 10.8 %reduce-scatter.2.cloned.1.call-done = bf16[1,216,768]{2,1,0:T(8,128)(2,1)} async-done(((bf16[32,216,768]{2,1,0:T(8,128)(2,1)}), bf16[1,216,768]{2,1,0:T(8,128)(2,1)}) %reduce-scatter.2.cloned.1.call-update) | async-done | bytes 331792 | tf_op jit(solution)/shard_map/reduce_scatter | solution.py:995
  386.9 38.3 %attend_back.7 = (f32[1024,768]{1,0:T(8,128)}, bf16[2,768,1024]{2,1,0:T(8,128)(2,1)}) custom-call(bf16[1024,768]{1,0:T(8,128)(2,1)} %bitcast.113, bf16[1024,768]{1,0:T(8,128)(2,1)} %get-tuple-element.65.refs_1_, bf16[6,1024,128]{2,1,0:T(8,128)(2,1)} %get-tuple-element.66.refs_2_, bf16[6,1024,128]{2,1,0:T(8,128)(2,1)} %get-tuple-element.67.refs_3_, ...), custom_call_target="tpu_custom_call" | custom-call | flops 32212254720 | bytes 15728640 | tf_op jit(solution)/shard_map/attend_back/pallas_call | solution.py:182
  425.3 3.5 fusion
  428.8 2.7 fusion.2
  431.5 2.4 add_convert_fusion
  434.8 77.0 %closing.1 = (f32[2,96,2304]{2,1,0:T(8,128)}, f32[16,768]{1,0:T(8,128)}, bf16[512,768]{1,0:T(8,128)(2,1)}) custom-call(f32[1024,768]{1,0:T(8,128)} %get-tuple-element.91.dq_ref, bf16[4096,768]{1,0:T(8,128)(2,1)} %bitcast.81, bf16[2,768,1024]{2,1,0:T(8,128)(2,1)} %get-tuple-element.73.refs_0_, bf16[2,768,1024]{2,1,0:T(8,128)(2,1)} %get-tuple-element.77.refs_1_, ...), custom_call_target="tpu_custom_call" | custom-call | flops 48318382080 | bytes 104857600 | tf_op jit(solution)/shard_map/closing/pallas_call | solution.py:818
  513.6 1.6 fusion.14
  515.3 1.6 slice.168
  517.2 1.3 pad_maximum_fusion.3
  522.4 3.1 pad_maximum_fusion
  (108 shorter events, 22.1 us)
Async XLA Ops:
  7.2 75.6 %copy-start = (s32[2,8]{1,0:T(2,128)S(1)}, s32[2,8]{1,0:T(2,128)}, u32[]{:S(2)}) copy-start(s32[2,8]{1,0:T(2,128)} %param.20) | copy-start | bytes 196
  7.2 156.5 %all-gather.5.cloned.1.call-start = ((), (), s32[]{:S(2)}) async-start(), calls=%async_computation.1 | async-start | bytes 1474560 | tf_op jit(solution)/shard_map/all_gather | solution.py:897
  7.9 155.7 %all-gather.7.cloned.1.call-start = ((), (), s32[]{:S(2)}) async-start(), calls=%async_computation.2 | async-start | bytes 5898240 | tf_op jit(solution)/shard_map/all_gather | solution.py:897
  8.7 160.6 %all-gather.9.cloned.1.call-start = ((), (), s32[]{:S(2)}) async-start(), calls=%async_computation.3 | async-start | bytes 5898240 | tf_op jit(solution)/shard_map/all_gather | solution.py:897
  18.1 61.6 %copy-start.7 = (bf16[2,512,768]{2,1,0:T(8,128)(2,1)S(1)}, bf16[2,512,768]{2,1,0:T(8,128)(2,1)}, u32[]{:S(2)}) copy-start(bf16[2,512,768]{2,1,0:T(8,128)(2,1)} %param.18) | copy-start | bytes 4718596
  79.7 2.5 copy-start.16
  79.8 82.6 %collective-permute-start = (bf16[512,768]{1,0:T(8,128)(2,1)S(1)}, bf16[512,768]{1,0:T(8,128)(2,1)S(1)}, u32[]{:S(2)}, u32[]{:S(2)}) collective-permute-start(bf16[512,768]{1,0:T(8,128)(2,1)S(1)} %get-tuple-element.108), channel_id=1, source_target_pairs={{0,4},{1,5},{2,6},{3,7},{4,0},{5,1},{6,2},{7,3},{8,12},{9,13},{10,... | collective-permute-start | bytes 2359304 | tf_op jit(solution)/shard_map/ppermute | solution.py:889
  82.1 304.8 %reduce-scatter.2.cloned.1.call-start = ((), (), s32[]{:S(2)}) async-start(), calls=%async_computation.4 | async-start | bytes 10948608 | tf_op jit(solution)/shard_map/reduce_scatter | solution.py:995
  156.1 4.4 copy-start.13
  231.8 1.4 copy-start.8
  231.8 202.0 %all-gather.11.cloned.1.call-start = ((), (), s32[]{:S(2)}) async-start(), calls=%async_computation.5 | async-start | bytes 2985984 | tf_op jit(solution)/shard_map/all_gather | solution.py:998
  233.3 89.3 %collective-permute-start.1 = (bf16[512,768]{1,0:T(8,128)(2,1)S(1)}, bf16[512,768]{1,0:T(8,128)(2,1)S(1)}, u32[]{:S(2)}, u32[]{:S(2)}) collective-permute-start(bf16[512,768]{1,0:T(8,128)(2,1)S(1)} %slice.126), channel_id=1, source_target_pairs={{0,4},{1,5},{2,6},{3,7},{4,0},{5,1},{6,2},{7,3},{8,12},{9,13},{10,... | collective-permute-start | bytes 2359304 | tf_op jit(solution)/shard_map/ppermute | solution.py:889
  235.5 38.0 %copy-start.10 = (bf16[4,192,2304]{2,1,0:T(8,128)(2,1)S(1)}, bf16[4,192,2304]{2,1,0:T(8,128)(2,1)}, u32[]{:S(2)}) copy-start(bf16[4,192,2304]{2,1,0:T(8,128)(2,1)} %get-tuple-element.74) | copy-start | bytes 10616836
  279.3 40.0 %copy-start.14 = (f32[16,768]{1,0:T(8,128)S(1)}, f32[16,768]{1,0:T(8,128)}, u32[]{:S(2)}) copy-start(f32[16,768]{1,0:T(8,128)} %get-tuple-element.92) | copy-start | bytes 147460
  279.3 44.7 %collective-permute-start.2 = (bf16[1024,768]{1,0:T(8,128)(2,1)}, bf16[1024,768]{1,0:T(8,128)(2,1)}, u32[]{:S(2)}, u32[]{:S(2)}) collective-permute-start(bf16[1024,768]{1,0:T(8,128)(2,1)} %convolution_convert_fusion.1), channel_id=1, source_target_pairs={{0,1},{1,0},{2,3},{3,2},{4,5},{5,4},{6,7},{7,6},{8,9},{9,8},{10,11... | collective-permute-start | bytes 4718600 | tf_op jit(solution)/shard_map/ppermute | solution.py:889
  322.6 2.7 copy-start.11
  330.4 101.1 %collective-permute-start.4 = (bf16[1024,768]{1,0:T(8,128)(2,1)S(1)}, bf16[1024,768]{1,0:T(8,128)(2,1)S(1)}, u32[]{:S(2)}, u32[]{:S(2)}) collective-permute-start(bf16[1024,768]{1,0:T(8,128)(2,1)S(1)} %add_convert_fusion.1), channel_id=1, source_target_pairs={{0,2},{1,3},{2,0},{3,1},{4,6},{5,7},{6,4},{7,5},{8,10},{9,11},{10,... | collective-permute-start | bytes 4718600 | tf_op jit(solution)/shard_map/ppermute | solution.py:889
  375.7 55.7 %collective-permute-start.3 = (bf16[1024,768]{1,0:T(8,128)(2,1)}, bf16[1024,768]{1,0:T(8,128)(2,1)}, u32[]{:S(2)}, u32[]{:S(2)}) collective-permute-start(bf16[1024,768]{1,0:T(8,128)(2,1)} %convolution_convert_fusion), channel_id=1, source_target_pairs={{0,1},{1,0},{2,3},{3,2},{4,5},{5,4},{6,7},{7,6},{8,9},{9,8},{10,11... | collective-permute-start | bytes 4718600 | tf_op jit(solution)/shard_map/ppermute | solution.py:889
  386.9 38.4 %copy-start.12 = (bf16[4,192,2304]{2,1,0:T(8,128)(2,1)S(1)}, bf16[4,192,2304]{2,1,0:T(8,128)(2,1)}, u32[]{:S(2)}) copy-start(bf16[4,192,2304]{2,1,0:T(8,128)(2,1)} %get-tuple-element.74) | copy-start | bytes 10616836
  425.3 3.5 copy-start.17
  428.8 2.7 copy-start.3
  434.8 78.8 %copy-start.2 = (bf16[8,216,768]{2,1,0:T(8,128)(2,1)S(1)}, bf16[8,216,768]{2,1,0:T(8,128)(2,1)}, u32[]{:S(2)}) copy-start(bf16[8,216,768]{2,1,0:T(8,128)(2,1)} %all-gather.11.cloned.1.call-done) | copy-start | bytes 7962628
  515.3 1.6 copy-start.9
  517.0 4.7 copy-start.15
  517.0 5.4 %copy-start.4 = (f32[8,24,768]{2,1,0:T(8,128)S(1)}, f32[8,24,768]{2,1,0:T(8,128)}, u32[]{:S(2)}) copy-start(f32[8,24,768]{2,1,0:T(8,128)} %get-tuple-element.98) | copy-start | bytes 1769476
  517.0 5.4 %copy-start.5 = (f32[8,24,768]{2,1,0:T(8,128)S(1)}, f32[8,24,768]{2,1,0:T(8,128)}, u32[]{:S(2)}) copy-start(f32[8,24,768]{2,1,0:T(8,128)} %get-tuple-element.99) | copy-start | bytes 1769476
  522.4 3.1 copy-start.6
  522.4 4.3 copy-start.1
Sparse Core Ops, SparseCore 0:
  9.9 40.4 all-gather.4
  52.2 58.0 all-gather.6
  112.2 57.0 all-gather.8
  232.0 154.8 reduce-scatter.1
  388.4 34.6 all-gather.10

commit v4 on v3

--- a/solution.py
+++ b/solution.py
@@ -57,7 +57,9 @@
     return jnp.where(place == 0, unit, out).astype(bf16)
 
 
-def attend_kernel(scale, head_dim, step, q_ref, k_ref, v_ref, extra_ref, o_ref, stat_ref, kb, vb):
+def attend_kernel(
+    scale, head_dim, step, q_ref, k_ref, v_ref, extra_ref, o_ref, p_ref, factor_ref, kb, vb
+):
     keys = k_ref.shape[0]
 
     @pl.when(pl.program_id(1) == 0)
@@ -70,24 +72,28 @@
     queries = q_ref[...]
     lane = lax.broadcasted_iota(jnp.int32, (1, lanes), 1)
     bias_lane = jnp.where(lane % head_dim == 0, 1.0, 0.0).astype(bf16)
-    outs, logs = ([], [])
+    outs, factors = ([], [])
     for h in range(2):
         own = jnp.where(head_lanes(h, head_dim), queries, bias_lane)
         best, acc = (None, None)
+        bests = []
         for first in range(0, keys, step):
             scores = dot(own, kb[h, first : first + step, :], 1, 1)
             high = jnp.max(scores, axis=1, keepdims=True)
             new_best = high if best is None else jnp.maximum(best, high)
             weights = jnp.exp2((scores - new_best) * factor).astype(bf16)
+            p_ref[h, :, first : first + step] = weights
             part = dot(weights, vb[h, first : first + step, :], 1, 0)
             acc = part if best is None else acc * jnp.exp2((best - new_best) * factor) + part
             best = new_best
+            bests.append(best)
         free = (1 - h) * head_dim + 1
         total = acc[:, free : free + 1]
         outs.append(acc / total)
-        logs.append(best + jnp.log2(total) * (1.0 / factor))
+        factors.append([jnp.exp2((high - best) * factor) / total for high in bests])
     o_ref[...] = jnp.where(head_lanes(0, head_dim), outs[0], outs[1]).astype(bf16)
-    stat_ref[...] = spread_lanes(logs[0], logs[1], 1.0, head_dim)
+    for s in range(keys // step):
+        factor_ref[s] = jnp.where(head_lanes(0, head_dim), factors[0][s], factors[1][s])
 
 
 def attend(queries, both, extra, head_dim):
@@ -108,17 +114,19 @@
         ],
         out_specs=[
             pl.BlockSpec((row_step, lanes), lambda h, i: (i, h)),
-            pl.BlockSpec((None, row_step, lanes), lambda h, i: (h, i, 0)),
+            pl.BlockSpec((None, 2, row_step, keys), lambda h, i: (h, 0, i, 0)),
+            pl.BlockSpec((None, keys // step, row_step, lanes), lambda h, i: (h, 0, i, 0)),
         ],
         out_shape=[
             jax.ShapeDtypeStruct((rows, width), bf16),
-            jax.ShapeDtypeStruct((pairs, rows, lanes), bf16),
+            jax.ShapeDtypeStruct((pairs, 2, rows, keys), bf16),
+            jax.ShapeDtypeStruct((pairs, keys // step, rows, lanes), f32),
         ],
         scratch_shapes=[pltpu.VMEM((2, keys, lanes), bf16), pltpu.VMEM((2, keys, lanes), bf16)],
         compiler_params=pltpu.CompilerParams(vmem_limit_bytes=vmem_grant),
         cost_estimate=pl.CostEstimate(
             flops=4 * rows * keys * width * 4,
-            bytes_accessed=keys * width * 4 + rows * width * 6,
+            bytes_accessed=keys * width * 4 + rows * width * 6 + 4 * pairs * rows * keys,
             transcendentals=rows * keys * width // head_dim,
         ),
         name="attend",
@@ -126,31 +134,34 @@
 
 
 def attend_back_kernel(scale, head_dim, row_step, resumed, *refs):
-    q_ref, da_ref, qx_ref, dax_ref, k_ref, v_ref, extra_ref = refs[:7]
-    start_ref = refs[7] if resumed else None
-    dq_ref, dkv_ref = refs[-2:]
+    q_ref, da_ref, dax_ref, factor_ref, p_ref, k_ref, v_ref, extra_ref = refs[:8]
+    start_ref = refs[8] if resumed else None
+    dq_ref, dkv_ref, scaled, scaled_extra = refs[-4:]
     j = pl.program_id(1)
     rows = q_ref.shape[0]
-    factor = scale * log2_e
+
+    @pl.when(j == 0)
+    def _():
+        factors = factor_ref[...]
+        scaled[...] = (da_ref[...].astype(f32) * factors).astype(bf16)
+        turned = pltpu.roll(factors, head_dim, 1)
+        scaled_extra[...] = (dax_ref[...].astype(f32) * turned).astype(bf16)
+
     keys, values, extra = (k_ref[...], v_ref[...], extra_ref[...])
     dk, dv = (None, None)
     for first in range(0, rows, row_step):
         part = slice(first, first + row_step)
-        queries, grads = (q_ref[part, :], da_ref[part, :])
-        queries_extra, grads_extra = (qx_ref[part, :], dax_ref[part, :])
+        queries, grads, grads_extra = (q_ref[part, :], scaled[part, :], scaled_extra[part, :])
+        none = jnp.zeros_like(queries)
         dq = None
         for h in range(2):
             sel = head_lanes(h, head_dim)
-            scores = dot(
-                jnp.where(sel, queries, queries_extra), jnp.where(sel, keys, extra), 1, 1
-            )
-            weights = jnp.exp2(scores * factor)
+            weights = p_ref[h, part, :]
             grad_weights = dot(
                 jnp.where(sel, grads, grads_extra), jnp.where(sel, values, extra), 1, 1
             )
-            grad_scores = (weights * grad_weights).astype(bf16)
-            none = jnp.zeros_like(queries)
-            part_dv = dot(jnp.where(sel, grads, none), weights.astype(bf16), 0, 0)
+            grad_scores = (weights.astype(f32) * grad_weights).astype(bf16)
+            part_dv = dot(jnp.where(sel, grads, none), weights, 0, 0)
             part_dk = dot(jnp.where(sel, queries, none), grad_scores, 0, 0)
             part_dq = dot(grad_scores, jnp.where(sel, keys, jnp.zeros_like(keys)), 1, 0)
             dv = part_dv if dv is None else dv + part_dv
@@ -170,12 +181,15 @@
     dkv_ref[1] = dv.astype(bf16)
 
 
-def attend_back(queries, grads, stats, deltas, both, extra, head_dim, first, count, start):
+def attend_back(
+    queries, grads, deltas, saved, factors, both, extra, head_dim, first, count, start
+):
     rows, width = queries.shape
     pairs = width // lanes
-    row_step = min(1024, rows)
-    step = min(512, count)
+    row_step = min(512, rows)
+    step = min(1024, count)
     skip = first // step
+    group = first * factors.shape[1] // both.shape[0]
     scale = head_dim ** (-0.5)
     resumed = start is not None
     more = [pl.BlockSpec((rows, lanes), lambda h, j: (0, h))] if resumed else []
@@ -186,7 +200,8 @@
             pl.BlockSpec((rows, lanes), lambda h, j: (0, h)),
             pl.BlockSpec((rows, lanes), lambda h, j: (0, h)),
             pl.BlockSpec((None, rows, lanes), lambda h, j: (h, 0, 0)),
-            pl.BlockSpec((None, rows, lanes), lambda h, j: (h, 0, 0)),
+            pl.BlockSpec((None, None, rows, lanes), lambda h, j: (h, group, 0, 0)),
+            pl.BlockSpec((None, 2, rows, step), lambda h, j: (h, 0, 0, j + skip)),
             pl.BlockSpec((step, lanes), lambda h, j: (j + skip, h)),
             pl.BlockSpec((step, lanes), lambda h, j: (j + skip, h + pairs)),
             pl.BlockSpec((step, lanes), lambda h, j: (j + skip, 0)),
@@ -200,14 +215,25 @@
             jax.ShapeDtypeStruct((rows, width), f32),
             jax.ShapeDtypeStruct((2, width, count), bf16),
         ],
+        scratch_shapes=[pltpu.VMEM((rows, lanes), bf16), pltpu.VMEM((rows, lanes), bf16)],
         compiler_params=pltpu.CompilerParams(vmem_limit_bytes=vmem_grant),
         cost_estimate=pl.CostEstimate(
-            flops=10 * rows * count * width * 4,
-            bytes_accessed=count * width * 8 + rows * width * 12,
-            transcendentals=rows * count * width // head_dim,
+            flops=8 * rows * count * width * 4,
+            bytes_accessed=count * width * 8 + rows * width * 16 + 4 * pairs * rows * count,
+            transcendentals=0,
         ),
         name="attend_back",
-    )(queries, grads, stats, deltas, both, both, extra, *([start] if resumed else []))
+    )(
+        queries,
+        grads,
+        deltas,
+        factors,
+        saved,
+        both,
+        both,
+        extra,
+        *([start] if resumed else []),
+    )
 
 
 def key_lanes(live, head_dim):
@@ -221,8 +247,7 @@
     owners,
     ring,
     pieces,
-    own_ref,
-    other_ref,
+    tokens_ref,
     weight_ref,
     packed_ref,
     x_ref,
@@ -242,7 +267,9 @@
 ):
     row, here = (lax.axis_index("dp"), lax.axis_index("ctx"))
     core = lax.rem(here, 2)
-    block, width = own_ref.shape
+    side = here // (ring // 2)
+    own_ref = tokens_ref.at[side]
+    block, width = tokens_ref.shape[1:]
     share = weight_ref.shape[0]
     half = share // 2
     mate, deep, far = ((row, here ^ 1), (row, here ^ 2), (row, here ^ (ring // 2)))
@@ -286,7 +313,7 @@
         send(weight_ref.at[pl.ds(core * half, half)], ws.at[row, pl.ds(core * half, half)], peer)
         for peer in owner_peers
     ]
-    moved = [send(other_ref.at[part], xs.at[1, part], far) for part in parts]
+    moved = [send(tokens_ref.at[1 - side, part], xs.at[1, part], far) for part in parts]
     own_deep = send(own_ref, xs.at[2], deep)
     own_mate = send(own_ref, xs.at[4], mate)
     vectors = [send(packed_ref, vec.at[row], peer) for peer in owner_peers]
@@ -314,7 +341,7 @@
 
     def bias(which):
         return jnp.concatenate(
-            [vec[d, :, which * share : (which + 1) * share] for d in range(owners)], axis=1
+            [vec[d, which : which + 1, :] for d in range(owners)], axis=1
         ).astype(f32)
 
     value_bias = bias(1)
@@ -361,9 +388,8 @@
         copy.wait()
 
 
-def opening(own, other, weight, packed, owners, ring):
-    block, width = own.shape
-    share = weight.shape[0]
+def opening(tokens, weight, packed, owners, ring):
+    block, width = tokens.shape[1:]
     blocks = ring
     pieces = 4
     any_space = pl.BlockSpec(memory_space=pl.ANY)
@@ -377,7 +403,7 @@
     ]
     return pl.pallas_call(
         functools.partial(opening_kernel, owners, ring, pieces),
-        in_specs=[any_space] * 4,
+        in_specs=[any_space] * 3,
         out_specs=[any_space] * 5,
         out_shape=shapes,
         scratch_shapes=[pltpu.VMEM(v.shape, v.dtype) for v in shapes]
@@ -394,7 +420,7 @@
             flops=8 * blocks * block * width * width, bytes_accessed=200 << 20, transcendentals=0
         ),
         name="opening",
-    )(own, other, weight, packed)
+    )(tokens, weight, packed)
 
 
 def middle_kernel(
@@ -497,8 +523,8 @@
     up_sum_ref[0:1, :] += jnp.concatenate(up_sums, axis=1)
 
 
-def middle(mixed, rows, cot, live, out_all, up_all, down_all, vectors, up_bias, head_dim):
-    count, width = rows.shape
+def middle(mixed, stream, cot, live, out_all, up_all, down_all, vectors, up_bias, head_dim):
+    count, width = mixed.shape
     inner = up_all.shape[1]
     pairs = width // lanes
     row_step = min(256, count)
@@ -558,7 +584,7 @@
             transcendentals=4 * count * inner,
         ),
         name="middle",
-    )(mixed, rows, cot, live, out_all, up_all, down_all, vectors, up_bias)
+    )(mixed, stream, cot, live, out_all, up_all, down_all, vectors, up_bias)
 
 
 def up_out_kernel(blocks, hidden_ref, dupper_ref, mixed_ref, dattn_ref, o_ref):
@@ -760,15 +786,9 @@
     waiting = [[], [], []]
     loads[0].wait()
     loads[1].wait()
-    small[...] = small_ref[...]
-    small[0:1, :] = jnp.sum(dq[...].astype(bf16).astype(f32), axis=0, keepdims=True)
-    for load in loads[2:]:
-        load.wait()
-    ones = jnp.ones((8, dkv.shape[2]), bf16)
-    small[1:2, :] = dot(ones, dkv[1], 1, 1)[0:1, :]
     pl.semaphore_wait(barrier, len(peers))
     home = send(home_ref, home_out_ref, (row, here ^ (ring // 2)), 3, at_back)
-    small_waits = [send(small, small_core, mate, 3, 0)]
+    small_waits = []
     for step in range(len(stages) + 2):
         for m in range(3):
             stage = step - m
@@ -776,6 +796,14 @@
                 for copy in waiting[m]:
                     copy.wait_recv()
                 waiting[m] = stages[stage](m)
+        if step == 0:
+            small[...] = small_ref[...]
+            small[0:1, :] = jnp.sum(dq[...].astype(bf16).astype(f32), axis=0, keepdims=True)
+            for load in loads[2:]:
+                load.wait()
+            ones = jnp.ones((8, dkv.shape[2]), bf16)
+            small[1:2, :] = dot(ones, dkv[1], 1, 1)[0:1, :]
+            small_waits = [send(small, small_core, mate, 3, 0)]
         if step == 1:
             small_waits[0].wait_recv()
             small_owner[0] = small[...] + small_core[...]
@@ -896,7 +924,6 @@
     def gather(array):
         return lax.all_gather(array, "dp", axis=0, tiled=True)
 
-    own, other = (pick(tokens, side), pick(tokens, 1 - side))
     bits = []
     bit = half // 2
     while bit:
@@ -932,25 +959,26 @@
         ffn_gain,
         ffn_shift,
     ]
-    packed = jnp.concatenate(singles + [up_bias])[None, :]
+    packed = jnp.concatenate([jnp.stack(singles), up_bias.reshape(-1, share)], axis=0)
     if laid:
         stream, qkv_all, vectors, queries, both = opening(
-            own, other, qkv_weight, packed, owners, ring
+            tokens, qkv_weight, packed, owners, ring
         )
         stream = stream.reshape(-1, width)
         qkv_all = qkv_all.reshape(width, -1)
-        vectors = vectors.reshape(owners, -1).astype(f32)
+        vectors = vectors.astype(f32)
         queries = queries.reshape(-1, width)
         both = both.reshape(-1, 2 * width)
     else:
         qkv_all = gather(qkv_weight)
-        vectors = gather(packed).astype(f32)
-        stream = jnp.concatenate([own, exchange(other, half)], axis=0)
+        vectors = gather(packed[None]).astype(f32)
+        other = exchange(pick(tokens, 1 - side), half)
+        stream = jnp.concatenate([pick(tokens, side), other], axis=0)
         for bit in bits:
             stream = jnp.concatenate([stream, exchange(stream, bit)], axis=0)
     rows = stream[:count_rows]
-    bias = [vectors[:, i * share : (i + 1) * share].reshape(1, width) for i in range(8)]
-    up_bias_all = vectors[:, 8 * share :].reshape(1, -1)
+    bias = [vectors[:, i].reshape(1, width) for i in range(8)]
+    up_bias_all = vectors[:, 8:].reshape(1, -1)
     if not laid:
         queries = (
             jnp.dot(rows, qkv_all[:, :width], preferred_element_type=f32) + bias[0]
@@ -964,7 +992,7 @@
     held, _ = lax.optimization_barrier((cotangent, stream))
     cot = jnp.concatenate([pick(held, side), exchange(pick(held, 1 - side), half)], axis=0)
 
-    mixed, stats = attend(queries, both, extra, head_dim)
+    mixed, saved, factors = attend(queries, both, extra, head_dim)
     (
         result,
         active,
@@ -979,7 +1007,7 @@
         up_sum,
     ) = middle(
         mixed,
-        rows,
+        stream,
         cot,
         live_rows,
         out_all,
@@ -1019,7 +1047,17 @@
                 held, grad_queries = lax.optimization_barrier((scattered, grad_queries))
                 gathered.append(spread(held))
             grad_queries, grad_both = attend_back(
-                queries, grad_mixed, stats, deltas, both, extra, head_dim, first, size, grad_queries
+                queries,
+                grad_mixed,
+                deltas,
+                saved,
+                factors,
+                both,
+                extra,
+                head_dim,
+                first,
+                size,
+                grad_queries,
             )
             shares.append((first, grad_both))
             return dot(grad_both.reshape(2 * width, size), kv_weight, 0, 1)

time: 543 us -> 532 us (0.980)
  Pallas kernels: 424 us -> 397 us
  waiting for transfers between devices: 17.9 us -> 38 us
  local copies, waits for them, and re-layouts: 29.8 us -> 24.1 us
    pallas_call x4, Pallas kernels: 153 us -> 125 us  [attend_back(): pl.pallas_call(functools.partial(attend_back_kernel, scale, head_dim, row...]
    ppermute x5, waiting for transfers between devices: 0.01 us -> 13.3 us  [exchange(): return lax.ppermute(array, 'ctx', [(i, i ^ bit) for i in range(ring)])]
    reduce_scatter x1, waiting for transfers between devices: 10.8 us -> 20.9 us  [scatter(): lax.psum_scatter(grad, ('dp', 'ctx'), scatter_dimension=0, tiled=True)]
    pallas_call x1, Pallas kernels: 77 us -> 70.6 us  [closing(): pl.pallas_call(functools.partial(closing_kernel, owners, ring, firsts), i...]
    pallas_call x1, Pallas kernels: 70.6 us -> 76.9 us  [attend(): pl.pallas_call(functools.partial(attend_kernel, scale, head_dim, step), g...]
    another operation x1 -> x15, local copies, waits for them, and re-layouts: 0.01 us -> 5.77 us  [the longest x8 5.26 us: shards(): jnp.stack(singles)]
  transfers between devices with their start and end apart: 10 -> 10, of which waited for: 2 -> 3; matrix products, arithmetic and copies ran while one was open for 10% -> 9% of each run, Pallas kernels for 53% -> 50%
where the time goes in v4:
time: 532 us; the launch traced here: 523 us
  Pallas kernels  397 us (75%)
  waiting for transfers between devices  38 us (7%)
  matrix products  24.2 us (5%)
  local copies, waits for them, and re-layouts  24.1 us (5%)
  other arithmetic  15.4 us (3%)
  between operations  14.6 us (3%)
  starting transfers between devices  9.61 us (2%)
    pallas_call x4, Pallas kernels, attend_back(): pl.pallas_call(functools.partial(attend_back_kernel, scale, head_dim, row...  125 us
    pallas_call x1, Pallas kernels, attend(): pl.pallas_call(functools.partial(attend_kernel, scale, head_dim, step), g...  76.9 us
    pallas_call x1, Pallas kernels, closing(): pl.pallas_call(functools.partial(closing_kernel, owners, ring, firsts), i...  70.6 us
    pallas_call x1, Pallas kernels, opening(): pl.pallas_call(functools.partial(opening_kernel, owners, ring, pieces), i...  61.5 us
    pallas_call x1, Pallas kernels, middle(): pl.pallas_call(functools.partial(middle_kernel, head_dim, chunk), grid=(c...  41.4 us
    dot_general x5, matrix products, dot(): lax.dot_general(left, right, (((left_dim,), (right_dim,)), ((), ())), pre...  24.2 us
    reduce_scatter x1, waiting for transfers between devices, scatter(): lax.psum_scatter(grad, ('dp', 'ctx'), scatter_dimension=0, tiled=True)  20.9 us
    ppermute x5, waiting for transfers between devices, exchange(): return lax.ppermute(array, 'ctx', [(i, i ^ bit) for i in range(ring)])  13.3 us
  transfers between devices with their start and end apart: 10, of which 3 were waited for; matrix products, arithmetic and copies ran while one was open for 9% of the time, Pallas kernels for 50%

profile of v4, /device:TPU:1, one launch (start us, length us, event | category | flops | bytes accessed | tf_op | source)
XLA Modules:
  0.0 522.5 jit_solution(17089869127430199244)
XLA Ops:
  14.8 1.2 concatenate.23.packed_ref
  16.0 61.5 %opening.1 = (bf16[8,512,768]{2,1,0:T(8,128)(2,1)}, bf16[4,192,2304]{2,1,0:T(8,128)(2,1)}, bf16[4,12,192]{2,1,0:T(8,128)(2,1)}, bf16[2,512,768]{2,1,0:T(8,128)(2,1)}, bf16[8,512,1536]{2,1,0:T(8,128)(2,1)}) custom-call(bf16[2,512,768]{2,1,0:T(8,128)(2,1)} %tokens_ref.1, bf16[192,2304]{1,0:T(8,128)(2,1)} %weight_ref.1, bf16[12,192]{1,0:T(8,128)(2,1)} %concatenate.23.packed_ref), custom_call_target="tpu_custom_call" | custom-call | flops 19327352832 | bytes 209715200 | tf_op jit(solution)/shard_map/opening/pallas_call | solution.py:404
  77.7 2.3 collective-permute-start
  81.8 1.7 select_convert_fusion.extra_ref.refs_7_
  83.5 76.9 %attend.1 = (bf16[1024,768]{1,0:T(8,128)(2,1)}, bf16[6,2,1024,4096]{3,2,1,0:T(8,128)(2,1)}, f32[6,2,1024,128]{3,2,1,0:T(8,128)}) custom-call(bf16[1024,768]{1,0:T(8,128)(2,1)} %bitcast.65, bf16[4096,1536]{1,0:T(8,128)(2,1)} %bitcast.55, bf16[4096,1536]{1,0:T(8,128)(2,1)} %bitcast.56, bf16[4096,128]{1,0:T(8,128)(2,1)} %select_convert_fusion.extra_ref.refs_7_), custom_call_target="tpu_custom_call" | custom-call | flops 51539607552 | bytes 117964800 | tf_op jit(solution)/shard_map/attend/pallas_call | solution.py:106
  164.1 1.2 pad_maximum_fusion.1.cot_ref
  165.4 2.3 all-gather.9.cloned.1.call-done.down_ref
  167.7 41.4 %middle.1 = (bf16[1024,768]{1,0:T(8,128)(2,1)}, bf16[1024,3072]{1,0:T(8,128)(2,1)}, bf16[1024,768]{1,0:T(8,128)(2,1)}, bf16[1024,768]{1,0:T(8,128)(2,1)}, bf16[1...) custom-call(bf16[1024,768]{1,0:T(8,128)(2,1)} %get-tuple-element.60., ...), custom_call_target="tpu_custom_call" | custom-call | flops 21743271936 | bytes 36175872 | tf_op jit(solution)/shard_map/middle/pallas_call | solution.py:539
  209.1 11.7 %up_grads.1.held_ref = bf16[32,216,768]{2,1,0:T(8,128)(2,1)} custom-call(bf16[1024,768]{1,0:T(8,128)(2,1)} %get-tuple-element.72.hidden_ref, bf16[1024,3072]{1,0:T(8,128)(2,1)} %get-tuple-element.73.dupper_ref, bf16[1024,768]{1,0:T(8,128)(2,1)} %get-tuple-element.60.mixed_ref, bf16[1024,768]{1,0:T(8,128)(2,1)} %get-tuple-element.74.dattn_ref), custom_call_target="tpu_custom_call" | custom-call | flops 6039797760 | bytes 19267584 | tf_op jit(solution)/shard_map/up_grads/pallas_call | solution.py:618
  220.8 9.2 %down_grads.1 = bf16[32,216,768]{2,1,0:T(8,128)(2,1)} custom-call(bf16[1024,3072]{1,0:T(8,128)(2,1)} %get-tuple-element.70.active_ref, bf16[1024,768]{1,0:T(8,128)(2,1)} %get-tuple-element.71.dbranch_ref, bf16[32,216,768]{2,1,0:T(8,128)(2,1)} %up_grads.1.held_ref), custom_call_target="tpu_custom_call", output_to_operand_aliasing={{}: (2, {})} | custom-call | flops 4831838208 | bytes 13762560 | tf_op jit(solution)/shard_map/down_grads/pallas_call | solution.py:640
  231.4 2.2 collective-permute-start.1
  233.7 31.7 %attend_back.4 = (f32[1024,768]{1,0:T(8,128)}, bf16[2,768,1024]{2,1,0:T(8,128)(2,1)}) custom-call(bf16[1024,768]{1,0:T(8,128)(2,1)} %bitcast.66, bf16[1024,768]{1,0:T(8,128)(2,1)} %get-tuple-element.66.refs_1_, bf16[6,1024,128]{2,1,0:T(8,128)(2,1)} %get-tuple-element.67.refs_2_, f32[6,2,1024,128]{3,2,1,0:T(8,128)} %get-tuple-element.68.refs_3_, ...), custom_call_target="tpu_custom_call" | custom-call | flops 25769803776 | bytes 44040192 | tf_op jit(solution)/shard_map/attend_back/pallas_call | solution.py:196
  265.3 5.9 %convolution_convert_fusion.1 = bf16[1024,768]{1,0:T(8,128)(2,1)} fusion(bf16[1536,1024]{1,0:T(8,128)(2,1)} %bitcast.93, bf16[768,2304]{1,0:T(8,128)(2,1)S(1)} %bitcast.78), kind=kOutput, calls=%fused_computation.5 | convolution fusion | flops 2416705536 | bytes 7077888 | tf_op jit(solution)/shard_map/dot_general | solution.py:37
  274.0 2.0 compare_select_fusion.2
  276.0 31.3 %attend_back.5 = (f32[1024,768]{1,0:T(8,128)}, bf16[2,768,1024]{2,1,0:T(8,128)(2,1)}) custom-call(bf16[1024,768]{1,0:T(8,128)(2,1)} %bitcast.67, bf16[1024,768]{1,0:T(8,128)(2,1)} %get-tuple-element.66.refs_1_, bf16[6,1024,128]{2,1,0:T(8,128)(2,1)} %get-tuple-element.67.refs_2_, f32[6,2,1024,128]{3,2,1,0:T(8,128)} %get-tuple-element.68.refs_3_, ...), custom_call_target="tpu_custom_call" | custom-call | flops 25769803776 | bytes 44040192 | tf_op jit(solution)/shard_map/attend_back/pallas_call | solution.py:196
  307.3 6.3 %add_convert_fusion.1 = bf16[1024,768]{1,0:T(8,128)(2,1)} fusion(bf16[1024,768]{1,0:T(8,128)(2,1)} %collective-permute-done.2, bf16[1536,1024]{1,0:T(8,128)(2,1)} %bitcast.94, bf16[768,2304]{1,0:T(8,128)(2,1)S(1)} %bitcast.79), kind=kOutput, calls=%fused_computation.1 | convolution fusion | flops 2418278400 | bytes 8650752 | tf_op jit(solution)/shard_map/dot_general | solution.py:37
  313.6 31.1 %attend_back.6 = (f32[1024,768]{1,0:T(8,128)}, bf16[2,768,1024]{2,1,0:T(8,128)(2,1)}) custom-call(bf16[1024,768]{1,0:T(8,128)(2,1)} %bitcast.68, bf16[1024,768]{1,0:T(8,128)(2,1)} %get-tuple-element.66.refs_1_, bf16[6,1024,128]{2,1,0:T(8,128)(2,1)} %get-tuple-element.67.refs_2_, f32[6,2,1024,128]{3,2,1,0:T(8,128)} %get-tuple-element.68.refs_3_, ...), custom_call_target="tpu_custom_call" | custom-call | flops 25769803776 | bytes 44040192 | tf_op jit(solution)/shard_map/attend_back/pallas_call | solution.py:196
  344.7 5.8 %convolution_convert_fusion = bf16[1024,768]{1,0:T(8,128)(2,1)} fusion(bf16[1536,1024]{1,0:T(8,128)(2,1)} %bitcast.95, bf16[768,2304]{1,0:T(8,128)(2,1)S(1)} %bitcast.80), kind=kOutput, calls=%fused_computation.4 | convolution fusion | flops 2416705536 | bytes 7077888 | tf_op jit(solution)/shard_map/dot_general | solution.py:37
  350.5 20.9 %reduce-scatter.2.cloned.1.call-done = bf16[1,216,768]{2,1,0:T(8,128)(2,1)} async-done(((bf16[32,216,768]{2,1,0:T(8,128)(2,1)}), bf16[1,216,768]{2,1,0:T(8,128)(2,1)}) %reduce-scatter.2.cloned.1.call-update) | async-done | bytes 331792 | tf_op jit(solution)/shard_map/reduce_scatter | solution.py:1023
  372.2 1.3 pad_maximum_fusion.2
  374.5 2.7 collective-permute-start.3
  377.3 31.4 %attend_back.7 = (f32[1024,768]{1,0:T(8,128)}, bf16[2,768,1024]{2,1,0:T(8,128)(2,1)}) custom-call(bf16[1024,768]{1,0:T(8,128)(2,1)} %bitcast.69, bf16[1024,768]{1,0:T(8,128)(2,1)} %get-tuple-element.66.refs_1_, bf16[6,1024,128]{2,1,0:T(8,128)(2,1)} %get-tuple-element.67.refs_2_, f32[6,2,1024,128]{3,2,1,0:T(8,128)} %get-tuple-element.68.refs_3_, ...), custom_call_target="tpu_custom_call" | custom-call | flops 25769803776 | bytes 44040192 | tf_op jit(solution)/shard_map/attend_back/pallas_call | solution.py:196
  408.7 3.5 fusion
  412.2 2.7 fusion.2
  414.9 13.3 %collective-permute-done.4 = bf16[1024,768]{1,0:T(8,128)(2,1)S(1)} collective-permute-done((bf16[1024,768]{1,0:T(8,128)(2,1)}, bf16[1024,768]{1,0:T(8,128)(2,1)S(1)}, u32[]{:S(2)}, u32[]{:S(2)}) %collective-permute-start.4) | collective-permute-done | bytes 1572896 | tf_op jit(solution)/shard_map/ppermute | solution.py:917
  430.0 70.6 %closing.1 = (f32[2,96,2304]{2,1,0:T(8,128)}, f32[16,768]{1,0:T(8,128)}, bf16[512,768]{1,0:T(8,128)(2,1)}) custom-call(f32[1024,768]{1,0:T(8,128)} %get-tuple-element.93.dq_ref, bf16[4096,768]{1,0:T(8,128)(2,1)} %bitcast.98, bf16[2,768,1024]{2,1,0:T(8,128)(2,1)} %get-tuple-element.75.refs_0_, bf16[2,768,1024]{2,1,0:T(8,128)(2,1)} %get-tuple-element.79.refs_1_, ...), custom_call_target="tpu_custom_call" | custom-call | flops 48318382080 | bytes 104857600 | tf_op jit(solution)/shard_map/closing/pallas_call | solution.py:846
  500.7 1.3 fusion.15
  502.7 1.6 fusion.14
  504.3 1.6 slice.160
  506.2 1.3 pad_maximum_fusion.3
  511.4 2.9 pad_maximum_fusion
  514.3 1.2 copy.42
  (118 shorter events, 26.0 us)
Async XLA Ops:
  7.2 73.5 %copy-start = (s32[2,8]{1,0:T(2,128)S(1)}, s32[2,8]{1,0:T(2,128)}, u32[]{:S(2)}) copy-start(s32[2,8]{1,0:T(2,128)} %param.20) | copy-start | bytes 196
  7.2 158.2 %all-gather.5.cloned.1.call-start = ((), (), s32[]{:S(2)}) async-start(), calls=%async_computation.1 | async-start | bytes 1474560 | tf_op jit(solution)/shard_map/all_gather | solution.py:925
  7.9 157.5 %all-gather.7.cloned.1.call-start = ((), (), s32[]{:S(2)}) async-start(), calls=%async_computation.2 | async-start | bytes 5898240 | tf_op jit(solution)/shard_map/all_gather | solution.py:925
  8.7 159.0 %all-gather.9.cloned.1.call-start = ((), (), s32[]{:S(2)}) async-start(), calls=%async_computation.3 | async-start | bytes 5898240 | tf_op jit(solution)/shard_map/all_gather | solution.py:925
  16.0 61.6 %copy-start.7 = (bf16[2,512,768]{2,1,0:T(8,128)(2,1)S(1)}, bf16[2,512,768]{2,1,0:T(8,128)(2,1)}, u32[]{:S(2)}) copy-start(bf16[2,512,768]{2,1,0:T(8,128)(2,1)} %param.18) | copy-start | bytes 4718596
  77.5 2.5 copy-start.19
  77.7 86.4 %collective-permute-start = (bf16[512,768]{1,0:T(8,128)(2,1)S(1)}, bf16[512,768]{1,0:T(8,128)(2,1)S(1)}, u32[]{:S(2)}, u32[]{:S(2)}) collective-permute-start(bf16[512,768]{1,0:T(8,128)(2,1)S(1)} %get-tuple-element.116), channel_id=1, source_target_pairs={{0,4},{1,5},{2,6},{3,7},{4,0},{5,1},{6,2},{7,3},{8,12},{9,13},{10,... | collective-permute-start | bytes 2359304 | tf_op jit(solution)/shard_map/ppermute | solution.py:917
  80.0 291.4 %reduce-scatter.2.cloned.1.call-start = ((), (), s32[]{:S(2)}) async-start(), calls=%async_computation.4 | async-start | bytes 10948608 | tf_op jit(solution)/shard_map/reduce_scatter | solution.py:1023
  83.5 76.9 %copy-start.13 = (bf16[4,12,192]{2,1,0:T(8,128)(2,1)S(1)}, bf16[4,12,192]{2,1,0:T(8,128)(2,1)}, u32[]{:S(2)}) copy-start(bf16[4,12,192]{2,1,0:T(8,128)(2,1)} %get-tuple-element.63) | copy-start | bytes 55300
  163.5 45.6 %copy-start.14 = (f32[2,768]{1,0:T(2,128)}, f32[2,768]{1,0:T(2,128)S(1)}, u32[]{:S(2)}) copy-start(f32[2,768]{1,0:T(2,128)S(1)} %broadcast.213) | copy-start | bytes 18436
  230.0 1.4 copy-start.8
  230.0 199.1 %all-gather.11.cloned.1.call-start = ((), (), s32[]{:S(2)}) async-start(), calls=%async_computation.5 | async-start | bytes 2985984 | tf_op jit(solution)/shard_map/all_gather | solution.py:1026
  231.4 140.6 %collective-permute-start.1 = (bf16[512,768]{1,0:T(8,128)(2,1)S(1)}, bf16[512,768]{1,0:T(8,128)(2,1)S(1)}, u32[]{:S(2)}, u32[]{:S(2)}) collective-permute-start(bf16[512,768]{1,0:T(8,128)(2,1)S(1)} %slice.118), channel_id=1, source_target_pairs={{0,4},{1,5},{2,6},{3,7},{4,0},{5,1},{6,2},{7,3},{8,12},{9,13},{10,... | collective-permute-start | bytes 2359304 | tf_op jit(solution)/shard_map/ppermute | solution.py:917
  233.7 31.7 %copy-start.10 = (bf16[4,192,2304]{2,1,0:T(8,128)(2,1)S(1)}, bf16[4,192,2304]{2,1,0:T(8,128)(2,1)}, u32[]{:S(2)}) copy-start(bf16[4,192,2304]{2,1,0:T(8,128)(2,1)} %get-tuple-element.76) | copy-start | bytes 10616836
  265.3 8.0 %copy-start.16 = (f32[16,768]{1,0:T(8,128)S(1)}, f32[16,768]{1,0:T(8,128)}, u32[]{:S(2)}) copy-start(f32[16,768]{1,0:T(8,128)} %get-tuple-element.94) | copy-start | bytes 147460
  271.2 36.0 %collective-permute-start.2 = (bf16[1024,768]{1,0:T(8,128)(2,1)}, bf16[1024,768]{1,0:T(8,128)(2,1)}, u32[]{:S(2)}, u32[]{:S(2)}) collective-permute-start(bf16[1024,768]{1,0:T(8,128)(2,1)} %convolution_convert_fusion.1), channel_id=1, source_target_pairs={{0,1},{1,0},{2,3},{3,2},{4,5},{5,4},{6,7},{7,6},{8,9},{9,8},{10,11... | collective-permute-start | bytes 4718600 | tf_op jit(solution)/shard_map/ppermute | solution.py:917
  276.0 31.3 %copy-start.11 = (bf16[4,192,2304]{2,1,0:T(8,128)(2,1)S(1)}, bf16[4,192,2304]{2,1,0:T(8,128)(2,1)}, u32[]{:S(2)}) copy-start(bf16[4,192,2304]{2,1,0:T(8,128)(2,1)} %get-tuple-element.76) | copy-start | bytes 10616836
  344.7 26.8 %copy-start.15 = (f32[2,768]{1,0:T(2,128)S(1)}, f32[2,768]{1,0:T(2,128)}, u32[]{:S(2)}) copy-start(f32[2,768]{1,0:T(2,128)} %copy-done.14) | copy-start | bytes 18436
  373.5 35.2 %copy-start.12 = (bf16[4,192,2304]{2,1,0:T(8,128)(2,1)S(1)}, bf16[4,192,2304]{2,1,0:T(8,128)(2,1)}, u32[]{:S(2)}) copy-start(bf16[4,192,2304]{2,1,0:T(8,128)(2,1)} %get-tuple-element.76) | copy-start | bytes 10616836
  373.5 54.7 %collective-permute-start.4 = (bf16[1024,768]{1,0:T(8,128)(2,1)}, bf16[1024,768]{1,0:T(8,128)(2,1)S(1)}, u32[]{:S(2)}, u32[]{:S(2)}) collective-permute-start(bf16[1024,768]{1,0:T(8,128)(2,1)} %add_convert_fusion.1), channel_id=1, source_target_pairs={{0,2},{1,3},{2,0},{3,1},{4,6},{5,7},{6,4},{7,5},{8,10},{9,11},{10,... | collective-permute-start | bytes 4718600 | tf_op jit(solution)/shard_map/ppermute | solution.py:917
  374.5 53.6 %collective-permute-start.3 = (bf16[1024,768]{1,0:T(8,128)(2,1)}, bf16[1024,768]{1,0:T(8,128)(2,1)S(1)}, u32[]{:S(2)}, u32[]{:S(2)}) collective-permute-start(bf16[1024,768]{1,0:T(8,128)(2,1)} %convolution_convert_fusion), channel_id=1, source_target_pairs={{0,1},{1,0},{2,3},{3,2},{4,5},{5,4},{6,7},{7,6},{8,9},{9,8},{10,11... | collective-permute-start | bytes 4718600 | tf_op jit(solution)/shard_map/ppermute | solution.py:917
  408.7 3.5 copy-start.18
  412.2 16.0 %copy-start.3 = (f32[1024,768]{1,0:T(8,128)S(1)}, f32[1024,768]{1,0:T(8,128)}, u32[]{:S(2)}) copy-start(f32[1024,768]{1,0:T(8,128)} %get-tuple-element.65) | copy-start | bytes 9437188
  430.0 72.6 %copy-start.2 = (bf16[8,216,768]{2,1,0:T(8,128)(2,1)S(1)}, bf16[8,216,768]{2,1,0:T(8,128)(2,1)}, u32[]{:S(2)}) copy-start(bf16[8,216,768]{2,1,0:T(8,128)(2,1)} %all-gather.11.cloned.1.call-done) | copy-start | bytes 7962628
  504.3 1.6 copy-start.9
  505.9 4.8 copy-start.17
  506.0 5.4 %copy-start.4 = (f32[8,24,768]{2,1,0:T(8,128)S(1)}, f32[8,24,768]{2,1,0:T(8,128)}, u32[]{:S(2)}) copy-start(f32[8,24,768]{2,1,0:T(8,128)} %get-tuple-element.106) | copy-start | bytes 1769476
  506.0 5.4 %copy-start.5 = (f32[8,24,768]{2,1,0:T(8,128)S(1)}, f32[8,24,768]{2,1,0:T(8,128)}, u32[]{:S(2)}) copy-start(f32[8,24,768]{2,1,0:T(8,128)} %get-tuple-element.107) | copy-start | bytes 1769476
  507.5 6.8 %copy-start.6 = (f32[2,96,2304]{2,1,0:T(8,128)S(1)}, f32[2,96,2304]{2,1,0:T(8,128)}, u32[]{:S(2)}) copy-start(f32[2,96,2304]{2,1,0:T(8,128)} %get-tuple-element.97) | copy-start | bytes 5308420
  511.4 4.2 copy-start.1
Sparse Core Ops, SparseCore 0:
  9.9 40.5 all-gather.4
  52.3 56.3 all-gather.6
  110.6 57.0 all-gather.8
  230.1 141.2 reduce-scatter.1
  372.9 52.2 all-gather.10

commit v5 on v4

--- a/solution.py
+++ b/solution.py
@@ -587,21 +587,30 @@
     )(mixed, stream, cot, live, out_all, up_all, down_all, vectors, up_bias)
 
 
-def up_out_kernel(blocks, hidden_ref, dupper_ref, mixed_ref, dattn_ref, o_ref):
+def put_pieces(value, keep_ref, give_ref):
+    share, width = keep_ref.shape[1:]
+    core = lax.rem(lax.axis_index("ctx"), 2)
+    value = value.reshape(-1, 2, share, width)
+    even, odd = (value[:, 0], value[:, 1])
+    keep_ref[...] = jnp.where(core == 0, even, odd).astype(bf16)
+    give_ref[...] = jnp.where(core == 0, odd, even).astype(bf16)
+
+
+def up_out_kernel(blocks, hidden_ref, dupper_ref, mixed_ref, dattn_ref, keep_ref, give_ref):
     s = pl.program_id(0)
 
     @pl.when(s < blocks)
     def _():
-        o_ref[...] = dot(hidden_ref[...], dupper_ref[...], 0, 0).astype(bf16).reshape(o_ref.shape)
+        put_pieces(dot(hidden_ref[...], dupper_ref[...], 0, 0), keep_ref, give_ref)
 
     @pl.when(s == blocks)
     def _():
-        o_ref[...] = dot(mixed_ref[...], dattn_ref[...], 0, 0).astype(bf16).reshape(o_ref.shape)
-
-
-def down_kernel(active_ref, dbranch_ref, held_ref, o_ref):
-    del held_ref
-    o_ref[...] = dot(active_ref[...], dbranch_ref[...], 0, 0).astype(bf16).reshape(o_ref.shape)
+        put_pieces(dot(mixed_ref[...], dattn_ref[...], 0, 0), keep_ref, give_ref)
+
+
+def down_kernel(active_ref, dbranch_ref, held_keep, held_give, keep_ref, give_ref):
+    del held_keep, held_give
+    put_pieces(dot(active_ref[...], dbranch_ref[...], 0, 0), keep_ref, give_ref)
 
 
 def middle_grads(hidden, dupper, mixed, dattn, active, dbranch, owners, ring):
@@ -612,10 +621,11 @@
     blocks = inner // width
     tall = inner // devices
     piece = blocks * share + tall + share
-    shape = jax.ShapeDtypeStruct((devices, piece, width), bf16)
+    shape = [jax.ShapeDtypeStruct((devices // 2, piece, width), bf16)] * 2
     params = pltpu.CompilerParams(vmem_limit_bytes=vmem_grant)
     whole = pl.BlockSpec((count, width), lambda s: (0, 0))
-    held = pl.pallas_call(
+    any_space = pl.BlockSpec(memory_space=pl.ANY)
+    keep, give = pl.pallas_call(
         functools.partial(up_out_kernel, blocks),
         grid=(blocks + 1,),
         in_specs=[
@@ -624,10 +634,13 @@
             whole,
             whole,
         ],
-        out_specs=pl.BlockSpec(
-            (devices, share, width),
-            lambda s: (0, jnp.where(s < blocks, s, piece // share - 1), 0),
-        ),
+        out_specs=[
+            pl.BlockSpec(
+                (devices // 2, share, width),
+                lambda s: (0, jnp.where(s < blocks, s, piece // share - 1), 0),
+            )
+        ]
+        * 2,
         out_shape=shape,
         compiler_params=params,
         cost_estimate=pl.CostEstimate(
@@ -643,11 +656,15 @@
         in_specs=[
             pl.BlockSpec((count, inner // owners), lambda s: (0, s)),
             whole,
-            pl.BlockSpec(memory_space=pl.ANY),
+            any_space,
+            any_space,
         ],
-        out_specs=pl.BlockSpec((ring, tall, width), lambda s: (s, blocks * share // tall, 0)),
+        out_specs=[
+            pl.BlockSpec((ring // 2, tall, width), lambda s: (s, blocks * share // tall, 0))
+        ]
+        * 2,
         out_shape=shape,
-        input_output_aliases={2: 0},
+        input_output_aliases={2: 0, 3: 1},
         compiler_params=params,
         cost_estimate=pl.CostEstimate(
             flops=2 * count * width * inner,
@@ -655,7 +672,7 @@
             transcendentals=0,
         ),
         name="down_grads",
-    )(active, dbranch, held)
+    )(active, dbranch, keep, give)
 
 
 def closing_kernel(owners, ring, firsts, dq_ref, x_ref, *refs):
@@ -959,7 +976,12 @@
         ffn_gain,
         ffn_shift,
     ]
-    packed = jnp.concatenate([jnp.stack(singles), up_bias.reshape(-1, share)], axis=0)
+    ups = up_bias.reshape(-1, share)
+    count_vectors = len(singles) + ups.shape[0]
+    which = lax.broadcasted_iota(jnp.int32, (count_vectors, share), 0)
+    packed = jnp.pad(ups, ((len(singles), 0), (0, 0)))
+    for i, v in enumerate(singles):
+        packed = jnp.where(which == i, v[None, :], packed)
     if laid:
         stream, qkv_all, vectors, queries, both = opening(
             tokens, qkv_weight, packed, owners, ring
@@ -1026,13 +1048,16 @@
         return jax.tree.map(lambda v: lax.all_gather(v, "ctx", axis=0, tiled=True), parts)
 
     if laid:
-        scattered = scatter(
-            middle_grads(hidden, grad_upper, mixed, grad_attn, active, grad_branch, owners, ring)
+        keep, give = middle_grads(
+            hidden, grad_upper, mixed, grad_attn, active, grad_branch, owners, ring
         )
+        given = exchange(give, 1)
+        scattered = None
     else:
         grads = (dot(hidden, grad_upper, 0, 0), dot(active, grad_branch, 0, 0), dot(mixed, grad_attn, 0, 0))
         scattered = tuple(scatter(grad.astype(bf16)) for grad in grads)
     gathered = []
+    calls = []
 
     kv_weight = qkv_all[:, width:]
     size = 2 * block
@@ -1040,12 +1065,25 @@
     shares = []
 
     def reduced(place, level):
-        nonlocal grad_queries
+        nonlocal grad_queries, scattered
         if level == len(bits):
             first = place * size
+            if laid and len(calls) == 1:
+                both_cores = keep + given
+                both_cores, grad_queries = lax.optimization_barrier((both_cores, grad_queries))
+                scattered = lax.psum_scatter(
+                    both_cores,
+                    ("dp", "ctx"),
+                    scatter_dimension=0,
+                    axis_index_groups=[
+                        [n for n in range(devices) if n % 2 == core] for core in range(2)
+                    ],
+                    tiled=True,
+                )
             if place == 0:
                 held, grad_queries = lax.optimization_barrier((scattered, grad_queries))
                 gathered.append(spread(held))
+            calls.append(place)
             grad_queries, grad_both = attend_back(
                 queries,
                 grad_mixed,
@@ -1064,7 +1102,14 @@
         low = reduced(place + (1 << level), level + 1).astype(bf16)
         low, grad_queries = lax.optimization_barrier((low, grad_queries))
         other = exchange(low, bits[level])
-        return reduced(place, level + 1) + other.astype(f32)
+        if level + 1 == len(bits):
+            return reduced(place, level + 1) + other.astype(f32)
+        if level + 2 < len(bits):
+            return reduced(place, level + 1) + other.astype(f32)
+        low = reduced(place + (1 << (level + 1)), level + 2).astype(bf16)
+        low, other, grad_queries = lax.optimization_barrier((low, other, grad_queries))
+        mate = exchange(low, bits[level + 1])
+        return reduced(place, level + 2) + mate.astype(f32) + other.astype(f32)
 
     grad_stream = reduced(0, 0)
     grad_query_low = grad_queries.astype(bf16)

time: 532 us -> 584 us (1.098)
  waiting for transfers between devices: 38 us -> 89 us
  other arithmetic: 15.4 us -> 21.8 us
    reduce_scatter x1, waiting for transfers between devices: 20.9 us -> 64.5 us  [reduced(): lax.psum_scatter(both_cores, ('dp', 'ctx'), scatter_dimension=0, axis_ind...]
    ppermute x5 -> x6, waiting for transfers between devices: 13.3 us -> 19.8 us  [exchange(): return lax.ppermute(array, 'ctx', [(i, i ^ bit) for i in range(ring)])]
  transfers between devices with their start and end apart: 10 -> 11, of which waited for: 3 -> 3; matrix products, arithmetic and copies ran while one was open for 9% -> 8% of each run, Pallas kernels for 50% -> 46%
where the time goes in v5:
time: 584 us; the launch traced here: 575 us
  Pallas kernels  396 us (68%)
  waiting for transfers between devices  89 us (15%)
  matrix products  24.7 us (4%)
  other arithmetic  21.8 us (4%)
  local copies, waits for them, and re-layouts  20.2 us (3%)
  between operations  14.6 us (2%)
  starting transfers between devices  9.3 us (2%)
    pallas_call x4, Pallas kernels, attend_back(): pl.pallas_call(functools.partial(attend_back_kernel, scale, head_dim, row...  125 us
    pallas_call x1, Pallas kernels, attend(): pl.pallas_call(functools.partial(attend_kernel, scale, head_dim, step), g...  76.9 us
    pallas_call x1, Pallas kernels, closing(): pl.pallas_call(functools.partial(closing_kernel, owners, ring, firsts), i...  70.4 us
    reduce_scatter x1, waiting for transfers between devices, reduced(): lax.psum_scatter(both_cores, ('dp', 'ctx'), scatter_dimension=0, axis_ind...  64.5 us
    pallas_call x1, Pallas kernels, opening(): pl.pallas_call(functools.partial(opening_kernel, owners, ring, pieces), i...  61.5 us
    pallas_call x1, Pallas kernels, middle(): pl.pallas_call(functools.partial(middle_kernel, head_dim, chunk), grid=(c...  41.4 us
    dot_general x5, matrix products, dot(): lax.dot_general(left, right, (((left_dim,), (right_dim,)), ((), ())), pre...  24.7 us
    ppermute x6, waiting for transfers between devices, exchange(): return lax.ppermute(array, 'ctx', [(i, i ^ bit) for i in range(ring)])  19.8 us
  transfers between devices with their start and end apart: 11, of which 3 were waited for; matrix products, arithmetic and copies ran while one was open for 8% of the time, Pallas kernels for 46%

profile of v5, /device:TPU:1, one launch (start us, length us, event | category | flops | bytes accessed | tf_op | source)
XLA Modules:
  0.0 575.3 jit_solution(8511463237844351446)
XLA Ops:
  9.5 1.5 select_select_fusion.packed_ref
  11.0 61.5 %opening.1 = (bf16[8,512,768]{2,1,0:T(8,128)(2,1)}, bf16[4,192,2304]{2,1,0:T(8,128)(2,1)}, bf16[4,12,192]{2,1,0:T(8,128)(2,1)}, bf16[2,512,768]{2,1,0:T(8,128)(2,1)}, bf16[8,512,1536]{2,1,0:T(8,128)(2,1)}) custom-call(bf16[2,512,768]{2,1,0:T(8,128)(2,1)} %tokens_ref.1, bf16[192,2304]{1,0:T(8,128)(2,1)} %weight_ref.1, ...), custom_call_target="tpu_custom_call" | custom-call | flops 19327352832 | bytes 209715200 | tf_op jit(solution)/shard_map/opening/pallas_call | solution.py:404
  72.7 2.3 collective-permute-start
  76.8 1.6 select_convert_fusion.extra_ref.refs_7_
  78.4 76.9 %attend.1 = (bf16[1024,768]{1,0:T(8,128)(2,1)}, bf16[6,2,1024,4096]{3,2,1,0:T(8,128)(2,1)}, f32[6,2,1024,128]{3,2,1,0:T(8,128)}) custom-call(bf16[1024,768]{1,0:T(8,128)(2,1)} %bitcast.65, bf16[4096,1536]{1,0:T(8,128)(2,1)} %bitcast.55, bf16[4096,1536]{1,0:T(8,128)(2,1)} %bitcast.56, bf16[4096,128]{1,0:T(8,128)(2,1)} %select_convert_fusion.extra_ref.refs_7_), custom_call_target="tpu_custom_call" | custom-call | flops 51539607552 | bytes 117964800 | tf_op jit(solution)/shard_map/attend/pallas_call | solution.py:106
  159.1 1.2 pad_maximum_fusion.1.cot_ref
  160.3 3.2 all-gather.9.cloned.1.call-done.down_ref
  163.5 41.4 %middle.1 = (bf16[1024,768]{1,0:T(8,128)(2,1)}, bf16[1024,3072]{1,0:T(8,128)(2,1)}, bf16[1024,768]{1,0:T(8,128)(2,1)}, bf16[1024,768]{1,0:T(8,128)(2,1)}, bf16[1...) custom-call(bf16[1024,768]{1,0:T(8,128)(2,1)} %get-tuple-element.67., ...), custom_call_target="tpu_custom_call" | custom-call | flops 21743271936 | bytes 36175872 | tf_op jit(solution)/shard_map/middle/pallas_call | solution.py:539
  205.0 11.7 %up_grads.1 = (bf16[16,216,768]{2,1,0:T(8,128)(2,1)}, bf16[16,216,768]{2,1,0:T(8,128)(2,1)}) custom-call(bf16[1024,768]{1,0:T(8,128)(2,1)} %get-tuple-element.79.hidden_ref, bf16[1024,3072]{1,0:T(8,128)(2,1)} %get-tuple-element.80.dupper_ref, bf16[1024,768]{1,0:T(8,128)(2,1)} %get-tuple-element.67.mixed_ref, bf16[1024,768]{1,0:T(8,128)(2,1)} %get-tuple-element.81.dattn_ref), custom_call_target="tpu_custom_call" | custom-call | flops 6039797760 | bytes 19267584 | tf_op jit(solution)/shard_map/up_grads/pallas_call | solution.py:628
  216.7 9.2 %down_grads.1 = (bf16[16,216,768]{2,1,0:T(8,128)(2,1)}, bf16[16,216,768]{2,1,0:T(8,128)(2,1)}) custom-call(bf16[1024,3072]{1,0:T(8,128)(2,1)} %get-tuple-element.77.active_ref, bf16[1024,768]{1,0:T(8,128)(2,1)} %get-tuple-element.78.dbranch_ref, bf16[16,216,768]{2,1,0:T(8,128)(2,1)} %get-tuple-element.82.held_keep, ...), custom_call_target="tpu_custom_call", output_to_operand_aliasing={{0}: (2, {}), {1}: (3, {})} | custom-call | flops 4831838208 | bytes 13762560 | tf_op jit(solution)/shard_map/down_grads/pallas_call | solution.py:653
  226.6 31.1 %attend_back.4 = (f32[1024,768]{1,0:T(8,128)}, bf16[2,768,1024]{2,1,0:T(8,128)(2,1)}) custom-call(bf16[1024,768]{1,0:T(8,128)(2,1)} %bitcast.66, bf16[1024,768]{1,0:T(8,128)(2,1)} %get-tuple-element.73.refs_1_, bf16[6,1024,128]{2,1,0:T(8,128)(2,1)} %get-tuple-element.74.refs_2_, f32[6,2,1024,128]{3,2,1,0:T(8,128)} %get-tuple-element.75.refs_3_, ...), custom_call_target="tpu_custom_call" | custom-call | flops 25769803776 | bytes 44040192 | tf_op jit(solution)/shard_map/attend_back/pallas_call | solution.py:196
  257.7 6.6 %convolution_convert_fusion.1 = bf16[1024,768]{1,0:T(8,128)(2,1)} fusion(bf16[1536,1024]{1,0:T(8,128)(2,1)} %bitcast.95, bf16[768,2304]{1,0:T(8,128)(2,1)} %bitcast.80), kind=kOutput, calls=%fused_computation.5 | convolution fusion | flops 2416705536 | bytes 7077888 | tf_op jit(solution)/shard_map/dot_general | solution.py:37
  264.2 3.9 add.124
  270.7 2.1 collective-permute-start.1
  273.6 2.0 compare_select_fusion.2
  275.6 31.2 %attend_back.5 = (f32[1024,768]{1,0:T(8,128)}, bf16[2,768,1024]{2,1,0:T(8,128)(2,1)}) custom-call(bf16[1024,768]{1,0:T(8,128)(2,1)} %bitcast.67, bf16[1024,768]{1,0:T(8,128)(2,1)} %get-tuple-element.73.refs_1_, bf16[6,1024,128]{2,1,0:T(8,128)(2,1)} %get-tuple-element.74.refs_2_, f32[6,2,1024,128]{3,2,1,0:T(8,128)} %get-tuple-element.75.refs_3_, ...), custom_call_target="tpu_custom_call" | custom-call | flops 25769803776 | bytes 44040192 | tf_op jit(solution)/shard_map/attend_back/pallas_call | solution.py:196
  306.8 6.2 %add_convert_fusion.1 = bf16[1024,768]{1,0:T(8,128)(2,1)} fusion(bf16[1024,768]{1,0:T(8,128)(2,1)} %collective-permute-done.3, bf16[1536,1024]{1,0:T(8,128)(2,1)} %bitcast.96, bf16[768,2304]{1,0:T(8,128)(2,1)S(1)} %bitcast.81), kind=kOutput, calls=%fused_computation.1 | convolution fusion | flops 2418278400 | bytes 8650752 | tf_op jit(solution)/shard_map/dot_general | solution.py:37
  313.0 1.3 collective-permute-start.4
  314.3 31.2 %attend_back.6 = (f32[1024,768]{1,0:T(8,128)}, bf16[2,768,1024]{2,1,0:T(8,128)(2,1)}) custom-call(bf16[1024,768]{1,0:T(8,128)(2,1)} %bitcast.68, bf16[1024,768]{1,0:T(8,128)(2,1)} %get-tuple-element.73.refs_1_, bf16[6,1024,128]{2,1,0:T(8,128)(2,1)} %get-tuple-element.74.refs_2_, f32[6,2,1024,128]{3,2,1,0:T(8,128)} %get-tuple-element.75.refs_3_, ...), custom_call_target="tpu_custom_call" | custom-call | flops 25769803776 | bytes 44040192 | tf_op jit(solution)/shard_map/attend_back/pallas_call | solution.py:196
  345.5 5.7 convolution_convert_fusion
  351.3 19.8 %collective-permute-done.4 = bf16[1024,768]{1,0:T(8,128)(2,1)S(1)} collective-permute-done((bf16[1024,768]{1,0:T(8,128)(2,1)}, bf16[1024,768]{1,0:T(8,128)(2,1)S(1)}, u32[]{:S(2)}, u32[]{:S(2)}) %collective-permute-start.4) | collective-permute-done | bytes 1572896 | tf_op jit(solution)/shard_map/ppermute | solution.py:934
  371.0 64.5 %reduce-scatter.2.cloned.1.call-done = bf16[1,216,768]{2,1,0:T(8,128)(2,1)} async-done(((bf16[16,216,768]{2,1,0:T(8,128)(2,1)}), bf16[1,216,768]{2,1,0:T(8,128)(2,1)}) %reduce-scatter.2.cloned.1.call-update) | async-done | bytes 331792 | tf_op jit(solution)/shard_map/reduce_scatter | solution.py:1074
  437.5 1.3 pad_maximum_fusion.2
  438.8 2.7 collective-permute-start.5
  441.5 31.0 %attend_back.7 = (f32[1024,768]{1,0:T(8,128)}, bf16[2,768,1024]{2,1,0:T(8,128)(2,1)}) custom-call(bf16[1024,768]{1,0:T(8,128)(2,1)} %bitcast.69, bf16[1024,768]{1,0:T(8,128)(2,1)} %get-tuple-element.73.refs_1_, bf16[6,1024,128]{2,1,0:T(8,128)(2,1)} %get-tuple-element.74.refs_2_, f32[6,2,1024,128]{3,2,1,0:T(8,128)} %get-tuple-element.75.refs_3_, ...), custom_call_target="tpu_custom_call" | custom-call | flops 25769803776 | bytes 44040192 | tf_op jit(solution)/shard_map/attend_back/pallas_call | solution.py:196
  472.5 3.5 fusion
  476.0 2.7 fusion.2
  480.6 70.4 %closing.1 = (f32[2,96,2304]{2,1,0:T(8,128)}, f32[16,768]{1,0:T(8,128)}, bf16[512,768]{1,0:T(8,128)(2,1)}) custom-call(f32[1024,768]{1,0:T(8,128)} %get-tuple-element.107.dq_ref, bf16[4096,768]{1,0:T(8,128)(2,1)} %bitcast.100, bf16[2,768,1024]{2,1,0:T(8,128)(2,1)} %get-tuple-element.86.refs_0_, bf16[2,768,1024]{2,1,0:T(8,128)(2,1)} %get-tuple-element.92.refs_1_, ...), custom_call_target="tpu_custom_call" | custom-call | flops 48318382080 | bytes 104857600 | tf_op jit(solution)/shard_map/closing/pallas_call | solution.py:863
  552.9 1.6 fusion.14
  554.6 1.6 slice.160
  561.6 1.3 pad_maximum_fusion.3
  564.2 2.9 pad_maximum_fusion
  (124 shorter events, 25.5 us)
Async XLA Ops:
  7.2 67.9 %copy-start = (s32[2,8]{1,0:T(2,128)S(1)}, s32[2,8]{1,0:T(2,128)}, u32[]{:S(2)}) copy-start(s32[2,8]{1,0:T(2,128)} %param.20) | copy-start | bytes 196
  7.2 153.1 %all-gather.5.cloned.1.call-start = ((), (), s32[]{:S(2)}) async-start(), calls=%async_computation.1 | async-start | bytes 1474560 | tf_op jit(solution)/shard_map/all_gather | solution.py:942
  7.9 152.4 %all-gather.7.cloned.1.call-start = ((), (), s32[]{:S(2)}) async-start(), calls=%async_computation.2 | async-start | bytes 5898240 | tf_op jit(solution)/shard_map/all_gather | solution.py:942
  8.7 154.9 %all-gather.9.cloned.1.call-start = ((), (), s32[]{:S(2)}) async-start(), calls=%async_computation.3 | async-start | bytes 5898240 | tf_op jit(solution)/shard_map/all_gather | solution.py:942
  11.0 61.5 %copy-start.7 = (bf16[2,512,768]{2,1,0:T(8,128)(2,1)S(1)}, bf16[2,512,768]{2,1,0:T(8,128)(2,1)}, u32[]{:S(2)}) copy-start(bf16[2,512,768]{2,1,0:T(8,128)(2,1)} %param.18) | copy-start | bytes 4718596
  72.5 2.8 copy-start.18
  72.7 86.4 %collective-permute-start = (bf16[512,768]{1,0:T(8,128)(2,1)S(1)}, bf16[512,768]{1,0:T(8,128)(2,1)S(1)}, u32[]{:S(2)}, u32[]{:S(2)}) collective-permute-start(bf16[512,768]{1,0:T(8,128)(2,1)S(1)} %get-tuple-element.130), channel_id=1, source_target_pairs={{0,4},{1,5},{2,6},{3,7},{4,0},{5,1},{6,2},{7,3},{8,12},{9,13},{10,... | collective-permute-start | bytes 2359304 | tf_op jit(solution)/shard_map/ppermute | solution.py:934
  75.0 360.6 %reduce-scatter.2.cloned.1.call-start = ((), (), s32[]{:S(2)}) async-start(), calls=%async_computation.4 | async-start | bytes 5640192 | tf_op jit(solution)/shard_map/reduce_scatter | solution.py:1074
  78.4 76.9 %copy-start.12 = (bf16[4,12,192]{2,1,0:T(8,128)(2,1)S(1)}, bf16[4,12,192]{2,1,0:T(8,128)(2,1)}, u32[]{:S(2)}) copy-start(bf16[4,12,192]{2,1,0:T(8,128)(2,1)} %get-tuple-element.70) | copy-start | bytes 55300
  158.4 46.5 %copy-start.13 = (f32[2,768]{1,0:T(2,128)}, f32[2,768]{1,0:T(2,128)S(1)}, u32[]{:S(2)}) copy-start(f32[2,768]{1,0:T(2,128)S(1)} %broadcast.239) | copy-start | bytes 18436
  225.9 38.3 %collective-permute-start.2 = (bf16[16,216,768]{2,1,0:T(8,128)(2,1)}, bf16[16,216,768]{2,1,0:T(8,128)(2,1)S(1)}, u32[]{:S(2)}, u32[]{:S(2)}) collective-permute-start(bf16[16,216,768]{2,1,0:T(8,128)(2,1)} %get-tuple-element.85), channel_id=1, source_target_pairs={{0,1},{1,0},{2,3},{3,2},{4,5},{5,4},{6,7},{7,6},{8,9},{9,8},{10,11... | collective-permute-start | bytes 15925256 | tf_op jit(solution)/shard_map/ppermute | solution.py:934
  257.6 6.6 %slice-start = ((s8[5308416]{0:T(1024)(128)(4,1)}), s8[4194304]{0:T(1024)(128)(4,1)S(1)}, s32[]{:S(2)}) async-start(s8[5308416]{0:T(1024)(128)(4,1)} %bitcast.70), calls=%async_computation.6 | async-start | bytes 8388608
  257.7 6.6 %slice-start.1 = ((s8[5308416]{0:T(1024)(128)(4,1)}), s8[1114112]{0:T(1024)(128)(4,1)S(1)}, s32[]{:S(2)}) async-start(s8[5308416]{0:T(1024)(128)(4,1)} %bitcast.70), calls=%async_computation.7 | async-start | bytes 2228224
  268.2 1.6 copy-start.15
  268.2 1.7 copy-start.8
  268.2 211.5 %all-gather.11.cloned.1.call-start = ((), (), s32[]{:S(2)}) async-start(), calls=%async_computation.5 | async-start | bytes 2985984 | tf_op jit(solution)/shard_map/all_gather | solution.py:1048
  268.8 38.0 %collective-permute-start.3 = (bf16[1024,768]{1,0:T(8,128)(2,1)}, bf16[1024,768]{1,0:T(8,128)(2,1)}, u32[]{:S(2)}, u32[]{:S(2)}) collective-permute-start(bf16[1024,768]{1,0:T(8,128)(2,1)} %convolution_convert_fusion.1), channel_id=1, source_target_pairs={{0,1},{1,0},{2,3},{3,2},{4,5},{5,4},{6,7},{7,6},{8,9},{9,8},{10,11... | collective-permute-start | bytes 4718600 | tf_op jit(solution)/shard_map/ppermute | solution.py:934
  270.7 165.5 %collective-permute-start.1 = (bf16[512,768]{1,0:T(8,128)(2,1)}, bf16[512,768]{1,0:T(8,128)(2,1)}, u32[]{:S(2)}, u32[]{:S(2)}) collective-permute-start(bf16[512,768]{1,0:T(8,128)(2,1)} %slice.118), channel_id=1, source_target_pairs={{0,4},{1,5},{2,6},{3,7},{4,0},{5,1},{6,2},{7,3},{8,12},{9,13},{10,... | collective-permute-start | bytes 2359304 | tf_op jit(solution)/shard_map/ppermute | solution.py:934
  275.5 31.2 %copy-start.10 = (bf16[4,192,2304]{2,1,0:T(8,128)(2,1)S(1)}, bf16[4,192,2304]{2,1,0:T(8,128)(2,1)}, u32[]{:S(2)}) copy-start(bf16[4,192,2304]{2,1,0:T(8,128)(2,1)} %get-tuple-element.87) | copy-start | bytes 10616836
  313.0 58.0 %collective-permute-start.4 = (bf16[1024,768]{1,0:T(8,128)(2,1)}, bf16[1024,768]{1,0:T(8,128)(2,1)S(1)}, u32[]{:S(2)}, u32[]{:S(2)}) collective-permute-start(bf16[1024,768]{1,0:T(8,128)(2,1)} %add_convert_fusion.1), channel_id=1, source_target_pairs={{0,2},{1,3},{2,0},{3,1},{4,6},{5,7},{6,4},{7,5},{8,10},{9,11},{10,... | collective-permute-start | bytes 4718600 | tf_op jit(solution)/shard_map/ppermute | solution.py:934
  345.5 90.1 %copy-start.14 = (f32[2,768]{1,0:T(2,128)S(1)}, f32[2,768]{1,0:T(2,128)}, u32[]{:S(2)}) copy-start(f32[2,768]{1,0:T(2,128)} %copy-done.13) | copy-start | bytes 18436
  438.8 33.7 %copy-start.11 = (bf16[4,192,2304]{2,1,0:T(8,128)(2,1)S(1)}, bf16[4,192,2304]{2,1,0:T(8,128)(2,1)}, u32[]{:S(2)}) copy-start(bf16[4,192,2304]{2,1,0:T(8,128)(2,1)} %get-tuple-element.87) | copy-start | bytes 10616836
  438.8 39.9 %collective-permute-start.5 = (bf16[1024,768]{1,0:T(8,128)(2,1)}, bf16[1024,768]{1,0:T(8,128)(2,1)S(1)}, u32[]{:S(2)}, u32[]{:S(2)}) collective-permute-start(bf16[1024,768]{1,0:T(8,128)(2,1)} %convolution_convert_fusion), channel_id=1, source_target_pairs={{0,1},{1,0},{2,3},{3,2},{4,5},{5,4},{6,7},{7,6},{8,9},{9,8},{10,11... | collective-permute-start | bytes 4718600 | tf_op jit(solution)/shard_map/ppermute | solution.py:934
  472.5 3.5 copy-start.17
  476.0 2.7 copy-start.3
  480.6 72.3 %copy-start.2 = (bf16[8,216,768]{2,1,0:T(8,128)(2,1)S(1)}, bf16[8,216,768]{2,1,0:T(8,128)(2,1)}, u32[]{:S(2)}) copy-start(bf16[8,216,768]{2,1,0:T(8,128)(2,1)} %all-gather.11.cloned.1.call-done) | copy-start | bytes 7962628
  554.6 1.6 copy-start.9
  556.2 7.4 %copy-start.16 = (f32[2]{0:T(128)S(1)}, f32[2]{0:T(128)}, u32[]{:S(2)}) copy-start(f32[2]{0:T(128)} %convert_multiply_fusion) | copy-start | bytes 28
  556.3 7.9 %copy-start.4 = (f32[8,24,768]{2,1,0:T(8,128)S(1)}, f32[8,24,768]{2,1,0:T(8,128)}, u32[]{:S(2)}) copy-start(f32[8,24,768]{2,1,0:T(8,128)} %get-tuple-element.120) | copy-start | bytes 1769476
  556.3 7.9 %copy-start.5 = (f32[8,24,768]{2,1,0:T(8,128)S(1)}, f32[8,24,768]{2,1,0:T(8,128)}, u32[]{:S(2)}) copy-start(f32[8,24,768]{2,1,0:T(8,128)} %get-tuple-element.121) | copy-start | bytes 1769476
  562.9 4.3 copy-start.6
  564.2 4.1 copy-start.1
Sparse Core Ops, SparseCore 0:
  9.9 36.7 all-gather.4
  48.5 56.0 all-gather.6
  106.4 57.0 all-gather.8
  268.3 167.2 reduce-scatter.1
  437.1 35.5 all-gather.10

commit v6 on v4

--- a/solution.py
+++ b/solution.py
@@ -658,13 +658,25 @@
     )(active, dbranch, held)
 
 
-def closing_kernel(owners, ring, firsts, dq_ref, x_ref, *refs):
-    shares = refs[: len(firsts)]
-    small_ref, home_ref, out_ref, small_out_ref, home_out_ref = refs[len(firsts) : len(firsts) + 5]
+def closing_kernel(
+    owners,
+    ring,
+    dq_ref,
+    x_ref,
+    share_ref,
+    sum_ref,
+    small_ref,
+    home_ref,
+    out_ref,
+    small_out_ref,
+    home_out_ref,
+    *refs,
+):
     (
         xs,
         dq,
         dkv,
+        before,
         whole,
         parts,
         in_core,
@@ -681,18 +693,17 @@
         load_sem,
         send_sem,
         recv_sem,
-    ) = refs[len(firsts) + 5 :]
+    ) = refs
     row, here = (lax.axis_index("dp"), lax.axis_index("ctx"))
     core, depth = (lax.rem(here, 2), here // 2)
     deep = ring // 2
     count = dq.shape[0]
     loads = [
         pltpu.make_async_copy(dq_ref, dq, load_sem.at[0]),
-        pltpu.make_async_copy(x_ref, xs, load_sem.at[1]),
+        pltpu.make_async_copy(x_ref.at[pl.ds(0, count)], xs, load_sem.at[1]),
+        pltpu.make_async_copy(share_ref, dkv, load_sem.at[2]),
+        pltpu.make_async_copy(sum_ref, before, load_sem.at[3]),
     ]
-    for i, first in enumerate(firsts):
-        columns = pl.ds(first, shares[i].shape[2])
-        loads.append(pltpu.make_async_copy(shares[i], dkv.at[:, :, columns], load_sem.at[2 + i]))
     for load in loads:
         load.start()
 
@@ -724,14 +735,16 @@
     at_done = at_piece + deep - 1
     at_back = at_done + deep - 1
     tile = 256
+    out_width = whole.shape[1]
 
     def to_core(m):
         def one(t, carry):
             columns = pl.ds(pl.multiple_of(t * tile, tile), tile)
             if m == 0:
-                whole[columns, :] = dot(xs[0:count, columns], dq[...].astype(bf16), 0, 0)
+                whole[columns, :] = dot(xs[:, columns], dq[...].astype(bf16), 0, 0)
             else:
-                whole[columns, :] = dot(xs[:, columns], dkv[m - 1], 0, 1)
+                held = before[columns, (m - 1) * out_width : m * out_width]
+                whole[columns, :] = held + dot(xs[:, columns], dkv[m - 1], 0, 1)
             return carry
 
         lax.fori_loop(0, whole.shape[0] // tile, one, 0)
@@ -802,7 +815,7 @@
             for load in loads[2:]:
                 load.wait()
             ones = jnp.ones((8, dkv.shape[2]), bf16)
-            small[1:2, :] = dot(ones, dkv[1], 1, 1)[0:1, :]
+            small[1:2, :] += dot(ones, dkv[1], 1, 1)[0:1, :]
             small_waits = [send(small, small_core, mate, 3, 0)]
         if step == 1:
             small_waits[0].wait_recv()
@@ -832,11 +845,8 @@
         copy.wait_send()
 
 
-def closing(dq, stream, shares, small, home, owners, ring):
+def closing(dq, stream, share, kv_sum, small, home, owners, ring):
     count, width = dq.shape
-    keys = stream.shape[0]
-    firsts = tuple(first for first, _ in shares)
-    shares = [v for _, v in shares]
     deep = ring // 2
     half = width // owners // 2
     piece = half // deep
@@ -844,8 +854,8 @@
     any_space = pl.BlockSpec(memory_space=pl.ANY)
     in_vmem = pl.BlockSpec(memory_space=pltpu.VMEM)
     return pl.pallas_call(
-        functools.partial(closing_kernel, owners, ring, firsts),
-        in_specs=[any_space] * (2 + len(shares)) + [in_vmem, any_space],
+        functools.partial(closing_kernel, owners, ring),
+        in_specs=[any_space] * 4 + [in_vmem, any_space],
         out_specs=[in_vmem, in_vmem, any_space],
         out_shape=[
             jax.ShapeDtypeStruct((2, half, 3 * width), f32),
@@ -853,9 +863,10 @@
             jax.ShapeDtypeStruct(home.shape, home.dtype),
         ],
         scratch_shapes=[
-            pltpu.VMEM((keys, width), bf16),
+            pltpu.VMEM((count, width), bf16),
             pltpu.VMEM((count, width), f32),
-            pltpu.VMEM((2, width, keys), bf16),
+            pltpu.VMEM(share.shape, bf16),
+            pltpu.VMEM(kv_sum.shape, f32),
             pltpu.VMEM((width, width), f32),
             pltpu.VMEM((3, owners, 2, half, width), bf16),
             pltpu.VMEM((3, owners, half, width), bf16),
@@ -869,7 +880,7 @@
             pltpu.VMEM(small.shape, f32),
             pltpu.VMEM((owners,) + small.shape, f32),
             pltpu.VMEM((deep,) + small.shape, f32),
-            pltpu.SemaphoreType.DMA((2 + len(shares),)),
+            pltpu.SemaphoreType.DMA((4,)),
             pltpu.SemaphoreType.DMA((4, slots)),
             pltpu.SemaphoreType.DMA((4, slots)),
         ],
@@ -877,10 +888,10 @@
             vmem_limit_bytes=vmem_grant, collective_id=0, has_side_effects=True
         ),
         cost_estimate=pl.CostEstimate(
-            flops=20 * keys * width * width, bytes_accessed=100 << 20, transcendentals=0
+            flops=6 * count * width * width, bytes_accessed=100 << 20, transcendentals=0
         ),
         name="closing",
-    )(dq, stream, *shares, small, home)
+    )(dq, stream, share, kv_sum, small, home)
 
 
 def shards(
@@ -959,7 +970,12 @@
         ffn_gain,
         ffn_shift,
     ]
-    packed = jnp.concatenate([jnp.stack(singles), up_bias.reshape(-1, share)], axis=0)
+    ups = up_bias.reshape(-1, share)
+    count_vectors = len(singles) + ups.shape[0]
+    which = lax.broadcasted_iota(jnp.int32, (count_vectors, share), 0)
+    packed = jnp.pad(ups, ((len(singles), 0), (0, 0)))
+    for i, v in enumerate(singles):
+        packed = jnp.where(which == i, v[None, :], packed)
     if laid:
         stream, qkv_all, vectors, queries, both = opening(
             tokens, qkv_weight, packed, owners, ring
@@ -1033,6 +1049,7 @@
         grads = (dot(hidden, grad_upper, 0, 0), dot(active, grad_branch, 0, 0), dot(mixed, grad_attn, 0, 0))
         scattered = tuple(scatter(grad.astype(bf16)) for grad in grads)
     gathered = []
+    kv_sums = []
 
     kv_weight = qkv_all[:, width:]
     size = 2 * block
@@ -1044,7 +1061,15 @@
         if level == len(bits):
             first = place * size
             if place == 0:
-                held, grad_queries = lax.optimization_barrier((scattered, grad_queries))
+                weight, vector = (0.0, 0.0)
+                for start, v in shares:
+                    v = v.reshape(2 * width, size)
+                    weight = weight + dot(stream[start : start + size], v, 0, 1)
+                    vector = vector + jnp.sum(v[width:], axis=1, dtype=f32)
+                held, weight, vector, grad_queries = lax.optimization_barrier(
+                    (scattered, weight, vector, grad_queries)
+                )
+                kv_sums.extend([weight, vector])
                 gathered.append(spread(held))
             grad_queries, grad_both = attend_back(
                 queries,
@@ -1064,7 +1089,14 @@
         low = reduced(place + (1 << level), level + 1).astype(bf16)
         low, grad_queries = lax.optimization_barrier((low, grad_queries))
         other = exchange(low, bits[level])
-        return reduced(place, level + 1) + other.astype(f32)
+        if level + 1 == len(bits):
+            return reduced(place, level + 1) + other.astype(f32)
+        if level + 2 < len(bits):
+            return reduced(place, level + 1) + other.astype(f32)
+        low = reduced(place + (1 << (level + 1)), level + 2).astype(bf16)
+        low, other, grad_queries = lax.optimization_barrier((low, other, grad_queries))
+        mate = exchange(low, bits[level + 1])
+        return reduced(place, level + 2) + mate.astype(f32) + other.astype(f32)
 
     grad_stream = reduced(0, 0)
     grad_query_low = grad_queries.astype(bf16)
@@ -1094,28 +1126,39 @@
         lane % 3 == 0, squares[0], jnp.where(lane % 3 == 1, squares[1], squares[2])
     )
     squares = jnp.where(mine, squares, 0.0)[None, :]
+    kv_weight_sum, value_sum = kv_sums
+    last_share = shares[-1][1]
     small = jnp.concatenate(
-        [jnp.zeros((2, width), f32), sums[:6], squares, up_sum[0].reshape(-1, width)], axis=0
+        [
+            jnp.zeros((1, width), f32),
+            value_sum[None, :],
+            sums[:6],
+            squares,
+            up_sum[0].reshape(-1, width),
+        ],
+        axis=0,
     )
     small = jnp.pad(small, ((0, -small.shape[0] % 8), (0, 0)))
     if laid:
         grad_qkv_weight, summed, other = closing(
-            grad_queries, stream, shares, small, grad_rows_low[block:], owners, ring
+            grad_queries,
+            stream,
+            last_share,
+            kv_weight_sum,
+            small,
+            grad_rows_low[block:],
+            owners,
+            ring,
         )
         grad_qkv_weight = grad_qkv_weight.reshape(share, 3 * width)
     else:
         other = exchange(grad_rows_low[block:], half)
-        kv_parts = []
-        for which in range(2):
-            part = 0.0
-            for first, v in shares:
-                part = part + dot(stream[first : first + size], v[which], 0, 1)
-            kv_parts.append(part)
-        grad_qkv_weight = jnp.concatenate([dot(rows, grad_query_low, 0, 0)] + kv_parts, axis=1)
+        kv_weight_sum = kv_weight_sum + dot(rows, last_share.reshape(2 * width, size), 0, 1)
+        grad_qkv_weight = jnp.concatenate([dot(rows, grad_query_low, 0, 0), kv_weight_sum], axis=1)
         grad_qkv_weight = spread(scatter(grad_qkv_weight.astype(bf16))).astype(f32)
         grad_query_bias = jnp.sum(grad_query_low, axis=0, dtype=f32)
-        grad_value_bias = sum(jnp.sum(v[1], axis=1, dtype=f32) for _, v in shares)
-        small = jnp.concatenate([grad_query_bias[None], grad_value_bias[None], small[2:]], axis=0)
+        value_sum = value_sum + jnp.sum(last_share[1], axis=1, dtype=f32)
+        small = jnp.concatenate([grad_query_bias[None], value_sum[None], small[2:]], axis=0)
         summed = lax.psum(small, ("dp", "ctx"))
 
     grad_tokens = arrange(grad_rows_low[:block], other)

time: 532 us -> 532 us (level)
  waiting for transfers between devices: 38 us -> 16.5 us
  matrix products: 24.2 us -> 39.1 us
  other arithmetic: 15.4 us -> 22.5 us
    reduce_scatter x1, waiting for transfers between devices: 20.9 us -> 0.01 us  [scatter(): lax.psum_scatter(grad, ('dp', 'ctx'), scatter_dimension=0, tiled=True)]
    dot_general x5 -> x8, matrix products: 24.2 us -> 39.1 us  [dot(): lax.dot_general(left, right, (((left_dim,), (right_dim,)), ((), ())), pre...]
  transfers between devices with their start and end apart: 10 -> 10, of which waited for: 3 -> 2; matrix products, arithmetic and copies ran while one was open for 9% -> 13% of each run, Pallas kernels for 50% -> 50%
where the time goes in v6:
time: 532 us; the launch traced here: 522 us
  Pallas kernels  395 us (74%)
  matrix products  39.1 us (7%)
  local copies, waits for them, and re-layouts  27.6 us (5%)
  other arithmetic  22.5 us (4%)
  waiting for transfers between devices  16.5 us (3%)
  between operations  14.4 us (3%)
  starting transfers between devices  7.26 us (1%)
    pallas_call x4, Pallas kernels, attend_back(): pl.pallas_call(functools.partial(attend_back_kernel, scale, head_dim, row...  125 us
    pallas_call x1, Pallas kernels, attend(): pl.pallas_call(functools.partial(attend_kernel, scale, head_dim, step), g...  76.9 us
    pallas_call x1, Pallas kernels, closing(): pl.pallas_call(functools.partial(closing_kernel, owners, ring), in_specs=...  68.9 us
    pallas_call x1, Pallas kernels, opening(): pl.pallas_call(functools.partial(opening_kernel, owners, ring, pieces), i...  61.5 us
    pallas_call x1, Pallas kernels, middle(): pl.pallas_call(functools.partial(middle_kernel, head_dim, chunk), grid=(c...  41.6 us
    dot_general x8, matrix products, dot(): lax.dot_general(left, right, (((left_dim,), (right_dim,)), ((), ())), pre...  39.1 us
    ppermute x5, waiting for transfers between devices, exchange(): return lax.ppermute(array, 'ctx', [(i, i ^ bit) for i in range(ring)])  11.9 us
    pallas_call x1, Pallas kernels, middle_grads(): pl.pallas_call(functools.partial(up_out_kernel, blocks), grid=(blocks + 1...  11.7 us
  transfers between devices with their start and end apart: 10, of which 2 were waited for; matrix products, arithmetic and copies ran while one was open for 13% of the time, Pallas kernels for 50%

profile of v6, /device:TPU:1, one launch (start us, length us, event | category | flops | bytes accessed | tf_op | source)
XLA Modules:
  0.0 522.4 jit_solution(10464163676487663748)
XLA Ops:
  11.0 61.5 %opening.1 = (bf16[8,512,768]{2,1,0:T(8,128)(2,1)}, bf16[4,192,2304]{2,1,0:T(8,128)(2,1)}, bf16[4,12,192]{2,1,0:T(8,128)(2,1)}, bf16[2,512,768]{2,1,0:T(8,128)(2,1)}, bf16[8,512,1536]{2,1,0:T(8,128)(2,1)}) custom-call(bf16[2,512,768]{2,1,0:T(8,128)(2,1)} %tokens_ref.1, bf16[192,2304]{1,0:T(8,128)(2,1)} %weight_ref.1, ...), custom_call_target="tpu_custom_call" | custom-call | flops 19327352832 | bytes 209715200 | tf_op jit(solution)/shard_map/opening/pallas_call | solution.py:404
  72.7 2.3 collective-permute-start
  76.9 1.6 select_convert_fusion.extra_ref.refs_7_
  78.5 76.9 %attend.1 = (bf16[1024,768]{1,0:T(8,128)(2,1)}, bf16[6,2,1024,4096]{3,2,1,0:T(8,128)(2,1)}, f32[6,2,1024,128]{3,2,1,0:T(8,128)}) custom-call(bf16[1024,768]{1,0:T(8,128)(2,1)} %bitcast.74, bf16[4096,1536]{1,0:T(8,128)(2,1)} %bitcast.64, bf16[4096,1536]{1,0:T(8,128)(2,1)} %bitcast.65, bf16[4096,128]{1,0:T(8,128)(2,1)} %select_convert_fusion.extra_ref.refs_7_), custom_call_target="tpu_custom_call" | custom-call | flops 51539607552 | bytes 117964800 | tf_op jit(solution)/shard_map/attend/pallas_call | solution.py:106
  160.4 3.2 all-gather.9.cloned.1.call-done.down_ref
  163.5 41.6 %middle.1 = (bf16[1024,768]{1,0:T(8,128)(2,1)}, bf16[1024,3072]{1,0:T(8,128)(2,1)}, bf16[1024,768]{1,0:T(8,128)(2,1)}, bf16[1024,768]{1,0:T(8,128)(2,1)}, bf16[1...) custom-call(bf16[1024,768]{1,0:T(8,128)(2,1)} %get-tuple-element.63., ...), custom_call_target="tpu_custom_call" | custom-call | flops 21743271936 | bytes 36175872 | tf_op jit(solution)/shard_map/middle/pallas_call | solution.py:539
  205.1 11.7 %up_grads.1.held_ref = bf16[32,216,768]{2,1,0:T(8,128)(2,1)} custom-call(bf16[1024,768]{1,0:T(8,128)(2,1)} %get-tuple-element.75.hidden_ref, bf16[1024,3072]{1,0:T(8,128)(2,1)} %get-tuple-element.76.dupper_ref, bf16[1024,768]{1,0:T(8,128)(2,1)} %get-tuple-element.63.mixed_ref, bf16[1024,768]{1,0:T(8,128)(2,1)} %get-tuple-element.77.dattn_ref), custom_call_target="tpu_custom_call" | custom-call | flops 6039797760 | bytes 19267584 | tf_op jit(solution)/shard_map/up_grads/pallas_call | solution.py:618
  216.8 9.2 %down_grads.1 = bf16[32,216,768]{2,1,0:T(8,128)(2,1)} custom-call(bf16[1024,3072]{1,0:T(8,128)(2,1)} %get-tuple-element.73.active_ref, bf16[1024,768]{1,0:T(8,128)(2,1)} %get-tuple-element.74.dbranch_ref, bf16[32,216,768]{2,1,0:T(8,128)(2,1)} %up_grads.1.held_ref), custom_call_target="tpu_custom_call", output_to_operand_aliasing={{}: (2, {})} | custom-call | flops 4831838208 | bytes 13762560 | tf_op jit(solution)/shard_map/down_grads/pallas_call | solution.py:640
  226.6 3.8 fusion.14
  232.6 2.1 slice.148
  234.7 2.1 collective-permute-start.1
  236.8 31.3 %attend_back.4 = (f32[1024,768]{1,0:T(8,128)}, bf16[2,768,1024]{2,1,0:T(8,128)(2,1)}) custom-call(bf16[1024,768]{1,0:T(8,128)(2,1)} %bitcast.75, bf16[1024,768]{1,0:T(8,128)(2,1)} %get-tuple-element.69.refs_1_, bf16[6,1024,128]{2,1,0:T(8,128)(2,1)} %get-tuple-element.70.refs_2_, f32[6,2,1024,128]{3,2,1,0:T(8,128)} %get-tuple-element.71.refs_3_, ...), custom_call_target="tpu_custom_call" | custom-call | flops 25769803776 | bytes 44040192 | tf_op jit(solution)/shard_map/attend_back/pallas_call | solution.py:196
  268.0 6.7 %convolution_convert_fusion.1 = bf16[1024,768]{1,0:T(8,128)(2,1)} fusion(bf16[1536,1024]{1,0:T(8,128)(2,1)} %bitcast.91, bf16[768,2304]{1,0:T(8,128)(2,1)} %bitcast.99), kind=kOutput, calls=%fused_computation.9 | convolution fusion | flops 2416705536 | bytes 7077888 | tf_op jit(solution)/shard_map/dot_general | solution.py:37
  276.1 31.2 %attend_back.5 = (f32[1024,768]{1,0:T(8,128)}, bf16[2,768,1024]{2,1,0:T(8,128)(2,1)}) custom-call(bf16[1024,768]{1,0:T(8,128)(2,1)} %bitcast.76, bf16[1024,768]{1,0:T(8,128)(2,1)} %get-tuple-element.69.refs_1_, bf16[6,1024,128]{2,1,0:T(8,128)(2,1)} %get-tuple-element.70.refs_2_, f32[6,2,1024,128]{3,2,1,0:T(8,128)} %get-tuple-element.71.refs_3_, ...), custom_call_target="tpu_custom_call" | custom-call | flops 25769803776 | bytes 44040192 | tf_op jit(solution)/shard_map/attend_back/pallas_call | solution.py:196
  307.9 1.8 convert_reduce_fusion.1
  309.8 4.8 fusion.18
  314.6 4.3 fusion.19
  318.9 5.0 add_convert_fusion.1
  324.9 31.4 %attend_back.6 = (f32[1024,768]{1,0:T(8,128)}, bf16[2,768,1024]{2,1,0:T(8,128)(2,1)}) custom-call(bf16[1024,768]{1,0:T(8,128)(2,1)} %bitcast.77, bf16[1024,768]{1,0:T(8,128)(2,1)} %get-tuple-element.69.refs_1_, bf16[6,1024,128]{2,1,0:T(8,128)(2,1)} %get-tuple-element.70.refs_2_, f32[6,2,1024,128]{3,2,1,0:T(8,128)} %get-tuple-element.71.refs_3_, ...), custom_call_target="tpu_custom_call" | custom-call | flops 25769803776 | bytes 44040192 | tf_op jit(solution)/shard_map/attend_back/pallas_call | solution.py:196
  356.3 1.7 convert_reduce_fusion
  358.0 8.0 %add_add_fusion.sum_ref = f32[768,1536]{1,0:T(8,128)} fusion(f32[768,1536]{1,0:T(8,128)} %fusion.18, f32[768,1536]{1,0:T(8,128)} %fusion.19, bf16[1024,768]{1,0:T(8,128)(2,1)S(1)} %bitcast.88, bf16[1536,1024]{1,0:T(8,128)(2,1)} %bitcast.95), kind=kOutput, calls=%fused_computation | convolution fusion | flops 2418278400 | bytes 18874368 | tf_op jit(solution)/shard_map/dot_general | solution.py:37
  366.0 3.8 convolution_convert_fusion
  369.9 11.9 %collective-permute-done.3 = bf16[1024,768]{1,0:T(8,128)(2,1)S(1)} collective-permute-done((bf16[1024,768]{1,0:T(8,128)(2,1)}, bf16[1024,768]{1,0:T(8,128)(2,1)S(1)}, u32[]{:S(2)}, u32[]{:S(2)}) %collective-permute-start.3) | collective-permute-done | bytes 1572896 | tf_op jit(solution)/shard_map/ppermute | solution.py:928
  381.8 2.0 compare_select_fusion.2
  387.0 31.3 %attend_back.7 = (f32[1024,768]{1,0:T(8,128)}, bf16[2,768,1024]{2,1,0:T(8,128)(2,1)}) custom-call(bf16[1024,768]{1,0:T(8,128)(2,1)} %bitcast.78, bf16[1024,768]{1,0:T(8,128)(2,1)} %get-tuple-element.69.refs_1_, bf16[6,1024,128]{2,1,0:T(8,128)(2,1)} %get-tuple-element.70.refs_2_, f32[6,2,1024,128]{3,2,1,0:T(8,128)} %get-tuple-element.71.refs_3_, ...), custom_call_target="tpu_custom_call" | custom-call | flops 25769803776 | bytes 44040192 | tf_op jit(solution)/shard_map/attend_back/pallas_call | solution.py:196
  419.0 3.8 fusion
  423.3 2.7 fusion.2
  426.0 2.4 add_convert_fusion
  429.3 68.9 %closing.1 = (f32[2,96,2304]{2,1,0:T(8,128)}, f32[16,768]{1,0:T(8,128)}, bf16[512,768]{1,0:T(8,128)(2,1)}) custom-call(f32[1024,768]{1,0:T(8,128)} %get-tuple-element.97.dq_ref, bf16[4096,768]{1,0:T(8,128)(2,1)} %bitcast.80, bf16[2,768,1024]{2,1,0:T(8,128)(2,1)} %get-tuple-element.92.share_ref, f32[768,1536]{1,0:T(8,128)} %add_add_fusion.sum_ref, ...), custom_call_target="tpu_custom_call" | custom-call | flops 3623878656 | bytes 104857600 | tf_op jit(solution)/shard_map/closing/pallas_call | solution.py:856
  500.3 1.6 slice.199
  501.9 1.6 fusion.15
  511.5 2.9 pad_maximum_fusion
  (135 shorter events, 32.9 us)
Async XLA Ops:
  7.2 68.7 %copy-start = (s32[2,8]{1,0:T(2,128)S(1)}, s32[2,8]{1,0:T(2,128)}, u32[]{:S(2)}) copy-start(s32[2,8]{1,0:T(2,128)} %param.20) | copy-start | bytes 196
  7.2 153.2 %all-gather.5.cloned.1.call-start = ((), (), s32[]{:S(2)}) async-start(), calls=%async_computation.1 | async-start | bytes 1474560 | tf_op jit(solution)/shard_map/all_gather | solution.py:936
  7.9 152.4 %all-gather.7.cloned.1.call-start = ((), (), s32[]{:S(2)}) async-start(), calls=%async_computation.2 | async-start | bytes 5898240 | tf_op jit(solution)/shard_map/all_gather | solution.py:936
  8.7 154.9 %all-gather.9.cloned.1.call-start = ((), (), s32[]{:S(2)}) async-start(), calls=%async_computation.3 | async-start | bytes 5898240 | tf_op jit(solution)/shard_map/all_gather | solution.py:936
  11.0 61.6 %copy-start.9 = (bf16[2,512,768]{2,1,0:T(8,128)(2,1)S(1)}, bf16[2,512,768]{2,1,0:T(8,128)(2,1)}, u32[]{:S(2)}) copy-start(bf16[2,512,768]{2,1,0:T(8,128)(2,1)} %param.18) | copy-start | bytes 4718596
  72.6 2.5 copy-start.22
  72.7 86.4 %collective-permute-start = (bf16[512,768]{1,0:T(8,128)(2,1)S(1)}, bf16[512,768]{1,0:T(8,128)(2,1)S(1)}, u32[]{:S(2)}, u32[]{:S(2)}) collective-permute-start(bf16[512,768]{1,0:T(8,128)(2,1)S(1)} %get-tuple-element.125), channel_id=1, source_target_pairs={{0,4},{1,5},{2,6},{3,7},{4,0},{5,1},{6,2},{7,3},{8,12},{9,13},{10,... | collective-permute-start | bytes 2359304 | tf_op jit(solution)/shard_map/ppermute | solution.py:928
  75.0 306.7 %reduce-scatter.2.cloned.1.call-start = ((), (), s32[]{:S(2)}) async-start(), calls=%async_computation.4 | async-start | bytes 10948608 | tf_op jit(solution)/shard_map/reduce_scatter | solution.py:1039
  78.5 76.9 %copy-start.18 = (bf16[4,12,192]{2,1,0:T(8,128)(2,1)S(1)}, bf16[4,12,192]{2,1,0:T(8,128)(2,1)}, u32[]{:S(2)}) copy-start(bf16[4,12,192]{2,1,0:T(8,128)(2,1)} %get-tuple-element.66) | copy-start | bytes 55300
  226.0 202.4 %all-gather.11.cloned.1.call-start = ((), (), s32[]{:S(2)}) async-start(), calls=%async_computation.5 | async-start | bytes 2985984 | tf_op jit(solution)/shard_map/all_gather | solution.py:1042
  226.6 3.8 copy-start.20
  234.7 149.1 %collective-permute-start.1 = (bf16[512,768]{1,0:T(8,128)(2,1)}, bf16[512,768]{1,0:T(8,128)(2,1)}, u32[]{:S(2)}, u32[]{:S(2)}) collective-permute-start(bf16[512,768]{1,0:T(8,128)(2,1)} %slice.148), channel_id=1, source_target_pairs={{0,4},{1,5},{2,6},{3,7},{4,0},{5,1},{6,2},{7,3},{8,12},{9,13},{10,... | collective-permute-start | bytes 2359304 | tf_op jit(solution)/shard_map/ppermute | solution.py:928
  268.0 7.8 %copy-start.11 = (bf16[2,768,1024]{2,1,0:T(8,128)(2,1)S(1)}, bf16[2,768,1024]{2,1,0:T(8,128)(2,1)}, u32[]{:S(2)}) copy-start(bf16[2,768,1024]{2,1,0:T(8,128)(2,1)} %get-tuple-element.78) | copy-start | bytes 9437188
  274.7 44.2 %collective-permute-start.2 = (bf16[1024,768]{1,0:T(8,128)(2,1)}, bf16[1024,768]{1,0:T(8,128)(2,1)}, u32[]{:S(2)}, u32[]{:S(2)}) collective-permute-start(bf16[1024,768]{1,0:T(8,128)(2,1)} %convolution_convert_fusion.1), channel_id=1, source_target_pairs={{0,1},{1,0},{2,3},{3,2},{4,5},{5,4},{6,7},{7,6},{8,9},{9,8},{10,11... | collective-permute-start | bytes 4718600 | tf_op jit(solution)/shard_map/ppermute | solution.py:928
  276.1 33.6 %copy-start.8 = (bf16[2,512,768]{2,1,0:T(8,128)(2,1)S(1)}, bf16[2,512,768]{2,1,0:T(8,128)(2,1)}, u32[]{:S(2)}) copy-start(bf16[2,512,768]{2,1,0:T(8,128)(2,1)} %get-tuple-element.114) | copy-start | bytes 4718596
  309.8 4.8 copy-start.12
  314.6 4.3 copy-start.15
  323.9 57.9 %collective-permute-start.3 = (bf16[1024,768]{1,0:T(8,128)(2,1)}, bf16[1024,768]{1,0:T(8,128)(2,1)S(1)}, u32[]{:S(2)}, u32[]{:S(2)}) collective-permute-start(bf16[1024,768]{1,0:T(8,128)(2,1)} %add_convert_fusion.1), channel_id=1, source_target_pairs={{0,2},{1,3},{2,0},{3,1},{4,6},{5,7},{6,4},{7,5},{8,10},{9,11},{10,... | collective-permute-start | bytes 4718600 | tf_op jit(solution)/shard_map/ppermute | solution.py:928
  358.0 8.0 %copy-start.13 = (bf16[2,768,1024]{2,1,0:T(8,128)(2,1)S(1)}, bf16[2,768,1024]{2,1,0:T(8,128)(2,1)}, u32[]{:S(2)}) copy-start(bf16[2,768,1024]{2,1,0:T(8,128)(2,1)} %get-tuple-element.86) | copy-start | bytes 9437188
  366.0 17.8 %copy-start.10 = (bf16[1024,768]{1,0:T(8,128)(2,1)S(1)}, bf16[1024,768]{1,0:T(8,128)(2,1)}, u32[]{:S(2)}) copy-start(bf16[1024,768]{1,0:T(8,128)(2,1)} %get-tuple-element.67) | copy-start | bytes 4718596
  386.3 32.0 %copy-start.17 = (f32[6,768]{1,0:T(8,128)S(1)}, f32[6,768]{1,0:T(8,128)}, u32[]{:S(2)}) copy-start(f32[6,768]{1,0:T(8,128)} %slice.161) | copy-start | bytes 55300
  386.3 32.0 %copy-start.19 = (f32[4,768]{1,0:T(4,128)S(1)}, f32[4,768]{1,0:T(4,128)}, u32[]{:S(2)}) copy-start(f32[4,768]{1,0:T(4,128)} %reshape_squeeze.27) | copy-start | bytes 36868
  386.3 39.6 %collective-permute-start.4 = (bf16[1024,768]{1,0:T(8,128)(2,1)}, bf16[1024,768]{1,0:T(8,128)(2,1)}, u32[]{:S(2)}, u32[]{:S(2)}) collective-permute-start(bf16[1024,768]{1,0:T(8,128)(2,1)} %convolution_convert_fusion), channel_id=1, source_target_pairs={{0,1},{1,0},{2,3},{3,2},{4,5},{5,4},{6,7},{7,6},{8,9},{9,8},{10,11... | collective-permute-start | bytes 4718600 | tf_op jit(solution)/shard_map/ppermute | solution.py:928
  419.0 3.8 copy-start.4
  419.0 4.3 copy-start.16
  423.3 2.7 copy-start.3
  429.3 70.9 %copy-start.2 = (bf16[8,216,768]{2,1,0:T(8,128)(2,1)S(1)}, bf16[8,216,768]{2,1,0:T(8,128)(2,1)}, u32[]{:S(2)}) copy-start(bf16[8,216,768]{2,1,0:T(8,128)(2,1)} %all-gather.11.cloned.1.call-done) | copy-start | bytes 7962628
  503.5 7.4 %copy-start.21 = (f32[2]{0:T(128)S(1)}, f32[2]{0:T(128)}, u32[]{:S(2)}) copy-start(f32[2]{0:T(128)} %convert_multiply_fusion) | copy-start | bytes 28
  503.6 7.9 %copy-start.5 = (f32[8,24,768]{2,1,0:T(8,128)S(1)}, f32[8,24,768]{2,1,0:T(8,128)}, u32[]{:S(2)}) copy-start(f32[8,24,768]{2,1,0:T(8,128)} %get-tuple-element.115) | copy-start | bytes 1769476
  503.6 7.9 %copy-start.6 = (f32[8,24,768]{2,1,0:T(8,128)S(1)}, f32[8,24,768]{2,1,0:T(8,128)}, u32[]{:S(2)}) copy-start(f32[8,24,768]{2,1,0:T(8,128)} %get-tuple-element.116) | copy-start | bytes 1769476
  510.2 4.3 copy-start.7
  511.5 4.1 copy-start.1
  (1 other events, 1.6 us)
Sparse Core Ops, SparseCore 0:
  9.9 36.7 all-gather.4
  48.5 56.0 all-gather.6
  106.4 57.0 all-gather.8
  226.1 154.7 reduce-scatter.1
  382.4 34.5 all-gather.10
